TPU v7x, 32 devices: a whole 2x2x4 slice. The times are simulated.
32 devices in a mesh: freq: 4 (over y, x), src: 8 (over z, core).
Axes of the slice: x: 2, y: 2, z: 4, core: 2. Of those that a mesh axis runs over, the one named last changes fastest.
Arguments:
- recorded: float32 [1024, 512, 128], P('src', 'freq'), may hold values from -0.54 to 0.54
- panels: float32 [512, 512, 128], P('src', 'freq'), may hold values from -0.18 to 0.18
Outputs:
- multiples: float32 [1024, 512, 128], P('src', 'freq')
All inputs are finite; a program needn't handle non-finite values.
Results may differ from a plain program's by a relative error of at most 0.00007.
Values sent between devices are 32-bit elements; how exact they have to be, the bound alone decides.
No kernel may reach another device: no remote copies, remote signals or barrier semaphores. Data moves between devices by JAX's collectives and lax.ppermute only.
A program may use at most 128 MiB of HBM per device.

v0:
```python
import functools

import jax
import jax.numpy as jnp
import ml_dtypes
import numpy as np
from jax import lax
from jax.experimental import pallas as pl
from jax.experimental.pallas import tpu as pltpu
from jax.sharding import PartitionSpec as P


NT = 128
NF = 64
SHARES = (16, 12, 4)
F32, BF16 = jnp.float32, jnp.bfloat16


def tables():
    phase = np.arange(NF)[:, None] * np.arange(NT)[None, :] % NT
    angle = 2.0 * np.pi / NT * phase
    forward = np.stack([np.cos(angle), -np.sin(angle)], axis=1)
    weight = np.where(np.arange(NF) == 0, 1.0, 2.0) / NT
    return forward, forward * weight[:, None, None]


def by_core(table):
    half = NF // 2
    low, high = table[:half].reshape(NF, NT), table[half:].reshape(NF, NT)
    return np.stack([np.concatenate([low, high]), np.concatenate([high, low])])


def parts(table):
    high = table.astype(ml_dtypes.bfloat16)
    low = (table - high.astype(np.float64)).astype(ml_dtypes.bfloat16)
    return high, low


def split(x):
    high = x.astype(BF16)
    return high, (x - high.astype(F32)).astype(BF16)


def bins_of(half):
    return tuple(half * share // sum(SHARES) for share in SHARES)


def forward_kernel(bins, core_ref, w_ref, x_ref, *out_refs):
    rows, m, t = x_ref.shape
    high, low = split(x_ref[...].reshape(rows * m, t))
    x = jnp.concatenate([high, low], axis=1)
    both = lax.dot_general(w_ref[0], x, (((1,), (1,)), ((), ())), preferred_element_type=F32)
    n = both.shape[0] // 2
    res = both[:n] + both[n:]
    at = 0
    for out, count in zip(out_refs, bins + bins):
        for i in range(rows):
            out[:, i, :] = res[at : at + 2 * count, i * m : (i + 1) * m]
        at += 2 * count


def forward(x, core, bins):
    n, m, t = x.shape
    table = by_core(tables()[0])
    shapes = [jax.ShapeDtypeStruct((2 * b, n, m), F32) for b in bins + bins]
    high, low = parts(table)
    w = np.concatenate(
        [np.concatenate([high, high], axis=2), np.concatenate([low, np.zeros_like(low)], axis=2)], axis=1
    )
    step = 8
    return pl.pallas_call(
        functools.partial(forward_kernel, bins),
        grid_spec=pltpu.PrefetchScalarGridSpec(
            num_scalar_prefetch=1,
            grid=(n // step,),
            in_specs=[
                pl.BlockSpec((1,) + w.shape[1:], lambda i, c: (c[0], 0, 0)),
                pl.BlockSpec((step, m, t), lambda i, c: (i, 0, 0)),
            ],
            out_specs=[pl.BlockSpec((s.shape[0], step, m), lambda i, c: (0, i, 0)) for s in shapes],
        ),
        out_shape=shapes,
        cost_estimate=pl.CostEstimate(flops=12 * x.size * NT, bytes_accessed=8 * x.size, transcendentals=0),
        name="forward",
    )(core, jnp.asarray(w), x)


def product_kernel(blocks, slot_ref, *refs):
    d_refs, g_refs = refs[: 2 * blocks], list(refs[2 * blocks : -5])
    out_a, out_b, lhs, rhs, held = refs[-5:]
    if g_refs[0].ndim == 4:
        g_refs = [ref.at[h] for ref in g_refs for h in range(2)]
    count = d_refs[0].shape[0] // 2
    rows, depth = d_refs[0].shape[1:]
    half, cols = g_refs[0].shape[1:]
    core = slot_ref[blocks]
    base_low = 2 * depth * blocks

    def one_bin(b, carry):
        for s in range(blocks):
            slot = slot_ref[s]
            for h in range(2):
                place = jnp.where(core == h, 0, half)
                for part in range(2):
                    if s == 0:
                        g = g_refs[h][2 * b + part]
                    else:
                        up = g_refs[2 + 4 * (s - 1) + h]
                        down = g_refs[2 + 4 * (blocks - s - 1) + 2 + h]
                        g = up[2 * b + part] + down[2 * b + part]
                    high, low = split(g)
                    at = pl.multiple_of(slot * 2 * depth + place, half)
                    to = slice(part * cols, (part + 1) * cols)
                    rhs[pl.ds(at, half), to] = high
                    rhs[pl.ds(at + depth, half), to] = high
                    rhs[pl.ds(pl.multiple_of(base_low + slot * depth + place, half), half), to] = low
        for a in range(blocks):
            for h in range(2):
                for part in range(2):
                    high, low = split(d_refs[2 * a + h][2 * b + part])
                    to = slice((2 * part + h) * rows, (2 * part + h + 1) * rows)
                    lhs[to, 2 * a * depth : (2 * a + 1) * depth] = high
                    lhs[to, (2 * a + 1) * depth : (2 * a + 2) * depth] = low
                    lhs[to, base_low + a * depth : base_low + (a + 1) * depth] = high
        p = jnp.dot(lhs[...], rhs[...], preferred_element_type=F32)
        held[2 * b] = p[: 2 * rows, :cols] - p[2 * rows :, cols:]
        held[2 * b + 1] = p[: 2 * rows, cols:] + p[2 * rows :, :cols]
        return carry

    lax.fori_loop(0, count, one_bin, 0)
    for c in range(2 * count):
        out_a[:, c, :] = held[c, :rows]
        out_b[:, c, :] = held[c, rows:]


def product(slots, d, g):
    blocks = len(d) // 2
    n, rows, depth = d[0].shape
    _, cols = g[0].shape[-2:]
    step = 8
    out = jax.ShapeDtypeStruct((rows, n, cols), F32)

    def spec(s):
        if len(s) == 4:
            return pl.BlockSpec((2, step) + s[2:], lambda i, c: (0, i, 0, 0))
        return pl.BlockSpec((step,) + s[1:], lambda i, c: (i, 0, 0))

    return pl.pallas_call(
        functools.partial(product_kernel, blocks),
        grid_spec=pltpu.PrefetchScalarGridSpec(
            num_scalar_prefetch=1,
            grid=(n // step,),
            in_specs=[spec(x.shape) for x in list(d) + list(g)],
            out_specs=[pl.BlockSpec((rows, step, cols), lambda i, c: (0, i, 0))] * 2,
            scratch_shapes=[
                pltpu.VMEM((4 * rows, 3 * blocks * depth), BF16),
                pltpu.VMEM((3 * blocks * depth, 2 * cols), BF16),
                pltpu.VMEM((step, 2 * rows, cols), F32),
            ],
        ),
        out_shape=[out, out],
        cost_estimate=pl.CostEstimate(
            flops=n // 2 * 2 * 4 * rows * 3 * blocks * depth * 2 * cols,
            bytes_accessed=4 * sum(x.size for x in list(d) + list(g)),
            transcendentals=0,
        ),
        name="product",
    )(slots, *d, *g)


def inverse_kernel(so_far, core_ref, w_ref, *refs):
    x_refs, out = refs[so_far:-1], refs[-1]
    for i in range(out.shape[0]):
        high, low = split(jnp.concatenate([x[i] for x in x_refs], axis=0))
        x = jnp.concatenate([high, low], axis=0)
        both = lax.dot_general(x, w_ref[0], (((0,), (0,)), ((), ())), preferred_element_type=F32)
        res = both[:, :NT] + both[:, NT:]
        out[i] = res + refs[0][i] if so_far else res


def inverse(ms, core, cuts, acc=None):
    rows, _, cols = ms[0].shape
    half = NF
    table = by_core(tables()[1])
    table = np.concatenate([table[:, a:b] for a, b in cuts] + [table[:, half + a : half + b] for a, b in cuts], axis=1)
    accs = [] if acc is None else [acc]
    high, low = parts(table)
    w = np.concatenate(
        [np.concatenate([high, low], axis=2), np.concatenate([high, np.zeros_like(low)], axis=2)], axis=1
    )
    step = 8
    return pl.pallas_call(
        functools.partial(inverse_kernel, len(accs)),
        grid_spec=pltpu.PrefetchScalarGridSpec(
            num_scalar_prefetch=1,
            grid=(rows // step,),
            in_specs=[pl.BlockSpec((1,) + w.shape[1:], lambda i, c: (c[0], 0, 0))]
            + [pl.BlockSpec((step,) + x.shape[1:], lambda i, c: (i, 0, 0)) for x in accs + ms],
            out_specs=pl.BlockSpec((step, cols, NT), lambda i, c: (i, 0, 0)),
        ),
        out_shape=jax.ShapeDtypeStruct((rows, cols, NT), F32),
        cost_estimate=pl.CostEstimate(
            flops=12 * rows * cols * NT * NT, bytes_accessed=8 * rows * cols * NT, transcendentals=0
        ),
        name="inverse",
    )(core, jnp.asarray(w), *accs, *ms)


def plain(recorded, panels):
    forth, back = (jnp.asarray(x, F32) for x in tables())
    best = lax.Precision.HIGHEST
    to_bins = lambda x: lax.all_to_all(
        jnp.einsum("fct,abt->fcab", forth, x, precision=best), "freq", split_axis=0, concat_axis=3, tiled=True
    )
    d = to_bins(recorded)
    g = lax.all_gather(to_bins(panels), "src", axis=2, tiled=True)
    mul = functools.partial(jnp.einsum, "fik,fkr->fir", precision=best)
    re = mul(d[:, 0], g[:, 0]) - mul(d[:, 1], g[:, 1])
    im = mul(d[:, 0], g[:, 1]) + mul(d[:, 1], g[:, 0])
    m = lax.all_to_all(jnp.stack([re, im], axis=1), "freq", split_axis=3, concat_axis=0, tiled=True)
    return jnp.einsum("fcir,fct->irt", m, back, precision=best)


def local(around, along, recorded, panels):
    tiled = all(x.shape[1] % 128 == 0 and x.shape[0] % 32 == 0 for x in (recorded, panels))
    if around != 4 or along != 8 or not tiled:
        return plain(recorded, panels)
    half = NF // 2
    levels = along // 2
    ring = list(range(around // 2)) + list(range(around - 1, around // 2 - 1, -1))
    clockwise = [(ring[i], ring[(i + 1) % around]) for i in range(around)]
    counter = [(b, a) for a, b in clockwise]
    upward = [(2 * z + c, 2 * z + 2 + c) for z in range(levels - 1) for c in range(2)]
    downward = [(b, a) for a, b in upward]
    partner = [(i, i ^ 1) for i in range(along)]

    me_ring, me_src = lax.axis_index("freq"), lax.axis_index("src")
    core, z = me_src % 2, me_src // 2
    at = jnp.where(me_ring < around // 2, me_ring, around // 2 + around - 1 - me_ring)
    core_at = core.astype(jnp.int32).reshape(1)
    bins = bins_of(half)
    chunks = len(bins)
    where = jnp.asarray(np.argsort(ring), jnp.int32)
    slots = (at - where[(z - jnp.arange(levels)) % levels]) % around
    slots = jnp.concatenate([slots.astype(jnp.int32), core_at])

    g_parts = forward(panels, core_at, bins)
    d_parts = forward(recorded, core_at, bins)
    ms = []
    for c in range(chunks):
        g_own = [g_parts[c], lax.ppermute(g_parts[chunks + c], "src", partner)]
        d_own = [d_parts[c], lax.ppermute(d_parts[chunks + c], "src", partner)]
        if c:
            g_own = [jnp.stack(g_own)]
        g = list(g_own)
        up, down = g_own, g_own
        for _ in range(1, levels):
            up = [lax.ppermute(x, "src", upward) for x in up]
            down = [lax.ppermute(x, "src", downward) for x in down]
            g += up + down
        d = [d_own] + [None] * (around - 1)
        right, left = d_own, d_own
        for a in range(1, around // 2):
            right = [lax.ppermute(x, "freq", clockwise) for x in right]
            left = [lax.ppermute(x, "freq", counter) for x in left]
            d[a], d[around - a] = right, left
        last = around // 2
        d[last] = [lax.ppermute(right[0], "freq", clockwise), lax.ppermute(left[1], "freq", counter)]
        d = [x for pair in d for x in pair]
        m = product(slots, d, g)
        ms.append([m[0], lax.ppermute(m[1], "src", partner)])
    edges = np.cumsum([0] + [2 * b for b in bins])
    cuts = list(zip(edges[:-1], edges[1:]))
    acc = inverse([m for pair in zip(*ms[:1]) for m in pair], core_at, cuts[:1])
    return inverse([m for pair in zip(*ms[1:]) for m in pair], core_at, cuts[1:], acc)


def solution(mesh):
    return jax.shard_map(
        functools.partial(local, mesh.shape["freq"], mesh.shape["src"]),
        mesh=mesh,
        in_specs=(P("src", "freq", None), P("src", "freq", None)),
        out_specs=P("src", "freq", None),
        check_vma=False,
    )
```

profile of v0, /device:TPU:0, one launch (start us, length us, event | category | flops | bytes accessed | tf_op | source)
XLA Modules:
  0.0 446.7 jit_solution(14274282115142182880)
XLA Ops:
  0.0 8.2 %forward.3 = (f32[32,64,128]{2,1,0:T(8,128)}, f32[24,64,128]{2,1,0:T(8,128)}, f32[8,64,128]{2,1,0:T(8,128)}, f32[32,64,128]{2,1,0:T(8,128)}, f32[24,64,128]{2,1,0:T(8,128)}, /*index=5*/f32[8,64,128]{2,1,0:T(8,128)}) custom-call(s32[1]{0:T(128)} %bitcast.core_ref, bf16[2,256,256]{2,1,0:T(8,128)(2,1)} %constant.64.clone.w_ref, f32[64,128,128]{2,1,0:T(8,128)} %x_ref.3), custom_call_target="tpu_custom_call" | custom-call | flops 1610612736 | bytes 8388608 | tf_op jit(solution)/shard_map/forward/pallas_call | solution.py:71
  8.8 15.2 %forward.2 = (f32[32,128,128]{2,1,0:T(8,128)}, f32[24,128,128]{2,1,0:T(8,128)}, f32[8,128,128]{2,1,0:T(8,128)}, f32[32,128,128]{2,1,0:T(8,128)}, f32[24,128,128]{2,1,0:T(8,128)}, /*index=5*/f32[8,128,128]{2,1,0:T(8,128)}) custom-call(s32[1]{0:T(128)} %bitcast.core_ref, bf16[2,256,256]{2,1,0:T(8,128)(2,1)} %constant.64.clone.w_ref, f32[128,128,128]{2,1,0:T(8,128)} %x_ref.2), custom_call_target="tpu_custom_call" | custom-call | flops 3221225472 | bytes 16777216 | tf_op jit(solution)/shard_map/forward/pallas_call | solution.py:71
  32.4 6.9 %collective-permute-done.36.refs_2_ = f32[8,128,128]{2,1,0:T(8,128)S(1)} collective-permute-done((f32[8,128,128]{2,1,0:T(8,128)}, f32[8,128,128]{2,1,0:T(8,128)S(1)}, u32[]{:S(2)}, u32[]{:S(2)}) %collective-permute-start.36) | collective-permute-done | bytes 524320 | tf_op jit(solution)/shard_map/ppermute | solution.py:264
  42.9 4.4 collective-permute-start.8
  48.7 5.0 %collective-permute-done.39.refs_7_ = f32[8,128,128]{2,1,0:T(8,128)S(1)} collective-permute-done((f32[8,128,128]{2,1,0:T(8,128)S(1)}, f32[8,128,128]{2,1,0:T(8,128)S(1)}, u32[]{:S(2)}, u32[]{:S(2)}) %collective-permute-start.39) | collective-permute-done | bytes 524320 | tf_op jit(solution)/shard_map/ppermute | solution.py:265
  56.2 13.3 %collective-permute-done.8.refs_10_ = f32[32,64,128]{2,1,0:T(8,128)S(1)} collective-permute-done((f32[32,64,128]{2,1,0:T(8,128)S(1)}, f32[32,64,128]{2,1,0:T(8,128)S(1)}, u32[]{:S(2)}, u32[]{:S(2)}) %collective-permute-start.8) | collective-permute-done | bytes 1048608 | tf_op jit(solution)/shard_map/ppermute | solution.py:258
  75.4 4.6 %collective-permute-start.12 = (f32[32,64,128]{2,1,0:T(8,128)S(1)}, f32[32,64,128]{2,1,0:T(8,128)S(1)}, u32[]{:S(2)}, u32[]{:S(2)}) collective-permute-start(f32[32,64,128]{2,1,0:T(8,128)S(1)} %collective-permute-done.8.refs_10_), channel_id=1, source_target_pairs={{0,2},{1,3},{2,4},{3,5},{4,6},{5,7},{8,10},{9,11},{10,12},{11,13},... | collective-permute-start | bytes 3145736 | tf_op jit(solution)/shard_map/ppermute | solution.py:258
  80.0 9.9 %collective-permute-done.22.refs_2_ = f32[24,128,128]{2,1,0:T(8,128)} collective-permute-done((f32[24,128,128]{2,1,0:T(8,128)}, f32[24,128,128]{2,1,0:T(8,128)}, u32[]{:S(2)}, u32[]{:S(2)}) %collective-permute-start.22) | collective-permute-done | bytes 1572896 | tf_op jit(solution)/shard_map/ppermute | solution.py:264
  92.2 5.3 %collective-permute-done.9.refs_11_ = f32[32,64,128]{2,1,0:T(8,128)S(1)} collective-permute-done((f32[32,64,128]{2,1,0:T(8,128)S(1)}, f32[32,64,128]{2,1,0:T(8,128)S(1)}, u32[]{:S(2)}, u32[]{:S(2)}) %collective-permute-start.9) | collective-permute-done | bytes 1048608 | tf_op jit(solution)/shard_map/ppermute | solution.py:258
  103.7 14.3 %collective-permute-done.12.refs_14_ = f32[32,64,128]{2,1,0:T(8,128)S(1)} collective-permute-done((f32[32,64,128]{2,1,0:T(8,128)S(1)}, f32[32,64,128]{2,1,0:T(8,128)S(1)}, u32[]{:S(2)}, u32[]{:S(2)}) %collective-permute-start.12) | collective-permute-done | bytes 1048608 | tf_op jit(solution)/shard_map/ppermute | solution.py:258
  118.0 4.5 %collective-permute-start.29 = (f32[2,24,64,128]{3,2,1,0:T(8,128)S(1)}, f32[2,24,64,128]{3,2,1,0:T(8,128)S(1)}, u32[]{:S(2)}, u32[]{:S(2)}) collective-permute-start(f32[2,24,64,128]{3,2,1,0:T(8,128)S(1)} %pad_maximum_fusion.refs_8_), channel_id=1, source_target_pairs={{0,2},{1,3},{2,4},{3,5},{4,6},{5,7},{8,10},{9,11},{10,12},{11,13},... | collective-permute-start | bytes 4718600 | tf_op jit(solution)/shard_map/ppermute | solution.py:258
  123.8 4.6 %collective-permute-start.13 = (f32[32,64,128]{2,1,0:T(8,128)S(1)}, f32[32,64,128]{2,1,0:T(8,128)S(1)}, u32[]{:S(2)}, u32[]{:S(2)}) collective-permute-start(f32[32,64,128]{2,1,0:T(8,128)S(1)} %collective-permute-done.9.refs_11_), channel_id=1, source_target_pairs={{0,2},{1,3},{2,4},{3,5},{4,6},{5,7},{8,10},{9,11},{10,12},{11,13},... | collective-permute-start | bytes 3145736 | tf_op jit(solution)/shard_map/ppermute | solution.py:258
  128.5 13.0 %collective-permute-done.1.refs_2_ = f32[32,128,128]{2,1,0:T(8,128)S(1)} collective-permute-done((f32[32,128,128]{2,1,0:T(8,128)}, f32[32,128,128]{2,1,0:T(8,128)S(1)}, u32[]{:S(2)}, u32[]{:S(2)}) %collective-permute-start.1) | collective-permute-done | bytes 2097184 | tf_op jit(solution)/shard_map/ppermute | solution.py:264
  142.9 7.8 %collective-permute-done.6.refs_6_ = f32[32,128,128]{2,1,0:T(8,128)S(1)} collective-permute-done((f32[32,128,128]{2,1,0:T(8,128)}, f32[32,128,128]{2,1,0:T(8,128)S(1)}, u32[]{:S(2)}, u32[]{:S(2)}) %collective-permute-start.6) | collective-permute-done | bytes 2097184 | tf_op jit(solution)/shard_map/ppermute | solution.py:265
  152.0 5.2 %collective-permute-done.29.refs_9_ = f32[2,24,64,128]{3,2,1,0:T(8,128)S(1)} collective-permute-done((f32[2,24,64,128]{3,2,1,0:T(8,128)S(1)}, f32[2,24,64,128]{3,2,1,0:T(8,128)S(1)}, u32[]{:S(2)}, u32[]{:S(2)}) %collective-permute-start.29) | collective-permute-done | bytes 1572896 | tf_op jit(solution)/shard_map/ppermute | solution.py:258
  163.2 16.4 %collective-permute-done.13.refs_15_ = f32[32,64,128]{2,1,0:T(8,128)S(1)} collective-permute-done((f32[32,64,128]{2,1,0:T(8,128)S(1)}, f32[32,64,128]{2,1,0:T(8,128)S(1)}, u32[]{:S(2)}, u32[]{:S(2)}) %collective-permute-start.13) | collective-permute-done | bytes 1048608 | tf_op jit(solution)/shard_map/ppermute | solution.py:258
  187.1 15.0 %collective-permute-done.16.refs_18_ = f32[32,64,128]{2,1,0:T(8,128)S(1)} collective-permute-done((f32[32,64,128]{2,1,0:T(8,128)S(1)}, f32[32,64,128]{2,1,0:T(8,128)S(1)}, u32[]{:S(2)}, u32[]{:S(2)}) %collective-permute-start.16) | collective-permute-done | bytes 1048608 | tf_op jit(solution)/shard_map/ppermute | solution.py:258
  206.6 18.8 %collective-permute-done.25.refs_7_ = f32[24,128,128]{2,1,0:T(8,128)} collective-permute-done((f32[24,128,128]{2,1,0:T(8,128)}, f32[24,128,128]{2,1,0:T(8,128)}, u32[]{:S(2)}, u32[]{:S(2)}) %collective-permute-start.25) | collective-permute-done | bytes 1572896 | tf_op jit(solution)/shard_map/ppermute | solution.py:265
  228.0 5.0 %collective-permute-done.31.refs_11_ = f32[2,24,64,128]{3,2,1,0:T(8,128)} collective-permute-done((f32[2,24,64,128]{3,2,1,0:T(8,128)S(1)}, f32[2,24,64,128]{3,2,1,0:T(8,128)}, u32[]{:S(2)}, u32[]{:S(2)}) %collective-permute-start.31) | collective-permute-done | bytes 1572896 | tf_op jit(solution)/shard_map/ppermute | solution.py:258
  233.0 4.5 %collective-permute-start.17 = (f32[32,64,128]{2,1,0:T(8,128)S(1)}, f32[32,64,128]{2,1,0:T(8,128)S(1)}, u32[]{:S(2)}, u32[]{:S(2)}) collective-permute-start(f32[32,64,128]{2,1,0:T(8,128)S(1)} %collective-permute-done.13.refs_15_), channel_id=1, source_target_pairs={{0,2},{1,3},{2,4},{3,5},{4,6},{5,7},{8,10},{9,11},{10,12},{11,13},... | collective-permute-start | bytes 3145736 | tf_op jit(solution)/shard_map/ppermute | solution.py:258
  238.8 18.5 %collective-permute-done.17.refs_19_ = f32[32,64,128]{2,1,0:T(8,128)S(1)} collective-permute-done((f32[32,64,128]{2,1,0:T(8,128)S(1)}, f32[32,64,128]{2,1,0:T(8,128)S(1)}, u32[]{:S(2)}, u32[]{:S(2)}) %collective-permute-start.17) | collective-permute-done | bytes 1048608 | tf_op jit(solution)/shard_map/ppermute | solution.py:258
  263.5 35.0 %collective-permute-done.2.refs_3_ = f32[32,128,128]{2,1,0:T(8,128)S(1)} collective-permute-done((f32[32,128,128]{2,1,0:T(8,128)S(1)}, f32[32,128,128]{2,1,0:T(8,128)S(1)}, u32[]{:S(2)}, u32[]{:S(2)}) %collective-permute-start.2) | collective-permute-done | bytes 2097184 | tf_op jit(solution)/shard_map/ppermute | solution.py:264
  298.6 4.5 %collective-permute-start.33 = (f32[2,24,64,128]{3,2,1,0:T(8,128)}, f32[2,24,64,128]{3,2,1,0:T(8,128)}, u32[]{:S(2)}, u32[]{:S(2)}) collective-permute-start(f32[2,24,64,128]{3,2,1,0:T(8,128)} %collective-permute-done.31.refs_11_), channel_id=1, source_target_pairs={{0,2},{1,3},{2,4},{3,5},{4,6},{5,7},{8,10},{9,11},{10,12},{11,13},... | collective-permute-start | bytes 4718600 | tf_op jit(solution)/shard_map/ppermute | solution.py:258
  307.2 18.7 %product.3 = (f32[128,32,128]{2,1,0:T(8,128)}, f32[128,32,128]{2,1,0:T(8,128)}) custom-call(s32[5]{0:T(128)} %pad_add_fusion.slot_ref, f32[32,128,128]{2,1,0:T(8,128)} %get-tuple-element.23.refs_0_, f32[32,128,128]{2,1,0:T(8,128)} %copy-done.2, f32[32,128,128]{2,1,0:T(8,128)} %copy-done.3, f32[32,128,128]{2,1,0:T(8,128)} %copy-done.7, ...), custom_call_target="tpu_custom_call" | custom-call | flops 6442450944 | bytes 31457280 | tf_op jit(solution)/shard_map/product/pallas_call | solution.py:148
  325.9 6.3 %collective-permute-done.24.refs_4_ = f32[24,128,128]{2,1,0:T(8,128)S(1)} collective-permute-done((f32[24,128,128]{2,1,0:T(8,128)}, f32[24,128,128]{2,1,0:T(8,128)S(1)}, u32[]{:S(2)}, u32[]{:S(2)}) %collective-permute-start.24) | collective-permute-done | bytes 1572896 | tf_op jit(solution)/shard_map/ppermute | solution.py:268
  333.4 29.6 %collective-permute-done.23.refs_3_ = f32[24,128,128]{2,1,0:T(8,128)} collective-permute-done((f32[24,128,128]{2,1,0:T(8,128)}, f32[24,128,128]{2,1,0:T(8,128)}, u32[]{:S(2)}, u32[]{:S(2)}) %collective-permute-start.23) | collective-permute-done | bytes 1572896 | tf_op jit(solution)/shard_map/ppermute | solution.py:264
  371.5 15.3 %product.4 = (f32[128,24,128]{2,1,0:T(8,128)}, f32[128,24,128]{2,1,0:T(8,128)}) custom-call(s32[5]{0:T(128)} %pad_add_fusion.slot_ref, f32[24,128,128]{2,1,0:T(8,128)} %get-tuple-element.29.refs_0_, f32[24,128,128]{2,1,0:T(8,128)} %collective-permute-done.21.refs_1_, f32[24,128,128]{2,1,0:T(8,128)} %collective-permute-done.22.refs_2_, ...), custom_call_target="tpu_custom_call" | custom-call | flops 4831838208 | bytes 23592960 | tf_op jit(solution)/shard_map/product/pallas_call | solution.py:148
  387.6 4.6 %collective-permute-start.47 = (f32[2,8,64,128]{3,2,1,0:T(8,128)}, f32[2,8,64,128]{3,2,1,0:T(8,128)S(1)}, u32[]{:S(2)}, u32[]{:S(2)}) collective-permute-start(f32[2,8,64,128]{3,2,1,0:T(8,128)} %collective-permute-done.45.refs_11_), channel_id=1, source_target_pairs={{0,2},{1,3},{2,4},{3,5},{4,6},{5,7},{8,10},{9,11},{10,12},{11,13},... | collective-permute-start | bytes 1572872 | tf_op jit(solution)/shard_map/ppermute | solution.py:258
  393.4 7.9 %collective-permute-done.40.refs_5_ = f32[8,128,128]{2,1,0:T(8,128)S(1)} collective-permute-done((f32[8,128,128]{2,1,0:T(8,128)S(1)}, f32[8,128,128]{2,1,0:T(8,128)S(1)}, u32[]{:S(2)}, u32[]{:S(2)}) %collective-permute-start.40) | collective-permute-done | bytes 524320 | tf_op jit(solution)/shard_map/ppermute | solution.py:268
  408.2 8.2 %product.5 = (f32[128,8,128]{2,1,0:T(8,128)}, f32[128,8,128]{2,1,0:T(8,128)}) custom-call(s32[5]{0:T(128)} %pad_add_fusion.slot_ref, f32[8,128,128]{2,1,0:T(8,128)} %get-tuple-element.34.refs_0_, f32[8,128,128]{2,1,0:T(8,128)} %copy-done.30, f32[8,128,128]{2,1,0:T(8,128)} %copy-done.31, f32[8,128,128]{2,1,0:T(8,128)} %collective-permute-done.37.refs_3_, ...), custom_call_target="tpu_custom_call" | custom-call | flops 1610612736 | bytes 7864320 | tf_op jit(solution)/shard_map/product/pallas_call | solution.py:148
  417.7 13.4 %inverse.2.refs_0_ = f32[128,128,128]{2,1,0:T(8,128)} custom-call(s32[1]{0:T(128)} %bitcast.core_ref, bf16[2,128,256]{2,1,0:T(8,128)(2,1)} %constant.65.clone.w_ref, f32[128,32,128]{2,1,0:T(8,128)} %get-tuple-element.27.refs_0_, f32[128,32,128]{2,1,0:T(8,128)} %copy-done.9), custom_call_target="tpu_custom_call" | custom-call | flops 3221225472 | bytes 16777216 | tf_op jit(solution)/shard_map/inverse/pallas_call | solution.py:192
  431.9 14.9 %inverse.3 = f32[128,128,128]{2,1,0:T(8,128)} custom-call(s32[1]{0:T(128)} %bitcast.core_ref, bf16[2,128,256]{2,1,0:T(8,128)(2,1)} %constant.66.clone.w_ref, f32[128,128,128]{2,1,0:T(8,128)} %inverse.2.refs_0_, f32[128,24,128]{2,1,0:T(8,128)} %get-tuple-element.33.refs_1_, f32[128,8,128]{2,1,0:T(8,128)} %get-tuple-element.38.refs_2_, ...), custom_call_target="tpu_custom_call" | custom-call | flops 3221225472 | bytes 16777216 | tf_op jit(solution)/shard_map/inverse/pallas_call | solution.py:192
  (170 shorter events, 87.2 us)
Async XLA Ops:
  27.0 28.4 %collective-permute-start.7 = (f32[32,64,128]{2,1,0:T(8,128)S(1)}, f32[32,64,128]{2,1,0:T(8,128)S(1)}, u32[]{:S(2)}, u32[]{:S(2)}) collective-permute-start(f32[32,64,128]{2,1,0:T(8,128)S(1)} %copy-done.41), channel_id=1, source_target_pairs={{0,1},{1,0},{2,3},{3,2},{4,5},{5,4},{6,7},{7,6},{8,9},{9,8},{10,11... | collective-permute-start | bytes 3145736 | tf_op jit(solution)/shard_map/ppermute | solution.py:251
  42.9 26.7 %collective-permute-start.8 = (f32[32,64,128]{2,1,0:T(8,128)S(1)}, f32[32,64,128]{2,1,0:T(8,128)S(1)}, u32[]{:S(2)}, u32[]{:S(2)}) collective-permute-start(f32[32,64,128]{2,1,0:T(8,128)S(1)} %copy-done.15), channel_id=1, source_target_pairs={{0,2},{1,3},{2,4},{3,5},{4,6},{5,7},{8,10},{9,11},{10,12},{11,13},... | collective-permute-start | bytes 3145736 | tf_op jit(solution)/shard_map/ppermute | solution.py:258
  47.4 26.7 %collective-permute-start.10 = (f32[32,64,128]{2,1,0:T(8,128)S(1)}, f32[32,64,128]{2,1,0:T(8,128)S(1)}, u32[]{:S(2)}, u32[]{:S(2)}) collective-permute-start(f32[32,64,128]{2,1,0:T(8,128)S(1)} %copy-done.15), channel_id=1, source_target_pairs={{2,0},{3,1},{4,2},{5,3},{6,4},{7,5},{10,8},{11,9},{12,10},{13,11},... | collective-permute-start | bytes 3145736 | tf_op jit(solution)/shard_map/ppermute | solution.py:259
  48.7 26.7 %collective-permute-start.21 = (f32[24,128,128]{2,1,0:T(8,128)}, f32[24,128,128]{2,1,0:T(8,128)}, u32[]{:S(2)}, u32[]{:S(2)}) collective-permute-start(f32[24,128,128]{2,1,0:T(8,128)} %get-tuple-element.30), channel_id=1, source_target_pairs={{0,1},{1,0},{2,3},{3,2},{4,5},{5,4},{6,7},{7,6},{8,9},{9,8},{10,11... | collective-permute-start | bytes 4718600 | tf_op jit(solution)/shard_map/ppermute | solution.py:252
  53.7 36.2 %collective-permute-start.22 = (f32[24,128,128]{2,1,0:T(8,128)}, f32[24,128,128]{2,1,0:T(8,128)}, u32[]{:S(2)}, u32[]{:S(2)}) collective-permute-start(f32[24,128,128]{2,1,0:T(8,128)} %get-tuple-element.29.refs_0_), channel_id=1, source_target_pairs={{0,8},{8,24},{24,16},{16,0},{1,9},{9,25},{25,17},{17,1},{2,10},{10... | collective-permute-start | bytes 4718600 | tf_op jit(solution)/shard_map/ppermute | solution.py:264
  55.4 35.5 %collective-permute-start.27 = (f32[24,128,128]{2,1,0:T(8,128)}, f32[24,128,128]{2,1,0:T(8,128)S(1)}, u32[]{:S(2)}, u32[]{:S(2)}) collective-permute-start(f32[24,128,128]{2,1,0:T(8,128)} %get-tuple-element.29.refs_0_), channel_id=1, source_target_pairs={{8,0},{24,8},{16,24},{0,16},{9,1},{25,9},{17,25},{1,17},{10,2},{26... | collective-permute-start | bytes 4718600 | tf_op jit(solution)/shard_map/ppermute | solution.py:265
  69.6 27.9 %collective-permute-start.9 = (f32[32,64,128]{2,1,0:T(8,128)S(1)}, f32[32,64,128]{2,1,0:T(8,128)S(1)}, u32[]{:S(2)}, u32[]{:S(2)}) collective-permute-start(f32[32,64,128]{2,1,0:T(8,128)S(1)} %collective-permute-done.7.refs_9_), channel_id=1, source_target_pairs={{0,2},{1,3},{2,4},{3,5},{4,6},{5,7},{8,10},{9,11},{10,12},{11,13},... | collective-permute-start | bytes 3145736 | tf_op jit(solution)/shard_map/ppermute | solution.py:258
  74.1 27.9 %collective-permute-start.11 = (f32[32,64,128]{2,1,0:T(8,128)S(1)}, f32[32,64,128]{2,1,0:T(8,128)S(1)}, u32[]{:S(2)}, u32[]{:S(2)}) collective-permute-start(f32[32,64,128]{2,1,0:T(8,128)S(1)} %collective-permute-done.7.refs_9_), channel_id=1, source_target_pairs={{2,0},{3,1},{4,2},{5,3},{6,4},{7,5},{10,8},{11,9},{12,10},{13,11},... | collective-permute-start | bytes 3145736 | tf_op jit(solution)/shard_map/ppermute | solution.py:259
  75.4 42.6 %collective-permute-start.12 = (f32[32,64,128]{2,1,0:T(8,128)S(1)}, f32[32,64,128]{2,1,0:T(8,128)S(1)}, u32[]{:S(2)}, u32[]{:S(2)}) collective-permute-start(f32[32,64,128]{2,1,0:T(8,128)S(1)} %collective-permute-done.8.refs_10_), channel_id=1, source_target_pairs={{0,2},{1,3},{2,4},{3,5},{4,6},{5,7},{8,10},{9,11},{10,12},{11,13},... | collective-permute-start | bytes 3145736 | tf_op jit(solution)/shard_map/ppermute | solution.py:258
  89.9 33.9 %collective-permute-start = (f32[32,128,128]{2,1,0:T(8,128)}, f32[32,128,128]{2,1,0:T(8,128)S(1)}, u32[]{:S(2)}, u32[]{:S(2)}) collective-permute-start(f32[32,128,128]{2,1,0:T(8,128)} %get-tuple-element.24), channel_id=1, source_target_pairs={{0,1},{1,0},{2,3},{3,2},{4,5},{5,4},{6,7},{7,6},{8,9},{9,8},{10,11... | collective-permute-start | bytes 6291464 | tf_op jit(solution)/shard_map/ppermute | solution.py:252
  90.9 31.6 %collective-permute-start.14 = (f32[32,64,128]{2,1,0:T(8,128)S(1)}, f32[32,64,128]{2,1,0:T(8,128)S(1)}, u32[]{:S(2)}, u32[]{:S(2)}) collective-permute-start(f32[32,64,128]{2,1,0:T(8,128)S(1)} %collective-permute-done.10.refs_12_), channel_id=1, source_target_pairs={{2,0},{3,1},{4,2},{5,3},{6,4},{7,5},{10,8},{11,9},{12,10},{13,11},... | collective-permute-start | bytes 3145736 | tf_op jit(solution)/shard_map/ppermute | solution.py:259
  97.5 43.9 %collective-permute-start.1 = (f32[32,128,128]{2,1,0:T(8,128)}, f32[32,128,128]{2,1,0:T(8,128)S(1)}, u32[]{:S(2)}, u32[]{:S(2)}) collective-permute-start(f32[32,128,128]{2,1,0:T(8,128)} %get-tuple-element.23.refs_0_), channel_id=1, source_target_pairs={{0,8},{8,24},{24,16},{16,0},{1,9},{9,25},{25,17},{17,1},{2,10},{10... | collective-permute-start | bytes 6291464 | tf_op jit(solution)/shard_map/ppermute | solution.py:264
  102.0 48.7 %collective-permute-start.6 = (f32[32,128,128]{2,1,0:T(8,128)}, f32[32,128,128]{2,1,0:T(8,128)S(1)}, u32[]{:S(2)}, u32[]{:S(2)}) collective-permute-start(f32[32,128,128]{2,1,0:T(8,128)} %get-tuple-element.23.refs_0_), channel_id=1, source_target_pairs={{8,0},{24,8},{16,24},{0,16},{9,1},{25,9},{17,25},{1,17},{10,2},{26... | collective-permute-start | bytes 6291464 | tf_op jit(solution)/shard_map/ppermute | solution.py:265
  118.0 39.1 %collective-permute-start.29 = (f32[2,24,64,128]{3,2,1,0:T(8,128)S(1)}, f32[2,24,64,128]{3,2,1,0:T(8,128)S(1)}, u32[]{:S(2)}, u32[]{:S(2)}) collective-permute-start(f32[2,24,64,128]{3,2,1,0:T(8,128)S(1)} %pad_maximum_fusion.refs_8_), channel_id=1, source_target_pairs={{0,2},{1,3},{2,4},{3,5},{4,6},{5,7},{8,10},{9,11},{10,12},{11,13},... | collective-permute-start | bytes 4718600 | tf_op jit(solution)/shard_map/ppermute | solution.py:258
  122.5 39.2 %collective-permute-start.30 = (f32[2,24,64,128]{3,2,1,0:T(8,128)S(1)}, f32[2,24,64,128]{3,2,1,0:T(8,128)S(1)}, u32[]{:S(2)}, u32[]{:S(2)}) collective-permute-start(f32[2,24,64,128]{3,2,1,0:T(8,128)S(1)} %pad_maximum_fusion.refs_8_), channel_id=1, source_target_pairs={{2,0},{3,1},{4,2},{5,3},{6,4},{7,5},{10,8},{11,9},{12,10},{13,11},... | collective-permute-start | bytes 4718600 | tf_op jit(solution)/shard_map/ppermute | solution.py:259
  123.8 55.8 %collective-permute-start.13 = (f32[32,64,128]{2,1,0:T(8,128)S(1)}, f32[32,64,128]{2,1,0:T(8,128)S(1)}, u32[]{:S(2)}, u32[]{:S(2)}) collective-permute-start(f32[32,64,128]{2,1,0:T(8,128)S(1)} %collective-permute-done.9.refs_11_), channel_id=1, source_target_pairs={{0,2},{1,3},{2,4},{3,5},{4,6},{5,7},{8,10},{9,11},{10,12},{11,13},... | collective-permute-start | bytes 3145736 | tf_op jit(solution)/shard_map/ppermute | solution.py:258
  141.4 85.5 %collective-permute-start.4 = (f32[32,128,128]{2,1,0:T(8,128)S(1)}, f32[32,128,128]{2,1,0:T(8,128)S(1)}, u32[]{:S(2)}, u32[]{:S(2)}) collective-permute-start(f32[32,128,128]{2,1,0:T(8,128)S(1)} %collective-permute-done.refs_1_), channel_id=1, source_target_pairs={{8,0},{24,8},{16,24},{0,16},{9,1},{25,9},{17,25},{1,17},{10,2},{26... | collective-permute-start | bytes 6291464 | tf_op jit(solution)/shard_map/ppermute | solution.py:265
  150.7 32.0 %collective-permute-start.15 = (f32[32,64,128]{2,1,0:T(8,128)S(1)}, f32[32,64,128]{2,1,0:T(8,128)S(1)}, u32[]{:S(2)}, u32[]{:S(2)}) collective-permute-start(f32[32,64,128]{2,1,0:T(8,128)S(1)} %collective-permute-done.11.refs_13_), channel_id=1, source_target_pairs={{2,0},{3,1},{4,2},{5,3},{6,4},{7,5},{10,8},{11,9},{12,10},{13,11},... | collective-permute-start | bytes 3145736 | tf_op jit(solution)/shard_map/ppermute | solution.py:259
  157.1 44.9 %collective-permute-start.16 = (f32[32,64,128]{2,1,0:T(8,128)S(1)}, f32[32,64,128]{2,1,0:T(8,128)S(1)}, u32[]{:S(2)}, u32[]{:S(2)}) collective-permute-start(f32[32,64,128]{2,1,0:T(8,128)S(1)} %collective-permute-done.12.refs_14_), channel_id=1, source_target_pairs={{0,2},{1,3},{2,4},{3,5},{4,6},{5,7},{8,10},{9,11},{10,12},{11,13},... | collective-permute-start | bytes 3145736 | tf_op jit(solution)/shard_map/ppermute | solution.py:258
  161.7 63.8 %collective-permute-start.25 = (f32[24,128,128]{2,1,0:T(8,128)}, f32[24,128,128]{2,1,0:T(8,128)}, u32[]{:S(2)}, u32[]{:S(2)}) collective-permute-start(f32[24,128,128]{2,1,0:T(8,128)} %collective-permute-done.21.refs_1_), channel_id=1, source_target_pairs={{8,0},{24,8},{16,24},{0,16},{9,1},{25,9},{17,25},{1,17},{10,2},{26... | collective-permute-start | bytes 4718600 | tf_op jit(solution)/shard_map/ppermute | solution.py:265
  182.7 50.2 %collective-permute-start.31 = (f32[2,24,64,128]{3,2,1,0:T(8,128)S(1)}, f32[2,24,64,128]{3,2,1,0:T(8,128)}, u32[]{:S(2)}, u32[]{:S(2)}) collective-permute-start(f32[2,24,64,128]{3,2,1,0:T(8,128)S(1)} %collective-permute-done.29.refs_9_), channel_id=1, source_target_pairs={{0,2},{1,3},{2,4},{3,5},{4,6},{5,7},{8,10},{9,11},{10,12},{11,13},... | collective-permute-start | bytes 4718600 | tf_op jit(solution)/shard_map/ppermute | solution.py:258
  202.1 35.4 %collective-permute-start.32 = (f32[2,24,64,128]{3,2,1,0:T(8,128)S(1)}, f32[2,24,64,128]{3,2,1,0:T(8,128)}, u32[]{:S(2)}, u32[]{:S(2)}) collective-permute-start(f32[2,24,64,128]{3,2,1,0:T(8,128)S(1)} %collective-permute-done.30.refs_10_), channel_id=1, source_target_pairs={{2,0},{3,1},{4,2},{5,3},{6,4},{7,5},{10,8},{11,9},{12,10},{13,11},... | collective-permute-start | bytes 4718600 | tf_op jit(solution)/shard_map/ppermute | solution.py:259
  205.1 57.9 %collective-permute-start.3 = (f32[32,128,128]{2,1,0:T(8,128)S(1)}, f32[32,128,128]{2,1,0:T(8,128)S(1)}, u32[]{:S(2)}, u32[]{:S(2)}) collective-permute-start(f32[32,128,128]{2,1,0:T(8,128)S(1)} %collective-permute-done.1.refs_2_), channel_id=1, source_target_pairs={{0,8},{8,24},{24,16},{16,0},{1,9},{9,25},{25,17},{17,1},{2,10},{10... | collective-permute-start | bytes 6291464 | tf_op jit(solution)/shard_map/ppermute | solution.py:268
  225.4 73.1 %collective-permute-start.2 = (f32[32,128,128]{2,1,0:T(8,128)S(1)}, f32[32,128,128]{2,1,0:T(8,128)S(1)}, u32[]{:S(2)}, u32[]{:S(2)}) collective-permute-start(f32[32,128,128]{2,1,0:T(8,128)S(1)} %collective-permute-done.refs_1_), channel_id=1, source_target_pairs={{0,8},{8,24},{24,16},{16,0},{1,9},{9,25},{25,17},{17,1},{2,10},{10... | collective-permute-start | bytes 6291464 | tf_op jit(solution)/shard_map/ppermute | solution.py:264
  226.9 76.2 %collective-permute-start.5 = (f32[32,128,128]{2,1,0:T(8,128)S(1)}, f32[32,128,128]{2,1,0:T(8,128)S(1)}, u32[]{:S(2)}, u32[]{:S(2)}) collective-permute-start(f32[32,128,128]{2,1,0:T(8,128)S(1)} %collective-permute-done.4.refs_7_), channel_id=1, source_target_pairs={{8,0},{24,8},{16,24},{0,16},{9,1},{25,9},{17,25},{1,17},{10,2},{26... | collective-permute-start | bytes 6291464 | tf_op jit(solution)/shard_map/ppermute | solution.py:268
  257.3 75.0 %collective-permute-start.24 = (f32[24,128,128]{2,1,0:T(8,128)}, f32[24,128,128]{2,1,0:T(8,128)S(1)}, u32[]{:S(2)}, u32[]{:S(2)}) collective-permute-start(f32[24,128,128]{2,1,0:T(8,128)} %collective-permute-done.22.refs_2_), channel_id=1, source_target_pairs={{0,8},{8,24},{24,16},{16,0},{1,9},{9,25},{25,17},{17,1},{2,10},{10... | collective-permute-start | bytes 4718600 | tf_op jit(solution)/shard_map/ppermute | solution.py:268
  261.5 101.6 %collective-permute-start.23 = (f32[24,128,128]{2,1,0:T(8,128)}, f32[24,128,128]{2,1,0:T(8,128)}, u32[]{:S(2)}, u32[]{:S(2)}) collective-permute-start(f32[24,128,128]{2,1,0:T(8,128)} %collective-permute-done.21.refs_1_), channel_id=1, source_target_pairs={{0,8},{8,24},{24,16},{16,0},{1,9},{9,25},{25,17},{17,1},{2,10},{10... | collective-permute-start | bytes 4718600 | tf_op jit(solution)/shard_map/ppermute | solution.py:264
  263.0 101.6 %collective-permute-start.26 = (f32[24,128,128]{2,1,0:T(8,128)}, f32[24,128,128]{2,1,0:T(8,128)}, u32[]{:S(2)}, u32[]{:S(2)}) collective-permute-start(f32[24,128,128]{2,1,0:T(8,128)} %collective-permute-done.25.refs_7_), channel_id=1, source_target_pairs={{8,0},{24,8},{16,24},{0,16},{9,1},{25,9},{17,25},{1,17},{10,2},{26... | collective-permute-start | bytes 4718600 | tf_op jit(solution)/shard_map/ppermute | solution.py:268
  298.6 67.5 %collective-permute-start.33 = (f32[2,24,64,128]{3,2,1,0:T(8,128)}, f32[2,24,64,128]{3,2,1,0:T(8,128)}, u32[]{:S(2)}, u32[]{:S(2)}) collective-permute-start(f32[2,24,64,128]{3,2,1,0:T(8,128)} %collective-permute-done.31.refs_11_), channel_id=1, source_target_pairs={{0,2},{1,3},{2,4},{3,5},{4,6},{5,7},{8,10},{9,11},{10,12},{11,13},... | collective-permute-start | bytes 4718600 | tf_op jit(solution)/shard_map/ppermute | solution.py:258
  304.5 65.7 %collective-permute-start.34 = (f32[2,24,64,128]{3,2,1,0:T(8,128)}, f32[2,24,64,128]{3,2,1,0:T(8,128)}, u32[]{:S(2)}, u32[]{:S(2)}) collective-permute-start(f32[2,24,64,128]{3,2,1,0:T(8,128)} %collective-permute-done.32.refs_12_), channel_id=1, source_target_pairs={{2,0},{3,1},{4,2},{5,3},{6,4},{7,5},{10,8},{11,9},{12,10},{13,11},... | collective-permute-start | bytes 4718600 | tf_op jit(solution)/shard_map/ppermute | solution.py:259
  333.4 83.0 %collective-permute-start.20 = (f32[128,32,128]{2,1,0:T(8,128)}, f32[128,32,128]{2,1,0:T(8,128)S(1)}, u32[]{:S(2)}, u32[]{:S(2)}) collective-permute-start(f32[128,32,128]{2,1,0:T(8,128)} %get-tuple-element.28), channel_id=1, source_target_pairs={{0,1},{1,0},{2,3},{3,2},{4,5},{5,4},{6,7},{7,6},{8,9},{9,8},{10,11... | collective-permute-start | bytes 6291464 | tf_op jit(solution)/shard_map/ppermute | solution.py:271
  386.9 44.2 %collective-permute-start.49 = (f32[128,24,128]{2,1,0:T(8,128)}, f32[128,24,128]{2,1,0:T(8,128)}, u32[]{:S(2)}, u32[]{:S(2)}) collective-permute-start(f32[128,24,128]{2,1,0:T(8,128)} %get-tuple-element.39), channel_id=1, source_target_pairs={{0,1},{1,0},{2,3},{3,2},{4,5},{5,4},{6,7},{7,6},{8,9},{9,8},{10,11... | collective-permute-start | bytes 4718600 | tf_op jit(solution)/shard_map/ppermute | solution.py:271
  (62 other events, 3422.9 us)
where the time goes:
time: 449 us; the launch traced here: 447 us
  waiting for transfers between devices  252 us (56%)
  Pallas kernels  93.9 us (21%)
  starting transfers between devices  92.4 us (21%)
  local copies, waits for them, and re-layouts  6.92 us (2%)
    ppermute x12, waiting for transfers between devices, local(): up = [lax.ppermute(x, 'src', upward) for x in up]  96.4 us
    ppermute x6, waiting for transfers between devices, local(): right = [lax.ppermute(x, 'freq', clockwise) for x in right]  94.5 us
    ppermute x12, starting transfers between devices, local(): up = [lax.ppermute(x, 'src', upward) for x in up]  53.2 us
    pallas_call x3, Pallas kernels, product(): pl.pallas_call(functools.partial(product_kernel, blocks), grid_spec=pltpu...  42.3 us
    ppermute x6, waiting for transfers between devices, local(): left = [lax.ppermute(x, 'freq', counter) for x in left]  34 us
    pallas_call x2, Pallas kernels, inverse(): pl.pallas_call(functools.partial(inverse_kernel, len(accs)), grid_spec=pl...  28.2 us
    pallas_call x2, Pallas kernels, forward(): pl.pallas_call(functools.partial(forward_kernel, bins), grid_spec=pltpu.P...  23.4 us
    ppermute x12, starting transfers between devices, local(): down = [lax.ppermute(x, 'src', downward) for x in down]  15.4 us
  transfers between devices with their start and end apart: 51, of which 28 were waited for; matrix products, arithmetic and copies ran while one was open for 0% of the time, Pallas kernels for 16%

commit v1 on v0

--- a/solution.py
+++ b/solution.py
@@ -12,7 +12,7 @@
 
 NT = 128
 NF = 64
-SHARES = (16, 12, 4)
+SHARES = (24, 8)
 F32, BF16 = jnp.float32, jnp.bfloat16
 
 
@@ -45,31 +45,41 @@
     return tuple(half * share // sum(SHARES) for share in SHARES)
 
 
-def forward_kernel(bins, core_ref, w_ref, x_ref, *out_refs):
+def forward_kernel(counts, core_ref, w_ref, x_ref, *out_refs):
     rows, m, t = x_ref.shape
-    high, low = split(x_ref[...].reshape(rows * m, t))
-    x = jnp.concatenate([high, low], axis=1)
-    both = lax.dot_general(w_ref[0], x, (((1,), (1,)), ((), ())), preferred_element_type=F32)
-    n = both.shape[0] // 2
-    res = both[:n] + both[n:]
-    at = 0
-    for out, count in zip(out_refs, bins + bins):
-        for i in range(rows):
-            out[:, i, :] = res[at : at + 2 * count, i * m : (i + 1) * m]
-        at += 2 * count
-
-
-def forward(x, core, bins):
+    group = 8
+
+    def some(q, carry):
+        first = pl.multiple_of(q * group, group)
+        high, low = split(x_ref[pl.ds(first, group)].reshape(group * m, t))
+        x = jnp.concatenate([high, low], axis=1)
+        both = lax.dot_general(w_ref[0], x, (((1,), (1,)), ((), ())), preferred_element_type=F32)
+        n = both.shape[0] // 2
+        res = both[:n] + both[n:]
+        at = 0
+        for out, count in zip(out_refs, counts):
+            view = out.at[:, pl.ds(first, group), :]
+            for i in range(group):
+                view[:, i, :] = res[at : at + count, i * m : (i + 1) * m]
+            at += count
+        return carry
+
+    lax.fori_loop(0, rows // group, some, 0)
+
+
+def forward(x, core, cuts):
     n, m, t = x.shape
     table = by_core(tables()[0])
-    shapes = [jax.ShapeDtypeStruct((2 * b, n, m), F32) for b in bins + bins]
+    table = np.concatenate([table[:, a:b] for a, b in cuts], axis=1)
+    counts = [b - a for a, b in cuts]
+    shapes = [jax.ShapeDtypeStruct((count, n, m), F32) for count in counts]
     high, low = parts(table)
     w = np.concatenate(
         [np.concatenate([high, high], axis=2), np.concatenate([low, np.zeros_like(low)], axis=2)], axis=1
     )
-    step = 8
+    step = 32
     return pl.pallas_call(
-        functools.partial(forward_kernel, bins),
+        functools.partial(forward_kernel, counts),
         grid_spec=pltpu.PrefetchScalarGridSpec(
             num_scalar_prefetch=1,
             grid=(n // step,),
@@ -95,8 +105,8 @@
     half, cols = g_refs[0].shape[1:]
     core = slot_ref[blocks]
     base_low = 2 * depth * blocks
-
-    def one_bin(b, carry):
+    step, steps = pl.program_id(0), pl.num_programs(0)
+    for b in range(count):
         for s in range(blocks):
             slot = slot_ref[s]
             for h in range(2):
@@ -111,51 +121,63 @@
                     high, low = split(g)
                     at = pl.multiple_of(slot * 2 * depth + place, half)
                     to = slice(part * cols, (part + 1) * cols)
-                    rhs[pl.ds(at, half), to] = high
-                    rhs[pl.ds(at + depth, half), to] = high
-                    rhs[pl.ds(pl.multiple_of(base_low + slot * depth + place, half), half), to] = low
+                    rhs[b % 2, pl.ds(at, half), to] = high
+                    rhs[b % 2, pl.ds(at + depth, half), to] = high
+                    rhs[b % 2, pl.ds(pl.multiple_of(base_low + slot * depth + place, half), half), to] = low
         for a in range(blocks):
             for h in range(2):
                 for part in range(2):
                     high, low = split(d_refs[2 * a + h][2 * b + part])
                     to = slice((2 * part + h) * rows, (2 * part + h + 1) * rows)
-                    lhs[to, 2 * a * depth : (2 * a + 1) * depth] = high
-                    lhs[to, (2 * a + 1) * depth : (2 * a + 2) * depth] = low
-                    lhs[to, base_low + a * depth : base_low + (a + 1) * depth] = high
-        p = jnp.dot(lhs[...], rhs[...], preferred_element_type=F32)
-        held[2 * b] = p[: 2 * rows, :cols] - p[2 * rows :, cols:]
-        held[2 * b + 1] = p[: 2 * rows, cols:] + p[2 * rows :, :cols]
-        return carry
-
-    lax.fori_loop(0, count, one_bin, 0)
-    for c in range(2 * count):
-        out_a[:, c, :] = held[c, :rows]
-        out_b[:, c, :] = held[c, rows:]
+                    lhs[b % 2, to, 2 * a * depth : (2 * a + 1) * depth] = high
+                    lhs[b % 2, to, (2 * a + 1) * depth : (2 * a + 2) * depth] = low
+                    lhs[b % 2, to, base_low + a * depth : base_low + (a + 1) * depth] = high
+        p = jnp.dot(lhs[b % 2], rhs[b % 2], preferred_element_type=F32)
+        row = 2 * (step * count + b)
+        held[row] = p[: 2 * rows, :cols] - p[2 * rows :, cols:]
+        held[row + 1] = p[: 2 * rows, cols:] + p[2 * rows :, :cols]
+
+    @pl.when(step == steps - 1)
+    def _():
+        for c in range(held.shape[0]):
+            out_a[:, c, :] = held[c, :rows]
+            out_b[:, c, :] = held[c, rows:]
 
 
 def product(slots, d, g):
     blocks = len(d) // 2
     n, rows, depth = d[0].shape
     _, cols = g[0].shape[-2:]
-    step = 8
+    step = 4
     out = jax.ShapeDtypeStruct((rows, n, cols), F32)
-
-    def spec(s):
-        if len(s) == 4:
-            return pl.BlockSpec((2, step) + s[2:], lambda i, c: (0, i, 0, 0))
-        return pl.BlockSpec((step,) + s[1:], lambda i, c: (i, 0, 0))
-
+    each = 1 if g[0].ndim == 4 else 2
+
+    def spec(x, hop=None):
+        def at(i, c):
+            if hop is None:
+                return i
+            z = c[blocks + 1]
+            there = z >= hop[1] if hop[0] else z + hop[1] < blocks
+            return jnp.where(there, i, 0)
+
+        if x.ndim == 4:
+            return pl.BlockSpec((2, step) + x.shape[2:], lambda i, c: (0, at(i, c), 0, 0))
+        return pl.BlockSpec((step,) + x.shape[1:], lambda i, c: (at(i, c), 0, 0))
+
+    hops = [None] * each
+    for s in range(1, blocks):
+        hops += [(True, s)] * each + [(False, s)] * each
     return pl.pallas_call(
         functools.partial(product_kernel, blocks),
         grid_spec=pltpu.PrefetchScalarGridSpec(
             num_scalar_prefetch=1,
             grid=(n // step,),
-            in_specs=[spec(x.shape) for x in list(d) + list(g)],
-            out_specs=[pl.BlockSpec((rows, step, cols), lambda i, c: (0, i, 0))] * 2,
+            in_specs=[spec(x) for x in d] + [spec(x, hop) for x, hop in zip(g, hops)],
+            out_specs=[pl.BlockSpec((rows, n, cols), lambda i, c: (0, 0, 0))] * 2,
             scratch_shapes=[
-                pltpu.VMEM((4 * rows, 3 * blocks * depth), BF16),
-                pltpu.VMEM((3 * blocks * depth, 2 * cols), BF16),
-                pltpu.VMEM((step, 2 * rows, cols), F32),
+                pltpu.VMEM((2, 4 * rows, 3 * blocks * depth), BF16),
+                pltpu.VMEM((2, 3 * blocks * depth, 2 * cols), BF16),
+                pltpu.VMEM((n, 2 * rows, cols), F32),
             ],
         ),
         out_shape=[out, out],
@@ -168,34 +190,36 @@
     )(slots, *d, *g)
 
 
-def inverse_kernel(so_far, core_ref, w_ref, *refs):
-    x_refs, out = refs[so_far:-1], refs[-1]
-    for i in range(out.shape[0]):
-        high, low = split(jnp.concatenate([x[i] for x in x_refs], axis=0))
-        x = jnp.concatenate([high, low], axis=0)
-        both = lax.dot_general(x, w_ref[0], (((0,), (0,)), ((), ())), preferred_element_type=F32)
-        res = both[:, :NT] + both[:, NT:]
-        out[i] = res + refs[0][i] if so_far else res
-
-
-def inverse(ms, core, cuts, acc=None):
+def inverse_kernel(core_ref, w_ref, *refs):
+    x_refs, out = refs[:-1], refs[-1]
+    group = 8
+
+    def some(q, carry):
+        for u in range(group):
+            i = q * group + u
+            high, low = split(jnp.concatenate([x[i] for x in x_refs], axis=0))
+            x = jnp.concatenate([high, low], axis=0)
+            both = lax.dot_general(x, w_ref[0], (((0,), (0,)), ((), ())), preferred_element_type=F32)
+            out[i] = both[:, :NT] + both[:, NT:]
+        return carry
+
+    lax.fori_loop(0, out.shape[0] // group, some, 0)
+
+
+def inverse(ms, core):
     rows, _, cols = ms[0].shape
-    half = NF
-    table = by_core(tables()[1])
-    table = np.concatenate([table[:, a:b] for a, b in cuts] + [table[:, half + a : half + b] for a, b in cuts], axis=1)
-    accs = [] if acc is None else [acc]
-    high, low = parts(table)
+    high, low = parts(by_core(tables()[1]))
     w = np.concatenate(
         [np.concatenate([high, low], axis=2), np.concatenate([high, np.zeros_like(low)], axis=2)], axis=1
     )
-    step = 8
+    step = 32
     return pl.pallas_call(
-        functools.partial(inverse_kernel, len(accs)),
+        inverse_kernel,
         grid_spec=pltpu.PrefetchScalarGridSpec(
             num_scalar_prefetch=1,
             grid=(rows // step,),
             in_specs=[pl.BlockSpec((1,) + w.shape[1:], lambda i, c: (c[0], 0, 0))]
-            + [pl.BlockSpec((step,) + x.shape[1:], lambda i, c: (i, 0, 0)) for x in accs + ms],
+            + [pl.BlockSpec((step,) + x.shape[1:], lambda i, c: (i, 0, 0)) for x in ms],
             out_specs=pl.BlockSpec((step, cols, NT), lambda i, c: (i, 0, 0)),
         ),
         out_shape=jax.ShapeDtypeStruct((rows, cols, NT), F32),
@@ -203,7 +227,7 @@
             flops=12 * rows * cols * NT * NT, bytes_accessed=8 * rows * cols * NT, transcendentals=0
         ),
         name="inverse",
-    )(core, jnp.asarray(w), *accs, *ms)
+    )(core, jnp.asarray(w), *ms)
 
 
 def plain(recorded, panels):
@@ -242,10 +266,15 @@
     chunks = len(bins)
     where = jnp.asarray(np.argsort(ring), jnp.int32)
     slots = (at - where[(z - jnp.arange(levels)) % levels]) % around
-    slots = jnp.concatenate([slots.astype(jnp.int32), core_at])
-
-    g_parts = forward(panels, core_at, bins)
-    d_parts = forward(recorded, core_at, bins)
+    slots = jnp.concatenate([slots.astype(jnp.int32), core_at, z.astype(jnp.int32).reshape(1)])
+    edges = [int(e) for e in np.cumsum([0] + [2 * b for b in bins])]
+    cuts = list(zip(edges[:-1], edges[1:]))
+    cuts += [(NF + a, NF + b) for a, b in cuts]
+
+    g_parts, d_parts = [], []
+    for which in (cuts[:1], cuts[1:]):
+        for x, to in ((panels, g_parts), (recorded, d_parts)):
+            to += forward(x, core_at, which)
     ms = []
     for c in range(chunks):
         g_own = [g_parts[c], lax.ppermute(g_parts[chunks + c], "src", partner)]
@@ -269,10 +298,7 @@
         d = [x for pair in d for x in pair]
         m = product(slots, d, g)
         ms.append([m[0], lax.ppermute(m[1], "src", partner)])
-    edges = np.cumsum([0] + [2 * b for b in bins])
-    cuts = list(zip(edges[:-1], edges[1:]))
-    acc = inverse([m for pair in zip(*ms[:1]) for m in pair], core_at, cuts[:1])
-    return inverse([m for pair in zip(*ms[1:]) for m in pair], core_at, cuts[1:], acc)
+    return inverse([m[0] for m in ms] + [m[1] for m in ms], core_at)
 
 
 def solution(mesh):

time: 449 us -> 435 us (0.969)
  waiting for transfers between devices: 252 us -> 269 us
  Pallas kernels: 93.9 us -> 78.9 us
  starting transfers between devices: 92.4 us -> 78.1 us
    ppermute x12 -> x9, waiting for transfers between devices: 96.4 us -> 25.3 us  [local(): up = [lax.ppermute(x, 'src', upward) for x in up]]
    ppermute x6 -> x4, waiting for transfers between devices: 34 us -> 102 us  [local(): left = [lax.ppermute(x, 'freq', counter) for x in left]]
    ppermute x12 -> x9, waiting for transfers between devices: 12.8 us -> 79.3 us  [local(): down = [lax.ppermute(x, 'src', downward) for x in down]]
    ppermute x6 -> x4, waiting for transfers between devices: 94.5 us -> 42.2 us  [local(): right = [lax.ppermute(x, 'freq', clockwise) for x in right]]
    pallas_call x4 -> x5, Pallas kernels: 51.7 us -> 39.3 us  [the longest x4 29.7 us: forward(): pl.pallas_call(functools.partial(forward_kernel, counts), grid_spec=pltpu...]
    ppermute x3 -> x2, waiting for transfers between devices: 6.33 us -> 16.4 us  [local(): lax.ppermute(right[0], 'freq', clockwise)]
    ppermute x3 -> x2, waiting for transfers between devices: 7.86 us -> 1.09 us  [local(): lax.ppermute(left[1], 'freq', counter)]
    ppermute x6 -> x4, starting transfers between devices: 10.5 us -> 5.52 us  [local(): right = [lax.ppermute(x, 'freq', clockwise) for x in right]]
  transfers between devices with their start and end apart: 51 -> 36, of which waited for: 28 -> 15; matrix products, arithmetic and copies ran while one was open for 0% -> 1% of each run, Pallas kernels for 16% -> 14%
where the time goes in v1:
time: 435 us; the launch traced here: 433 us
  waiting for transfers between devices  269 us (62%)
  Pallas kernels  78.9 us (18%)
  starting transfers between devices  78.1 us (18%)
  local copies, waits for them, and re-layouts  4.39 us (1%)
    ppermute x4, waiting for transfers between devices, local(): left = [lax.ppermute(x, 'freq', counter) for x in left]  102 us
    ppermute x9, waiting for transfers between devices, local(): down = [lax.ppermute(x, 'src', downward) for x in down]  79.3 us
    ppermute x9, starting transfers between devices, local(): up = [lax.ppermute(x, 'src', upward) for x in up]  50.7 us
    ppermute x4, waiting for transfers between devices, local(): right = [lax.ppermute(x, 'freq', clockwise) for x in right]  42.2 us
    pallas_call x2, Pallas kernels, product(): pl.pallas_call(functools.partial(product_kernel, blocks), grid_spec=pltpu...  39.6 us
    pallas_call x4, Pallas kernels, forward(): pl.pallas_call(functools.partial(forward_kernel, counts), grid_spec=pltpu...  29.7 us
    ppermute x9, waiting for transfers between devices, local(): up = [lax.ppermute(x, 'src', upward) for x in up]  25.3 us
    ppermute x2, waiting for transfers between devices, local(): lax.ppermute(right[0], 'freq', clockwise)  16.4 us
  transfers between devices with their start and end apart: 36, of which 15 were waited for; matrix products, arithmetic and copies ran while one was open for 1% of the time, Pallas kernels for 14%

profile of v1, /device:TPU:0, one launch (start us, length us, event | category | flops | bytes accessed | tf_op | source)
XLA Modules:
  0.0 432.6 jit_solution(6053235348101983933)
XLA Ops:
  0.0 9.7 %forward.5 = (f32[16,128,128]{2,1,0:T(8,128)}, f32[48,128,128]{2,1,0:T(8,128)}, f32[16,128,128]{2,1,0:T(8,128)}) custom-call(s32[1]{0:T(128)} %bitcast.core_ref, bf16[2,160,256]{2,1,0:T(8,128)(2,1)} %constant.65.clone.w_ref, f32[128,128,128]{2,1,0:T(8,128)} %x_ref.5), custom_call_target="tpu_custom_call" | custom-call | flops 3221225472 | bytes 16777216 | tf_op jit(solution)/shard_map/forward/pallas_call | solution.py:81
  10.2 5.9 %forward.7 = (f32[16,64,128]{2,1,0:T(8,128)}, f32[48,64,128]{2,1,0:T(8,128)}, f32[16,64,128]{2,1,0:T(8,128)}) custom-call(s32[1]{0:T(128)} %bitcast.core_ref, bf16[2,160,256]{2,1,0:T(8,128)(2,1)} %constant.65.clone.w_ref, f32[64,128,128]{2,1,0:T(8,128)} %x_ref.7), custom_call_target="tpu_custom_call" | custom-call | flops 1610612736 | bytes 8388608 | tf_op jit(solution)/shard_map/forward/pallas_call | solution.py:81
  16.2 5.4 %forward.6.refs_8_ = f32[48,64,128]{2,1,0:T(8,128)} custom-call(s32[1]{0:T(128)} %bitcast.core_ref, bf16[2,96,256]{2,1,0:T(8,128)(2,1)} %constant.64.clone.w_ref, f32[64,128,128]{2,1,0:T(8,128)} %x_ref.7), custom_call_target="tpu_custom_call" | custom-call | flops 1610612736 | bytes 8388608 | tf_op jit(solution)/shard_map/forward/pallas_call | solution.py:81
  22.8 6.6 %collective-permute-start.8 = (f32[48,64,128]{2,1,0:T(8,128)}, f32[48,64,128]{2,1,0:T(8,128)}, u32[]{:S(2)}, u32[]{:S(2)}) collective-permute-start(f32[48,64,128]{2,1,0:T(8,128)} %forward.6.refs_8_), channel_id=1, source_target_pairs={{0,2},{1,3},{2,4},{3,5},{4,6},{5,7},{8,10},{9,11},{10,12},{11,13},... | collective-permute-start | bytes 4718600 | tf_op jit(solution)/shard_map/ppermute | solution.py:287
  29.5 2.0 collective-permute-start.26
  34.1 21.2 %collective-permute-done.26.refs_6_ = f32[16,128,128]{2,1,0:T(8,128)S(1)} collective-permute-done((f32[16,128,128]{2,1,0:T(8,128)S(1)}, f32[16,128,128]{2,1,0:T(8,128)S(1)}, u32[]{:S(2)}, u32[]{:S(2)}) %collective-permute-start.26) | collective-permute-done | bytes 1048608 | tf_op jit(solution)/shard_map/ppermute | solution.py:294
  55.3 6.6 %collective-permute-done.10.refs_12_ = f32[48,64,128]{2,1,0:T(8,128)} collective-permute-done((f32[48,64,128]{2,1,0:T(8,128)}, f32[48,64,128]{2,1,0:T(8,128)}, u32[]{:S(2)}, u32[]{:S(2)}) %collective-permute-start.10) | collective-permute-done | bytes 1572896 | tf_op jit(solution)/shard_map/ppermute | solution.py:288
  63.3 5.7 %collective-permute-start.12 = (f32[48,64,128]{2,1,0:T(8,128)}, f32[48,64,128]{2,1,0:T(8,128)}, u32[]{:S(2)}, u32[]{:S(2)}) collective-permute-start(f32[48,64,128]{2,1,0:T(8,128)} %collective-permute-done.8.refs_10_), channel_id=1, source_target_pairs={{0,2},{1,3},{2,4},{3,5},{4,6},{5,7},{8,10},{9,11},{10,12},{11,13},... | collective-permute-start | bytes 4718600 | tf_op jit(solution)/shard_map/ppermute | solution.py:287
  69.0 15.4 %collective-permute-done.29.refs_10_ = f32[2,16,64,128]{3,2,1,0:T(8,128)S(1)} collective-permute-done((f32[2,16,64,128]{3,2,1,0:T(8,128)S(1)}, f32[2,16,64,128]{3,2,1,0:T(8,128)S(1)}, u32[]{:S(2)}, u32[]{:S(2)}) %collective-permute-start.29) | collective-permute-done | bytes 1048608 | tf_op jit(solution)/shard_map/ppermute | solution.py:288
  85.4 4.9 %collective-permute-start.28 = (f32[2,16,64,128]{3,2,1,0:T(8,128)S(1)}, f32[2,16,64,128]{3,2,1,0:T(8,128)}, u32[]{:S(2)}, u32[]{:S(2)}) collective-permute-start(f32[2,16,64,128]{3,2,1,0:T(8,128)S(1)} %pad_maximum_fusion.refs_8_), channel_id=1, source_target_pairs={{0,2},{1,3},{2,4},{3,5},{4,6},{5,7},{8,10},{9,11},{10,12},{11,13},... | collective-permute-start | bytes 3145736 | tf_op jit(solution)/shard_map/ppermute | solution.py:287
  90.2 8.7 %forward.4.refs_0_ = f32[48,128,128]{2,1,0:T(8,128)} custom-call(s32[1]{0:T(128)} %bitcast.core_ref, bf16[2,96,256]{2,1,0:T(8,128)(2,1)} %constant.64.clone.w_ref, f32[128,128,128]{2,1,0:T(8,128)} %x_ref.5), custom_call_target="tpu_custom_call" | custom-call | flops 3221225472 | bytes 16777216 | tf_op jit(solution)/shard_map/forward/pallas_call | solution.py:81
  98.9 24.1 %collective-permute-done.28.refs_9_ = f32[2,16,64,128]{3,2,1,0:T(8,128)} collective-permute-done((f32[2,16,64,128]{3,2,1,0:T(8,128)S(1)}, f32[2,16,64,128]{3,2,1,0:T(8,128)}, u32[]{:S(2)}, u32[]{:S(2)}) %collective-permute-start.28) | collective-permute-done | bytes 1048608 | tf_op jit(solution)/shard_map/ppermute | solution.py:287
  126.3 5.2 %collective-permute-start.9 = (f32[48,64,128]{2,1,0:T(8,128)}, f32[48,64,128]{2,1,0:T(8,128)S(1)}, u32[]{:S(2)}, u32[]{:S(2)}) collective-permute-start(f32[48,64,128]{2,1,0:T(8,128)} %collective-permute-done.7.refs_9_), channel_id=1, source_target_pairs={{0,2},{1,3},{2,4},{3,5},{4,6},{5,7},{8,10},{9,11},{10,12},{11,13},... | collective-permute-start | bytes 4718600 | tf_op jit(solution)/shard_map/ppermute | solution.py:287
  133.0 28.5 %collective-permute-done.11.refs_13_ = f32[48,64,128]{2,1,0:T(8,128)S(1)} collective-permute-done((f32[48,64,128]{2,1,0:T(8,128)}, f32[48,64,128]{2,1,0:T(8,128)S(1)}, u32[]{:S(2)}, u32[]{:S(2)}) %collective-permute-start.11) | collective-permute-done | bytes 1572896 | tf_op jit(solution)/shard_map/ppermute | solution.py:288
  162.8 4.6 %collective-permute-start.16 = (f32[48,64,128]{2,1,0:T(8,128)}, f32[48,64,128]{2,1,0:T(8,128)S(1)}, u32[]{:S(2)}, u32[]{:S(2)}) collective-permute-start(f32[48,64,128]{2,1,0:T(8,128)} %collective-permute-done.12.refs_14_), channel_id=1, source_target_pairs={{0,2},{1,3},{2,4},{3,5},{4,6},{5,7},{8,10},{9,11},{10,12},{11,13},... | collective-permute-start | bytes 4718600 | tf_op jit(solution)/shard_map/ppermute | solution.py:287
  167.5 26.7 %collective-permute-done.6.refs_6_ = f32[48,128,128]{2,1,0:T(8,128)S(1)} collective-permute-done((f32[48,128,128]{2,1,0:T(8,128)}, f32[48,128,128]{2,1,0:T(8,128)S(1)}, u32[]{:S(2)}, u32[]{:S(2)}) %collective-permute-start.6) | collective-permute-done | bytes 3145760 | tf_op jit(solution)/shard_map/ppermute | solution.py:294
  195.5 6.3 %collective-permute-start.13 = (f32[48,64,128]{2,1,0:T(8,128)S(1)}, f32[48,64,128]{2,1,0:T(8,128)}, u32[]{:S(2)}, u32[]{:S(2)}) collective-permute-start(f32[48,64,128]{2,1,0:T(8,128)S(1)} %collective-permute-done.9.refs_11_), channel_id=1, source_target_pairs={{0,2},{1,3},{2,4},{3,5},{4,6},{5,7},{8,10},{9,11},{10,12},{11,13},... | collective-permute-start | bytes 4718600 | tf_op jit(solution)/shard_map/ppermute | solution.py:287
  204.7 54.0 %collective-permute-done.4.refs_7_ = f32[48,128,128]{2,1,0:T(8,128)} collective-permute-done((f32[48,128,128]{2,1,0:T(8,128)}, f32[48,128,128]{2,1,0:T(8,128)}, u32[]{:S(2)}, u32[]{:S(2)}) %collective-permute-start.4) | collective-permute-done | bytes 3145760 | tf_op jit(solution)/shard_map/ppermute | solution.py:294
  261.4 6.3 %collective-permute-start.17 = (f32[48,64,128]{2,1,0:T(8,128)}, f32[48,64,128]{2,1,0:T(8,128)}, u32[]{:S(2)}, u32[]{:S(2)}) collective-permute-start(f32[48,64,128]{2,1,0:T(8,128)} %collective-permute-done.13.refs_15_), channel_id=1, source_target_pairs={{0,2},{1,3},{2,4},{3,5},{4,6},{5,7},{8,10},{9,11},{10,12},{11,13},... | collective-permute-start | bytes 4718600 | tf_op jit(solution)/shard_map/ppermute | solution.py:287
  268.3 26.5 %collective-permute-done.19.refs_21_ = f32[48,64,128]{2,1,0:T(8,128)} collective-permute-done((f32[48,64,128]{2,1,0:T(8,128)}, f32[48,64,128]{2,1,0:T(8,128)}, u32[]{:S(2)}, u32[]{:S(2)}) %collective-permute-start.19) | collective-permute-done | bytes 1572896 | tf_op jit(solution)/shard_map/ppermute | solution.py:288
  294.8 1.7 collective-permute-start.21
  297.6 1.6 collective-permute-start.22
  299.2 41.2 %collective-permute-done.2.refs_3_ = f32[48,128,128]{2,1,0:T(8,128)} collective-permute-done((f32[48,128,128]{2,1,0:T(8,128)}, f32[48,128,128]{2,1,0:T(8,128)}, u32[]{:S(2)}, u32[]{:S(2)}) %collective-permute-start.2) | collective-permute-done | bytes 3145760 | tf_op jit(solution)/shard_map/ppermute | solution.py:293
  341.8 5.5 %collective-permute-start.30 = (f32[2,16,64,128]{3,2,1,0:T(8,128)}, f32[2,16,64,128]{3,2,1,0:T(8,128)}, u32[]{:S(2)}, u32[]{:S(2)}) collective-permute-start(f32[2,16,64,128]{3,2,1,0:T(8,128)} %collective-permute-done.28.refs_9_), channel_id=1, source_target_pairs={{0,2},{1,3},{2,4},{3,5},{4,6},{5,7},{8,10},{9,11},{10,12},{11,13},... | collective-permute-start | bytes 3145736 | tf_op jit(solution)/shard_map/ppermute | solution.py:287
  347.3 28.3 %product.2 = (f32[128,48,128]{2,1,0:T(8,128)}, f32[128,48,128]{2,1,0:T(8,128)}) custom-call(s32[6]{0:T(128)} %pad_add_fusion.slot_ref, f32[48,128,128]{2,1,0:T(8,128)} %forward.4.refs_0_, f32[48,128,128]{2,1,0:T(8,128)} %collective-permute-done.refs_1_, f32[48,128,128]{2,1,0:T(8,128)} %collective-permute-done.1.refs_2_, ...), custom_call_target="tpu_custom_call" | custom-call | flops 9663676416 | bytes 47185920 | tf_op jit(solution)/shard_map/product/pallas_call | solution.py:170
  379.6 5.5 %collective-permute-start.32 = (f32[2,16,64,128]{3,2,1,0:T(8,128)}, f32[2,16,64,128]{3,2,1,0:T(8,128)}, u32[]{:S(2)}, u32[]{:S(2)}) collective-permute-start(f32[2,16,64,128]{3,2,1,0:T(8,128)} %collective-permute-done.30.refs_11_), channel_id=1, source_target_pairs={{0,2},{1,3},{2,4},{3,5},{4,6},{5,7},{8,10},{9,11},{10,12},{11,13},... | collective-permute-start | bytes 3145736 | tf_op jit(solution)/shard_map/ppermute | solution.py:287
  385.2 16.4 %collective-permute-done.23.refs_4_ = f32[16,128,128]{2,1,0:T(8,128)} collective-permute-done((f32[16,128,128]{2,1,0:T(8,128)}, f32[16,128,128]{2,1,0:T(8,128)}, u32[]{:S(2)}, u32[]{:S(2)}) %collective-permute-start.23) | collective-permute-done | bytes 1048608 | tf_op jit(solution)/shard_map/ppermute | solution.py:297
  402.6 2.3 collective-permute-done.33.refs_14_
  406.1 11.3 %product.3 = (f32[128,16,128]{2,1,0:T(8,128)}, f32[128,16,128]{2,1,0:T(8,128)}) custom-call(s32[6]{0:T(128)} %pad_add_fusion.slot_ref, f32[16,128,128]{2,1,0:T(8,128)} %get-tuple-element.18.refs_0_, f32[16,128,128]{2,1,0:T(8,128)} %copy-done.9, f32[16,128,128]{2,1,0:T(8,128)} %collective-permute-done.21.refs_2_, ...), custom_call_target="tpu_custom_call" | custom-call | flops 3221225472 | bytes 15728640 | tf_op jit(solution)/shard_map/product/pallas_call | solution.py:170
  417.4 2.9 collective-permute-done.35.refs_3_
  421.3 1.7 copy-done.3
  423.0 9.6 %inverse.1 = f32[128,128,128]{2,1,0:T(8,128)} custom-call(s32[1]{0:T(128)} %bitcast.core_ref, bf16[2,256,256]{2,1,0:T(8,128)(2,1)} %constant.66.clone.w_ref, f32[128,48,128]{2,1,0:T(8,128)} %get-tuple-element.17.refs_0_, f32[128,16,128]{2,1,0:T(8,128)} %get-tuple-element.22.refs_1_, f32[128,48,128]{2,1,0:T(8,128)} %copy-done.3, f32[128,16,128]{2,1,0:T(8,128)} %copy-done.12), custom_call_target="tpu_custom_call" | custom-call | flops 3221225472 | bytes 16777216 | tf_op jit(solution)/shard_map/inverse/pallas_call | solution.py:216
  (81 shorter events, 30.0 us)
Async XLA Ops:
  21.6 40.4 %collective-permute-start.10 = (f32[48,64,128]{2,1,0:T(8,128)}, f32[48,64,128]{2,1,0:T(8,128)}, u32[]{:S(2)}, u32[]{:S(2)}) collective-permute-start(f32[48,64,128]{2,1,0:T(8,128)} %forward.6.refs_8_), channel_id=1, source_target_pairs={{2,0},{3,1},{4,2},{5,3},{6,4},{7,5},{10,8},{11,9},{12,10},{13,11},... | collective-permute-start | bytes 4718600 | tf_op jit(solution)/shard_map/ppermute | solution.py:288
  22.8 40.4 %collective-permute-start.8 = (f32[48,64,128]{2,1,0:T(8,128)}, f32[48,64,128]{2,1,0:T(8,128)}, u32[]{:S(2)}, u32[]{:S(2)}) collective-permute-start(f32[48,64,128]{2,1,0:T(8,128)} %forward.6.refs_8_), channel_id=1, source_target_pairs={{0,2},{1,3},{2,4},{3,5},{4,6},{5,7},{8,10},{9,11},{10,12},{11,13},... | collective-permute-start | bytes 4718600 | tf_op jit(solution)/shard_map/ppermute | solution.py:287
  29.5 102.0 %collective-permute-start = (f32[48,128,128]{2,1,0:T(8,128)}, f32[48,128,128]{2,1,0:T(8,128)}, u32[]{:S(2)}, u32[]{:S(2)}) collective-permute-start(f32[48,128,128]{2,1,0:T(8,128)} %get-tuple-element.15), channel_id=1, source_target_pairs={{0,1},{1,0},{2,3},{3,2},{4,5},{5,4},{6,7},{7,6},{8,9},{9,8},{10,11... | collective-permute-start | bytes 9437192 | tf_op jit(solution)/shard_map/ppermute | solution.py:281
  29.5 25.8 %collective-permute-start.26 = (f32[16,128,128]{2,1,0:T(8,128)S(1)}, f32[16,128,128]{2,1,0:T(8,128)S(1)}, u32[]{:S(2)}, u32[]{:S(2)}) collective-permute-start(f32[16,128,128]{2,1,0:T(8,128)S(1)} %copy-done.8), channel_id=1, source_target_pairs={{8,0},{24,8},{16,24},{0,16},{9,1},{25,9},{17,25},{1,17},{10,2},{26... | collective-permute-start | bytes 3145736 | tf_op jit(solution)/shard_map/ppermute | solution.py:294
  32.8 51.5 %collective-permute-start.29 = (f32[2,16,64,128]{3,2,1,0:T(8,128)S(1)}, f32[2,16,64,128]{3,2,1,0:T(8,128)S(1)}, u32[]{:S(2)}, u32[]{:S(2)}) collective-permute-start(f32[2,16,64,128]{3,2,1,0:T(8,128)S(1)} %pad_maximum_fusion.refs_8_), channel_id=1, source_target_pairs={{2,0},{3,1},{4,2},{5,3},{6,4},{7,5},{10,8},{11,9},{12,10},{13,11},... | collective-permute-start | bytes 3145736 | tf_op jit(solution)/shard_map/ppermute | solution.py:288
  55.3 69.1 %collective-permute-start.7 = (f32[48,64,128]{2,1,0:T(8,128)}, f32[48,64,128]{2,1,0:T(8,128)}, u32[]{:S(2)}, u32[]{:S(2)}) collective-permute-start(f32[48,64,128]{2,1,0:T(8,128)} %get-tuple-element.16), channel_id=1, source_target_pairs={{0,1},{1,0},{2,3},{3,2},{4,5},{5,4},{6,7},{7,6},{8,9},{9,8},{10,11... | collective-permute-start | bytes 4718600 | tf_op jit(solution)/shard_map/ppermute | solution.py:280
  62.0 63.0 %collective-permute-start.14 = (f32[48,64,128]{2,1,0:T(8,128)}, f32[48,64,128]{2,1,0:T(8,128)}, u32[]{:S(2)}, u32[]{:S(2)}) collective-permute-start(f32[48,64,128]{2,1,0:T(8,128)} %collective-permute-done.10.refs_12_), channel_id=1, source_target_pairs={{2,0},{3,1},{4,2},{5,3},{6,4},{7,5},{10,8},{11,9},{12,10},{13,11},... | collective-permute-start | bytes 4718600 | tf_op jit(solution)/shard_map/ppermute | solution.py:288
  63.3 63.0 %collective-permute-start.12 = (f32[48,64,128]{2,1,0:T(8,128)}, f32[48,64,128]{2,1,0:T(8,128)}, u32[]{:S(2)}, u32[]{:S(2)}) collective-permute-start(f32[48,64,128]{2,1,0:T(8,128)} %collective-permute-done.8.refs_10_), channel_id=1, source_target_pairs={{0,2},{1,3},{2,4},{3,5},{4,6},{5,7},{8,10},{9,11},{10,12},{11,13},... | collective-permute-start | bytes 4718600 | tf_op jit(solution)/shard_map/ppermute | solution.py:287
  85.4 37.6 %collective-permute-start.28 = (f32[2,16,64,128]{3,2,1,0:T(8,128)S(1)}, f32[2,16,64,128]{3,2,1,0:T(8,128)}, u32[]{:S(2)}, u32[]{:S(2)}) collective-permute-start(f32[2,16,64,128]{3,2,1,0:T(8,128)S(1)} %pad_maximum_fusion.refs_8_), channel_id=1, source_target_pairs={{0,2},{1,3},{2,4},{3,5},{4,6},{5,7},{8,10},{9,11},{10,12},{11,13},... | collective-permute-start | bytes 3145736 | tf_op jit(solution)/shard_map/ppermute | solution.py:287
  123.0 71.2 %collective-permute-start.6 = (f32[48,128,128]{2,1,0:T(8,128)}, f32[48,128,128]{2,1,0:T(8,128)S(1)}, u32[]{:S(2)}, u32[]{:S(2)}) collective-permute-start(f32[48,128,128]{2,1,0:T(8,128)} %forward.4.refs_0_), channel_id=1, source_target_pairs={{8,0},{24,8},{16,24},{0,16},{9,1},{25,9},{17,25},{1,17},{10,2},{26... | collective-permute-start | bytes 9437192 | tf_op jit(solution)/shard_map/ppermute | solution.py:294
  124.4 71.1 %collective-permute-start.1 = (f32[48,128,128]{2,1,0:T(8,128)}, f32[48,128,128]{2,1,0:T(8,128)}, u32[]{:S(2)}, u32[]{:S(2)}) collective-permute-start(f32[48,128,128]{2,1,0:T(8,128)} %forward.4.refs_0_), channel_id=1, source_target_pairs={{0,8},{8,24},{24,16},{16,0},{1,9},{9,25},{25,17},{17,1},{2,10},{10... | collective-permute-start | bytes 9437192 | tf_op jit(solution)/shard_map/ppermute | solution.py:293
  125.0 36.5 %collective-permute-start.11 = (f32[48,64,128]{2,1,0:T(8,128)}, f32[48,64,128]{2,1,0:T(8,128)S(1)}, u32[]{:S(2)}, u32[]{:S(2)}) collective-permute-start(f32[48,64,128]{2,1,0:T(8,128)} %collective-permute-done.7.refs_9_), channel_id=1, source_target_pairs={{2,0},{3,1},{4,2},{5,3},{6,4},{7,5},{10,8},{11,9},{12,10},{13,11},... | collective-permute-start | bytes 4718600 | tf_op jit(solution)/shard_map/ppermute | solution.py:288
  126.3 36.5 %collective-permute-start.9 = (f32[48,64,128]{2,1,0:T(8,128)}, f32[48,64,128]{2,1,0:T(8,128)S(1)}, u32[]{:S(2)}, u32[]{:S(2)}) collective-permute-start(f32[48,64,128]{2,1,0:T(8,128)} %collective-permute-done.7.refs_9_), channel_id=1, source_target_pairs={{0,2},{1,3},{2,4},{3,5},{4,6},{5,7},{8,10},{9,11},{10,12},{11,13},... | collective-permute-start | bytes 4718600 | tf_op jit(solution)/shard_map/ppermute | solution.py:287
  131.5 127.1 %collective-permute-start.4 = (f32[48,128,128]{2,1,0:T(8,128)}, f32[48,128,128]{2,1,0:T(8,128)}, u32[]{:S(2)}, u32[]{:S(2)}) collective-permute-start(f32[48,128,128]{2,1,0:T(8,128)} %collective-permute-done.refs_1_), channel_id=1, source_target_pairs={{8,0},{24,8},{16,24},{0,16},{9,1},{25,9},{17,25},{1,17},{10,2},{26... | collective-permute-start | bytes 9437192 | tf_op jit(solution)/shard_map/ppermute | solution.py:294
  161.5 40.2 %collective-permute-start.18 = (f32[48,64,128]{2,1,0:T(8,128)}, f32[48,64,128]{2,1,0:T(8,128)S(1)}, u32[]{:S(2)}, u32[]{:S(2)}) collective-permute-start(f32[48,64,128]{2,1,0:T(8,128)} %collective-permute-done.14.refs_16_), channel_id=1, source_target_pairs={{2,0},{3,1},{4,2},{5,3},{6,4},{7,5},{10,8},{11,9},{12,10},{13,11},... | collective-permute-start | bytes 4718600 | tf_op jit(solution)/shard_map/ppermute | solution.py:288
  162.8 40.3 %collective-permute-start.16 = (f32[48,64,128]{2,1,0:T(8,128)}, f32[48,64,128]{2,1,0:T(8,128)S(1)}, u32[]{:S(2)}, u32[]{:S(2)}) collective-permute-start(f32[48,64,128]{2,1,0:T(8,128)} %collective-permute-done.12.refs_14_), channel_id=1, source_target_pairs={{0,2},{1,3},{2,4},{3,5},{4,6},{5,7},{8,10},{9,11},{10,12},{11,13},... | collective-permute-start | bytes 4718600 | tf_op jit(solution)/shard_map/ppermute | solution.py:287
  194.2 65.9 %collective-permute-start.15 = (f32[48,64,128]{2,1,0:T(8,128)S(1)}, f32[48,64,128]{2,1,0:T(8,128)}, u32[]{:S(2)}, u32[]{:S(2)}) collective-permute-start(f32[48,64,128]{2,1,0:T(8,128)S(1)} %collective-permute-done.11.refs_13_), channel_id=1, source_target_pairs={{2,0},{3,1},{4,2},{5,3},{6,4},{7,5},{10,8},{11,9},{12,10},{13,11},... | collective-permute-start | bytes 4718600 | tf_op jit(solution)/shard_map/ppermute | solution.py:288
  195.5 65.9 %collective-permute-start.13 = (f32[48,64,128]{2,1,0:T(8,128)S(1)}, f32[48,64,128]{2,1,0:T(8,128)}, u32[]{:S(2)}, u32[]{:S(2)}) collective-permute-start(f32[48,64,128]{2,1,0:T(8,128)S(1)} %collective-permute-done.9.refs_11_), channel_id=1, source_target_pairs={{0,2},{1,3},{2,4},{3,5},{4,6},{5,7},{8,10},{9,11},{10,12},{11,13},... | collective-permute-start | bytes 4718600 | tf_op jit(solution)/shard_map/ppermute | solution.py:287
  201.8 95.8 %collective-permute-start.3 = (f32[48,128,128]{2,1,0:T(8,128)}, f32[48,128,128]{2,1,0:T(8,128)}, u32[]{:S(2)}, u32[]{:S(2)}) collective-permute-start(f32[48,128,128]{2,1,0:T(8,128)} %collective-permute-done.1.refs_2_), channel_id=1, source_target_pairs={{0,8},{8,24},{24,16},{16,0},{1,9},{9,25},{25,17},{17,1},{2,10},{10... | collective-permute-start | bytes 9437192 | tf_op jit(solution)/shard_map/ppermute | solution.py:297
  203.1 137.3 %collective-permute-start.2 = (f32[48,128,128]{2,1,0:T(8,128)}, f32[48,128,128]{2,1,0:T(8,128)}, u32[]{:S(2)}, u32[]{:S(2)}) collective-permute-start(f32[48,128,128]{2,1,0:T(8,128)} %collective-permute-done.refs_1_), channel_id=1, source_target_pairs={{0,8},{8,24},{24,16},{16,0},{1,9},{9,25},{25,17},{17,1},{2,10},{10... | collective-permute-start | bytes 9437192 | tf_op jit(solution)/shard_map/ppermute | solution.py:293
  258.6 83.1 %collective-permute-start.5 = (f32[48,128,128]{2,1,0:T(8,128)}, f32[48,128,128]{2,1,0:T(8,128)}, u32[]{:S(2)}, u32[]{:S(2)}) collective-permute-start(f32[48,128,128]{2,1,0:T(8,128)} %collective-permute-done.4.refs_7_), channel_id=1, source_target_pairs={{8,0},{24,8},{16,24},{0,16},{9,1},{25,9},{17,25},{1,17},{10,2},{26... | collective-permute-start | bytes 9437192 | tf_op jit(solution)/shard_map/ppermute | solution.py:297
  260.0 34.8 %collective-permute-start.19 = (f32[48,64,128]{2,1,0:T(8,128)}, f32[48,64,128]{2,1,0:T(8,128)}, u32[]{:S(2)}, u32[]{:S(2)}) collective-permute-start(f32[48,64,128]{2,1,0:T(8,128)} %collective-permute-done.15.refs_17_), channel_id=1, source_target_pairs={{2,0},{3,1},{4,2},{5,3},{6,4},{7,5},{10,8},{11,9},{12,10},{13,11},... | collective-permute-start | bytes 4718600 | tf_op jit(solution)/shard_map/ppermute | solution.py:288
  261.4 35.8 %collective-permute-start.17 = (f32[48,64,128]{2,1,0:T(8,128)}, f32[48,64,128]{2,1,0:T(8,128)}, u32[]{:S(2)}, u32[]{:S(2)}) collective-permute-start(f32[48,64,128]{2,1,0:T(8,128)} %collective-permute-done.13.refs_15_), channel_id=1, source_target_pairs={{0,2},{1,3},{2,4},{3,5},{4,6},{5,7},{8,10},{9,11},{10,12},{11,13},... | collective-permute-start | bytes 4718600 | tf_op jit(solution)/shard_map/ppermute | solution.py:287
  294.8 80.7 %collective-permute-start.21 = (f32[16,128,128]{2,1,0:T(8,128)}, f32[16,128,128]{2,1,0:T(8,128)}, u32[]{:S(2)}, u32[]{:S(2)}) collective-permute-start(f32[16,128,128]{2,1,0:T(8,128)} %get-tuple-element.18.refs_0_), channel_id=1, source_target_pairs={{0,8},{8,24},{24,16},{16,0},{1,9},{9,25},{25,17},{17,1},{2,10},{10... | collective-permute-start | bytes 3145736 | tf_op jit(solution)/shard_map/ppermute | solution.py:293
  297.2 78.5 %collective-permute-start.24 = (f32[16,128,128]{2,1,0:T(8,128)}, f32[16,128,128]{2,1,0:T(8,128)}, u32[]{:S(2)}, u32[]{:S(2)}) collective-permute-start(f32[16,128,128]{2,1,0:T(8,128)} %copy-done.9), channel_id=1, source_target_pairs={{8,0},{24,8},{16,24},{0,16},{9,1},{25,9},{17,25},{1,17},{10,2},{26... | collective-permute-start | bytes 3145736 | tf_op jit(solution)/shard_map/ppermute | solution.py:294
  297.6 80.5 %collective-permute-start.22 = (f32[16,128,128]{2,1,0:T(8,128)}, f32[16,128,128]{2,1,0:T(8,128)}, u32[]{:S(2)}, u32[]{:S(2)}) collective-permute-start(f32[16,128,128]{2,1,0:T(8,128)} %copy-done.9), channel_id=1, source_target_pairs={{0,8},{8,24},{24,16},{16,0},{1,9},{9,25},{25,17},{17,1},{2,10},{10... | collective-permute-start | bytes 3145736 | tf_op jit(solution)/shard_map/ppermute | solution.py:293
  340.5 37.9 %collective-permute-start.31 = (f32[2,16,64,128]{3,2,1,0:T(8,128)}, f32[2,16,64,128]{3,2,1,0:T(8,128)}, u32[]{:S(2)}, u32[]{:S(2)}) collective-permute-start(f32[2,16,64,128]{3,2,1,0:T(8,128)} %copy-done.11), channel_id=1, source_target_pairs={{2,0},{3,1},{4,2},{5,3},{6,4},{7,5},{10,8},{11,9},{12,10},{13,11},... | collective-permute-start | bytes 3145736 | tf_op jit(solution)/shard_map/ppermute | solution.py:288
  341.8 37.9 %collective-permute-start.30 = (f32[2,16,64,128]{3,2,1,0:T(8,128)}, f32[2,16,64,128]{3,2,1,0:T(8,128)}, u32[]{:S(2)}, u32[]{:S(2)}) collective-permute-start(f32[2,16,64,128]{3,2,1,0:T(8,128)} %collective-permute-done.28.refs_9_), channel_id=1, source_target_pairs={{0,2},{1,3},{2,4},{3,5},{4,6},{5,7},{8,10},{9,11},{10,12},{11,13},... | collective-permute-start | bytes 3145736 | tf_op jit(solution)/shard_map/ppermute | solution.py:287
  375.6 44.8 %collective-permute-start.34 = (f32[128,48,128]{2,1,0:T(8,128)}, f32[128,48,128]{2,1,0:T(8,128)S(1)}, u32[]{:S(2)}, u32[]{:S(2)}) collective-permute-start(f32[128,48,128]{2,1,0:T(8,128)} %get-tuple-element.23), channel_id=1, source_target_pairs={{0,1},{1,0},{2,3},{3,2},{4,5},{5,4},{6,7},{7,6},{8,9},{9,8},{10,11... | collective-permute-start | bytes 9437192 | tf_op jit(solution)/shard_map/ppermute | solution.py:300
  375.6 25.9 %collective-permute-start.23 = (f32[16,128,128]{2,1,0:T(8,128)}, f32[16,128,128]{2,1,0:T(8,128)}, u32[]{:S(2)}, u32[]{:S(2)}) collective-permute-start(f32[16,128,128]{2,1,0:T(8,128)} %collective-permute-done.21.refs_2_), channel_id=1, source_target_pairs={{0,8},{8,24},{24,16},{16,0},{1,9},{9,25},{25,17},{17,1},{2,10},{10... | collective-permute-start | bytes 3145736 | tf_op jit(solution)/shard_map/ppermute | solution.py:297
  378.3 26.5 %collective-permute-start.33 = (f32[2,16,64,128]{3,2,1,0:T(8,128)}, f32[2,16,64,128]{3,2,1,0:T(8,128)}, u32[]{:S(2)}, u32[]{:S(2)}) collective-permute-start(f32[2,16,64,128]{3,2,1,0:T(8,128)} %collective-permute-done.31.refs_12_), channel_id=1, source_target_pairs={{2,0},{3,1},{4,2},{5,3},{6,4},{7,5},{10,8},{11,9},{12,10},{13,11},... | collective-permute-start | bytes 3145736 | tf_op jit(solution)/shard_map/ppermute | solution.py:288
  379.6 26.4 %collective-permute-start.32 = (f32[2,16,64,128]{3,2,1,0:T(8,128)}, f32[2,16,64,128]{3,2,1,0:T(8,128)}, u32[]{:S(2)}, u32[]{:S(2)}) collective-permute-start(f32[2,16,64,128]{3,2,1,0:T(8,128)} %collective-permute-done.30.refs_11_), channel_id=1, source_target_pairs={{0,2},{1,3},{2,4},{3,5},{4,6},{5,7},{8,10},{9,11},{10,12},{11,13},... | collective-permute-start | bytes 3145736 | tf_op jit(solution)/shard_map/ppermute | solution.py:287
  (18 other events, 857.5 us)

commit v2 on v1

--- a/solution.py
+++ b/solution.py
@@ -12,7 +12,7 @@
 
 NT = 128
 NF = 64
-SHARES = (24, 8)
+SHARES = (20, 12)
 F32, BF16 = jnp.float32, jnp.bfloat16
 
 
@@ -67,8 +67,9 @@
     lax.fori_loop(0, rows // group, some, 0)
 
 
-def forward(x, core, cuts):
-    n, m, t = x.shape
+def forward(x, core, cuts, start=0, n=None):
+    m, t = x.shape[1:]
+    n = x.shape[0] if n is None else n
     table = by_core(tables()[0])
     table = np.concatenate([table[:, a:b] for a, b in cuts], axis=1)
     counts = [b - a for a, b in cuts]
@@ -77,7 +78,7 @@
     w = np.concatenate(
         [np.concatenate([high, high], axis=2), np.concatenate([low, np.zeros_like(low)], axis=2)], axis=1
     )
-    step = 32
+    step = 32 if n > 64 else 16
     return pl.pallas_call(
         functools.partial(forward_kernel, counts),
         grid_spec=pltpu.PrefetchScalarGridSpec(
@@ -85,109 +86,180 @@
             grid=(n // step,),
             in_specs=[
                 pl.BlockSpec((1,) + w.shape[1:], lambda i, c: (c[0], 0, 0)),
-                pl.BlockSpec((step, m, t), lambda i, c: (i, 0, 0)),
+                pl.BlockSpec((step, m, t), lambda i, c: (i + start // step, 0, 0)),
             ],
             out_specs=[pl.BlockSpec((s.shape[0], step, m), lambda i, c: (0, i, 0)) for s in shapes],
         ),
         out_shape=shapes,
-        cost_estimate=pl.CostEstimate(flops=12 * x.size * NT, bytes_accessed=8 * x.size, transcendentals=0),
+        cost_estimate=pl.CostEstimate(
+            flops=12 * n * m * t * NT, bytes_accessed=8 * n * m * t, transcendentals=0
+        ),
         name="forward",
     )(core, jnp.asarray(w), x)
 
 
-def product_kernel(blocks, slot_ref, *refs):
-    d_refs, g_refs = refs[: 2 * blocks], list(refs[2 * blocks : -5])
-    out_a, out_b, lhs, rhs, held = refs[-5:]
-    if g_refs[0].ndim == 4:
-        g_refs = [ref.at[h] for ref in g_refs for h in range(2)]
-    count = d_refs[0].shape[0] // 2
-    rows, depth = d_refs[0].shape[1:]
-    half, cols = g_refs[0].shape[1:]
-    core = slot_ref[blocks]
-    base_low = 2 * depth * blocks
+ALL, EARLY, LATE = range(3)
+
+
+def sides(part, levels):
+    pairs = [[("own", 0)]] + [[("up", s), ("down", levels - s)] for s in range(1, levels)]
+    return [[x for x in pair if part != EARLY or x[1] < levels - 1] for pair in pairs]
+
+
+def product_kernel(part, levels, places, d_keys, g_keys, slot_ref, *refs):
+    d_refs = {}
+    for (a, at), ref in zip(d_keys, refs):
+        d_refs.setdefault(a, []).append((at, ref))
+    g_refs = {}
+    for (way, hop, h), ref in zip(g_keys, refs[len(d_keys) :]):
+        for i in range(2) if h is None else (h,):
+            g_refs[way, hop, i] = ref.at[i] if h is None else ref
+    rest = refs[len(d_keys) + len(g_keys) :]
+    lhs, rhs = rest[-2:]
+    count = refs[0].shape[0] // 2
+    depth = refs[0].shape[2]
+    rows = lhs.shape[1] // 4
+    half, cols = next(iter(g_refs.values())).shape[1:]
+    core, chosen, far = (slot_ref[levels + i] for i in range(3))
     step, steps = pl.program_id(0), pl.num_programs(0)
+
+    def put_g(b, slot, h, half_of, g):
+        high, low = split(g)
+        place = jnp.where(core == h, 0, half)
+        at = pl.multiple_of(slot * 3 * depth + place, half)
+        to = slice(half_of * cols, (half_of + 1) * cols)
+        for i, value in enumerate((high, high, low)):
+            rhs[b % 2, pl.ds(at + i * depth, half), to] = value
+
+    def put_d(b, place, a):
+        for at, ref in d_refs[a]:
+            for half_of in range(2):
+                high, low = split(ref[2 * b + half_of])
+                first = 2 * rows * half_of + at
+                for i, value in enumerate((high, low, high)):
+                    to = slice((3 * place + i) * depth, (3 * place + i + 1) * depth)
+                    lhs[b % 2, first : first + ref.shape[1], to] = value
+
     for b in range(count):
-        for s in range(blocks):
-            slot = slot_ref[s]
-            for h in range(2):
-                place = jnp.where(core == h, 0, half)
-                for part in range(2):
-                    if s == 0:
-                        g = g_refs[h][2 * b + part]
-                    else:
-                        up = g_refs[2 + 4 * (s - 1) + h]
-                        down = g_refs[2 + 4 * (blocks - s - 1) + 2 + h]
-                        g = up[2 * b + part] + down[2 * b + part]
-                    high, low = split(g)
-                    at = pl.multiple_of(slot * 2 * depth + place, half)
-                    to = slice(part * cols, (part + 1) * cols)
-                    rhs[b % 2, pl.ds(at, half), to] = high
-                    rhs[b % 2, pl.ds(at + depth, half), to] = high
-                    rhs[b % 2, pl.ds(pl.multiple_of(base_low + slot * depth + place, half), half), to] = low
-        for a in range(blocks):
-            for h in range(2):
-                for part in range(2):
-                    high, low = split(d_refs[2 * a + h][2 * b + part])
-                    to = slice((2 * part + h) * rows, (2 * part + h + 1) * rows)
-                    lhs[b % 2, to, 2 * a * depth : (2 * a + 1) * depth] = high
-                    lhs[b % 2, to, (2 * a + 1) * depth : (2 * a + 2) * depth] = low
-                    lhs[b % 2, to, base_low + a * depth : base_low + (a + 1) * depth] = high
-        p = jnp.dot(lhs[b % 2], rhs[b % 2], preferred_element_type=F32)
+        for h in range(2):
+            for half_of in range(2):
+                row = 2 * b + half_of
+                for s, pair in enumerate(sides(part, levels)):
+                    put_g(b, slot_ref[s], h, half_of, sum(g_refs[way, hop, h][row] for way, hop in pair))
+                if part == LATE:
+                    last = g_refs["up", levels - 1, h][row] + g_refs["down", levels - 1, h][row]
+                    put_g(b, 1, h, half_of, jnp.where(far > 0, last, 0.0))
+        for place, which in enumerate(places):
+            if len(which) == 1:
+                put_d(b, place, which[0])
+            else:
+                for a in which:
+                    pl.when(chosen == a)(functools.partial(put_d, b, place, a))
+        deep = 3 * depth * len(places)
+        p = jnp.dot(lhs[b % 2, :, :deep], rhs[b % 2, :deep, :], preferred_element_type=F32)
+        real = p[: 2 * rows, :cols] - p[2 * rows :, cols:]
+        imaginary = p[: 2 * rows, cols:] + p[2 * rows :, :cols]
+        if part == EARLY:
+            rest[0][2 * b], rest[0][2 * b + 1] = real, imaginary
+            continue
+        if part == LATE:
+            real, imaginary = real + rest[0][2 * b], imaginary + rest[0][2 * b + 1]
+        held = rest[-3]
         row = 2 * (step * count + b)
-        held[row] = p[: 2 * rows, :cols] - p[2 * rows :, cols:]
-        held[row + 1] = p[: 2 * rows, cols:] + p[2 * rows :, :cols]
-
-    @pl.when(step == steps - 1)
-    def _():
-        for c in range(held.shape[0]):
-            out_a[:, c, :] = held[c, :rows]
-            out_b[:, c, :] = held[c, rows:]
-
-
-def product(slots, d, g):
-    blocks = len(d) // 2
-    n, rows, depth = d[0].shape
-    _, cols = g[0].shape[-2:]
+        held[row], held[row + 1] = real, imaginary
+
+    if part != EARLY:
+
+        @pl.when(step == steps - 1)
+        def _():
+            out_a, out_b, held = rest[-5:-2]
+            for c in range(held.shape[0]):
+                out_a[:, c, :] = held[c, :rows]
+                out_b[:, c, :] = held[c, rows:]
+
+
+def product(part, me, d, g, so_far=None):
+    slot, core, z = me
+    levels = slot.shape[0]
+    around = len(d)
+    diag = around // 2
+    depth = d[0][0].shape[2]
+    n = d[0][0].shape[0]
+    rows = sum(x.shape[1] for x in d[0]) // 2
+    _, cols = g["own", 0][0].shape[-2:]
     step = 4
-    out = jax.ShapeDtypeStruct((rows, n, cols), F32)
-    each = 1 if g[0].ndim == 4 else 2
-
-    def spec(x, hop=None):
-        def at(i, c):
-            if hop is None:
-                return i
-            z = c[blocks + 1]
-            there = z >= hop[1] if hop[0] else z + hop[1] < blocks
-            return jnp.where(there, i, 0)
-
+
+    far_s = jnp.where(z == 0, 1, levels - 1)
+    far_a = slot[far_s]
+    far = ((z == 0) | (z == levels - 1)) & (far_a != diag)
+    chosen = jnp.where(far, far_a, 0)
+    others = [a for a in range(around) if a != diag]
+    if part == ALL:
+        places, to = [[a] for a in range(around)], slot
+    elif part == EARLY:
+        index = np.array([others.index(a) if a in others else len(others) for a in range(around)])
+        places, to = [[a] for a in others], jnp.asarray(index)[slot]
+    else:
+        places, to = [[diag], others], jnp.where(slot == diag, 0, 2)
+    scalars = [to, jnp.stack([core, chosen, far.astype(jnp.int32)])]
+
+    operands, d_keys, g_keys, needed = [], [], [], []
+    for a in sorted(set(sum(places, []))):
+        at = 0
+        for x in d[a]:
+            d_keys.append((a, at))
+            operands.append(x)
+            needed.append(jnp.where(chosen == a, 1, 0) if part == LATE and a != diag else 1)
+            at += x.shape[1]
+    for s, pair in enumerate(sides(part, levels)):
+        for way, hop in pair:
+            there = {"own": True, "up": z >= hop, "down": z + hop < levels}[way]
+            if part == LATE:
+                there = there & ((slot[s] == diag) | (hop == levels - 1))
+            for h, x in enumerate(g[way, hop]):
+                g_keys.append((way, hop, h if len(g[way, hop]) == 2 else None))
+                operands.append(x)
+                needed.append(jnp.where(there, 1, 0))
+    if so_far is not None:
+        operands.append(so_far)
+        needed.append(1)
+    scalars.append(jnp.stack([jnp.asarray(x, jnp.int32) for x in needed]))
+    scalars = jnp.concatenate([x.astype(jnp.int32) for x in scalars])
+    first = levels + 3
+
+    def spec(i, x):
+        at = lambda j, c: jnp.where(c[first + i] > 0, j, 0)
         if x.ndim == 4:
-            return pl.BlockSpec((2, step) + x.shape[2:], lambda i, c: (0, at(i, c), 0, 0))
-        return pl.BlockSpec((step,) + x.shape[1:], lambda i, c: (at(i, c), 0, 0))
-
-    hops = [None] * each
-    for s in range(1, blocks):
-        hops += [(True, s)] * each + [(False, s)] * each
+            return pl.BlockSpec((2, step) + x.shape[2:], lambda j, c: (0, at(j, c), 0, 0))
+        return pl.BlockSpec((step,) + x.shape[1:], lambda j, c: (at(j, c), 0, 0))
+
+    scratch = [
+        pltpu.VMEM((2, 4 * rows, 3 * depth * len(places)), BF16),
+        pltpu.VMEM((2, 3 * depth * (len(places) + 1), 2 * cols), BF16),
+    ]
+    if part == EARLY:
+        out = jax.ShapeDtypeStruct((n, 2 * rows, cols), F32)
+        out_specs = pl.BlockSpec((step, 2 * rows, cols), lambda i, c: (i, 0, 0))
+    else:
+        out = [jax.ShapeDtypeStruct((rows, n, cols), F32)] * 2
+        out_specs = [pl.BlockSpec((rows, n, cols), lambda i, c: (0, 0, 0))] * 2
+        scratch = [pltpu.VMEM((n, 2 * rows, cols), F32)] + scratch
     return pl.pallas_call(
-        functools.partial(product_kernel, blocks),
+        functools.partial(product_kernel, part, levels, places, d_keys, g_keys),
         grid_spec=pltpu.PrefetchScalarGridSpec(
             num_scalar_prefetch=1,
             grid=(n // step,),
-            in_specs=[spec(x) for x in d] + [spec(x, hop) for x, hop in zip(g, hops)],
-            out_specs=[pl.BlockSpec((rows, n, cols), lambda i, c: (0, 0, 0))] * 2,
-            scratch_shapes=[
-                pltpu.VMEM((2, 4 * rows, 3 * blocks * depth), BF16),
-                pltpu.VMEM((2, 3 * blocks * depth, 2 * cols), BF16),
-                pltpu.VMEM((n, 2 * rows, cols), F32),
-            ],
-        ),
-        out_shape=[out, out],
+            in_specs=[spec(i, x) for i, x in enumerate(operands)],
+            out_specs=out_specs,
+            scratch_shapes=scratch,
+        ),
+        out_shape=out,
         cost_estimate=pl.CostEstimate(
-            flops=n // 2 * 2 * 4 * rows * 3 * blocks * depth * 2 * cols,
-            bytes_accessed=4 * sum(x.size for x in list(d) + list(g)),
+            flops=n // 2 * 2 * 4 * rows * 3 * len(places) * depth * 2 * cols,
+            bytes_accessed=4 * sum(x.size for x in operands),
             transcendentals=0,
         ),
-        name="product",
-    )(slots, *d, *g)
+    )(scalars, *operands)
 
 
 def inverse_kernel(core_ref, w_ref, *refs):
@@ -265,38 +337,50 @@
     bins = bins_of(half)
     chunks = len(bins)
     where = jnp.asarray(np.argsort(ring), jnp.int32)
-    slots = (at - where[(z - jnp.arange(levels)) % levels]) % around
-    slots = jnp.concatenate([slots.astype(jnp.int32), core_at, z.astype(jnp.int32).reshape(1)])
+    slot = ((at - where[(z - jnp.arange(levels)) % levels]) % around).astype(jnp.int32)
+    me = (slot, core.astype(jnp.int32), z)
     edges = [int(e) for e in np.cumsum([0] + [2 * b for b in bins])]
     cuts = list(zip(edges[:-1], edges[1:]))
     cuts += [(NF + a, NF + b) for a, b in cuts]
 
-    g_parts, d_parts = [], []
-    for which in (cuts[:1], cuts[1:]):
-        for x, to in ((panels, g_parts), (recorded, d_parts)):
-            to += forward(x, core_at, which)
+    def transform(*args):
+        return list(forward(*args))
+
+    n = recorded.shape[0]
+    ahead = n // 4
+    head = transform(recorded, core_at, cuts[:1], 0, ahead)
+    g_parts = transform(panels, core_at, cuts[:1])
+    d_parts = transform(recorded, core_at, cuts[:1], ahead, n - ahead)
+    g_parts += transform(panels, core_at, cuts[1:])
+    d_parts += transform(recorded, core_at, cuts[1:])
     ms = []
     for c in range(chunks):
         g_own = [g_parts[c], lax.ppermute(g_parts[chunks + c], "src", partner)]
-        d_own = [d_parts[c], lax.ppermute(d_parts[chunks + c], "src", partner)]
+        d_swapped = lax.ppermute(d_parts[chunks + c], "src", partner)
+        d_own = [d_parts[c], d_swapped] if c else head + [d_parts[c], d_swapped]
         if c:
             g_own = [jnp.stack(g_own)]
-        g = list(g_own)
+        g = {("own", 0): g_own}
         up, down = g_own, g_own
-        for _ in range(1, levels):
+        for s in range(1, levels):
             up = [lax.ppermute(x, "src", upward) for x in up]
             down = [lax.ppermute(x, "src", downward) for x in down]
-            g += up + down
-        d = [d_own] + [None] * (around - 1)
+            g["up", s], g["down", s] = up, down
+        d = {0: d_own}
         right, left = d_own, d_own
         for a in range(1, around // 2):
             right = [lax.ppermute(x, "freq", clockwise) for x in right]
             left = [lax.ppermute(x, "freq", counter) for x in left]
             d[a], d[around - a] = right, left
         last = around // 2
-        d[last] = [lax.ppermute(right[0], "freq", clockwise), lax.ppermute(left[1], "freq", counter)]
-        d = [x for pair in d for x in pair]
-        m = product(slots, d, g)
+        mine = len(d_own) - 1
+        d[last] = [lax.ppermute(x, "freq", clockwise) for x in right[:mine]]
+        d[last].append(lax.ppermute(left[mine], "freq", counter))
+        if c < chunks - 1:
+            m = product(ALL, me, d, g)
+        else:
+            m = product(EARLY, me, d, g)
+            m = product(LATE, me, d, g, m)
         ms.append([m[0], lax.ppermute(m[1], "src", partner)])
     return inverse([m[0] for m in ms] + [m[1] for m in ms], core_at)
 

time: 435 us -> 462 us (1.062)
  Pallas kernels: 78.9 us -> 97.2 us
  waiting for transfers between devices: 269 us -> 279 us
  starting transfers between devices: 78.1 us -> 71.7 us
    ppermute x6 -> x7, waiting for transfers between devices: 17.5 us -> 90.3 us  [the longest x3 90.3 us: local(): d[last] = [lax.ppermute(x, 'freq', clockwise) for x in right[:mine]]]
    ppermute x4 -> x5, waiting for transfers between devices: 102 us -> 34.7 us  [local(): left = [lax.ppermute(x, 'freq', counter) for x in left]]
    ppermute x9, waiting for transfers between devices: 79.3 us -> 118 us  [local(): down = [lax.ppermute(x, 'src', downward) for x in down]]
    ppermute x4 -> x5, waiting for transfers between devices: 42.2 us -> 8.21 us  [local(): right = [lax.ppermute(x, 'freq', clockwise) for x in right]]
    pallas_call x2 -> x3, Pallas kernels: 39.6 us -> 54.3 us  [product(): pl.pallas_call(functools.partial(product_kernel, part, levels, places, d_...]
    ppermute x9, starting transfers between devices: 50.7 us -> 40.1 us  [local(): up = [lax.ppermute(x, 'src', upward) for x in up]]
    ppermute x4 -> x5, starting transfers between devices: 5.52 us -> 9.53 us  [local(): right = [lax.ppermute(x, 'freq', clockwise) for x in right]]
    pallas_call x4 -> x5, Pallas kernels: 29.7 us -> 33.2 us  [forward(): pl.pallas_call(functools.partial(forward_kernel, counts), grid_spec=pltpu...]
  transfers between devices with their start and end apart: 36 -> 39, of which waited for: 15 -> 19; matrix products, arithmetic and copies ran while one was open for 1% -> 1% of each run, Pallas kernels for 14% -> 18%
where the time goes in v2:
time: 462 us; the launch traced here: 461 us
  waiting for transfers between devices  279 us (60%)
  Pallas kernels  97.2 us (21%)
  starting transfers between devices  71.7 us (16%)
  local copies, waits for them, and re-layouts  7.25 us (2%)
    ppermute x9, waiting for transfers between devices, local(): down = [lax.ppermute(x, 'src', downward) for x in down]  118 us
    ppermute x3, waiting for transfers between devices, local(): d[last] = [lax.ppermute(x, 'freq', clockwise) for x in right[:mine]]  90.3 us
    pallas_call x3, Pallas kernels, product(): pl.pallas_call(functools.partial(product_kernel, part, levels, places, d_...  54.3 us
    ppermute x9, starting transfers between devices, local(): up = [lax.ppermute(x, 'src', upward) for x in up]  40.1 us
    ppermute x5, waiting for transfers between devices, local(): left = [lax.ppermute(x, 'freq', counter) for x in left]  34.7 us
    pallas_call x5, Pallas kernels, forward(): pl.pallas_call(functools.partial(forward_kernel, counts), grid_spec=pltpu...  33.2 us
    ppermute x9, waiting for transfers between devices, local(): up = [lax.ppermute(x, 'src', upward) for x in up]  24.1 us
    ppermute x9, starting transfers between devices, local(): down = [lax.ppermute(x, 'src', downward) for x in down]  11.6 us
  transfers between devices with their start and end apart: 39, of which 19 were waited for; matrix products, arithmetic and copies ran while one was open for 1% of the time, Pallas kernels for 18%

profile of v2, /device:TPU:0, one launch (start us, length us, event | category | flops | bytes accessed | tf_op | source)
XLA Modules:
  0.0 461.0 jit_solution(1022967333241808695)
XLA Ops:
  0.0 3.3 forward.5.refs_0_
  6.3 6.5 %forward.9 = (f32[24,64,128]{2,1,0:T(8,128)}, f32[40,64,128]{2,1,0:T(8,128)}, f32[24,64,128]{2,1,0:T(8,128)}) custom-call(s32[1]{0:T(128)} %bitcast.core_ref, bf16[2,176,256]{2,1,0:T(8,128)(2,1)} %constant.87.clone.w_ref, f32[64,128,128]{2,1,0:T(8,128)} %x_ref.9), custom_call_target="tpu_custom_call" | custom-call | flops 1610612736 | bytes 8388608 | tf_op jit(solution)/shard_map/forward/pallas_call | solution.py:82
  13.0 5.4 %forward.8.refs_12_ = f32[40,64,128]{2,1,0:T(8,128)} custom-call(s32[1]{0:T(128)} %bitcast.core_ref, bf16[2,80,256]{2,1,0:T(8,128)(2,1)} %constant.86.clone.w_ref, f32[64,128,128]{2,1,0:T(8,128)} %x_ref.9), custom_call_target="tpu_custom_call" | custom-call | flops 1610612736 | bytes 8388608 | tf_op jit(solution)/shard_map/forward/pallas_call | solution.py:82
  19.7 5.6 %collective-permute-start.11 = (f32[40,64,128]{2,1,0:T(8,128)}, f32[40,64,128]{2,1,0:T(8,128)}, u32[]{:S(2)}, u32[]{:S(2)}) collective-permute-start(f32[40,64,128]{2,1,0:T(8,128)} %forward.8.refs_12_), channel_id=1, source_target_pairs={{0,2},{1,3},{2,4},{3,5},{4,6},{5,7},{8,10},{9,11},{10,12},{11,13},... | collective-permute-start | bytes 3932168 | tf_op jit(solution)/shard_map/ppermute | solution.py:366
  25.3 10.6 %forward.7 = (f32[24,128,128]{2,1,0:T(8,128)}, f32[40,128,128]{2,1,0:T(8,128)}, f32[24,128,128]{2,1,0:T(8,128)}) custom-call(s32[1]{0:T(128)} %bitcast.core_ref, bf16[2,176,256]{2,1,0:T(8,128)(2,1)} %constant.87.clone.w_ref, f32[128,128,128]{2,1,0:T(8,128)} %x_ref.7), custom_call_target="tpu_custom_call" | custom-call | flops 3221225472 | bytes 16777216 | tf_op jit(solution)/shard_map/forward/pallas_call | solution.py:82
  39.1 7.3 %forward.6.refs_1_ = f32[40,96,128]{2,1,0:T(8,128)} custom-call(s32[1]{0:T(128)} %bitcast.core_ref, bf16[2,80,256]{2,1,0:T(8,128)(2,1)} %constant.86.clone.w_ref, f32[128,128,128]{2,1,0:T(8,128)} %x_ref.7), custom_call_target="tpu_custom_call" | custom-call | flops 2415919104 | bytes 12582912 | tf_op jit(solution)/shard_map/forward/pallas_call | solution.py:82
  46.4 5.3 %collective-permute-done.13.refs_24_ = f32[40,64,128]{2,1,0:T(8,128)} collective-permute-done((f32[40,64,128]{2,1,0:T(8,128)}, f32[40,64,128]{2,1,0:T(8,128)}, u32[]{:S(2)}, u32[]{:S(2)}) %collective-permute-start.13) | collective-permute-done | bytes 1310752 | tf_op jit(solution)/shard_map/ppermute | solution.py:367
  54.9 75.3 %collective-permute-done.4.refs_6_ = f32[40,32,128]{2,1,0:T(8,128)S(1)} collective-permute-done((f32[40,32,128]{2,1,0:T(8,128)S(1)}, f32[40,32,128]{2,1,0:T(8,128)S(1)}, u32[]{:S(2)}, u32[]{:S(2)}) %collective-permute-start.4) | collective-permute-done | bytes 655392 | tf_op jit(solution)/shard_map/ppermute | solution.py:377
  134.9 4.6 %collective-permute-start.31 = (f32[2,24,64,128]{3,2,1,0:T(8,128)S(1)}, f32[2,24,64,128]{3,2,1,0:T(8,128)S(1)}, u32[]{:S(2)}, u32[]{:S(2)}) collective-permute-start(f32[2,24,64,128]{3,2,1,0:T(8,128)S(1)} %pad_maximum_fusion.refs_6_.refs_8_), channel_id=1, source_target_pairs={{0,2},{1,3},{2,4},{3,5},{4,6},{5,7},{8,10},{9,11},{10,12},{11,13},... | collective-permute-start | bytes 4718600 | tf_op jit(solution)/shard_map/ppermute | solution.py:366
  140.9 34.7 %collective-permute-done.9.refs_10_ = f32[40,96,128]{2,1,0:T(8,128)S(1)} collective-permute-done((f32[40,96,128]{2,1,0:T(8,128)}, f32[40,96,128]{2,1,0:T(8,128)S(1)}, u32[]{:S(2)}, u32[]{:S(2)}) %collective-permute-start.9) | collective-permute-done | bytes 1966112 | tf_op jit(solution)/shard_map/ppermute | solution.py:373
  181.3 19.6 %collective-permute-done.16.refs_25_ = f32[40,64,128]{2,1,0:T(8,128)S(1)} collective-permute-done((f32[40,64,128]{2,1,0:T(8,128)S(1)}, f32[40,64,128]{2,1,0:T(8,128)S(1)}, u32[]{:S(2)}, u32[]{:S(2)}) %collective-permute-start.16) | collective-permute-done | bytes 1310752 | tf_op jit(solution)/shard_map/ppermute | solution.py:367
  208.7 20.2 %collective-permute-done.14.refs_20_ = f32[40,64,128]{2,1,0:T(8,128)S(1)} collective-permute-done((f32[40,64,128]{2,1,0:T(8,128)}, f32[40,64,128]{2,1,0:T(8,128)S(1)}, u32[]{:S(2)}, u32[]{:S(2)}) %collective-permute-start.14) | collective-permute-done | bytes 1310752 | tf_op jit(solution)/shard_map/ppermute | solution.py:367
  229.0 3.2 collective-permute-start.35
  232.1 3.5 collective-permute-done.19.refs_18_
  237.0 6.3 %collective-permute-start.20 = (f32[40,64,128]{2,1,0:T(8,128)S(1)}, f32[40,64,128]{2,1,0:T(8,128)}, u32[]{:S(2)}, u32[]{:S(2)}) collective-permute-start(f32[40,64,128]{2,1,0:T(8,128)S(1)} %collective-permute-done.12.refs_15_), channel_id=1, source_target_pairs={{0,2},{1,3},{2,4},{3,5},{4,6},{5,7},{8,10},{9,11},{10,12},{11,13},... | collective-permute-start | bytes 3932168 | tf_op jit(solution)/shard_map/ppermute | solution.py:366
  243.3 19.4 %collective-permute-done.33.refs_9_.refs_12_ = f32[2,24,64,128]{3,2,1,0:T(8,128)S(1)} collective-permute-done((f32[2,24,64,128]{3,2,1,0:T(8,128)S(1)}, f32[2,24,64,128]{3,2,1,0:T(8,128)S(1)}, u32[]{:S(2)}, u32[]{:S(2)}) %collective-permute-start.33) | collective-permute-done | bytes 1572896 | tf_op jit(solution)/shard_map/ppermute | solution.py:367
  263.4 5.8 %collective-permute-done.35.refs_8_.refs_11_ = f32[2,24,64,128]{3,2,1,0:T(8,128)S(1)} collective-permute-done((f32[2,24,64,128]{3,2,1,0:T(8,128)S(1)}, f32[2,24,64,128]{3,2,1,0:T(8,128)S(1)}, u32[]{:S(2)}, u32[]{:S(2)}) %collective-permute-start.35) | collective-permute-done | bytes 1572896 | tf_op jit(solution)/shard_map/ppermute | solution.py:366
  270.5 20.3 %collective-permute-done.17.refs_21_ = f32[40,64,128]{2,1,0:T(8,128)} collective-permute-done((f32[40,64,128]{2,1,0:T(8,128)S(1)}, f32[40,64,128]{2,1,0:T(8,128)}, u32[]{:S(2)}, u32[]{:S(2)}) %collective-permute-start.17) | collective-permute-done | bytes 1310752 | tf_op jit(solution)/shard_map/ppermute | solution.py:367
  294.0 3.3 collective-permute-done.20.refs_19_
  299.4 18.7 %collective-permute-done.15.refs_16_ = f32[40,64,128]{2,1,0:T(8,128)S(1)} collective-permute-done((f32[40,64,128]{2,1,0:T(8,128)S(1)}, f32[40,64,128]{2,1,0:T(8,128)S(1)}, u32[]{:S(2)}, u32[]{:S(2)}) %collective-permute-start.15) | collective-permute-done | bytes 1310752 | tf_op jit(solution)/shard_map/ppermute | solution.py:367
  319.3 4.7 %collective-permute-done.21.refs_22_ = f32[40,64,128]{2,1,0:T(8,128)S(1)} collective-permute-done((f32[40,64,128]{2,1,0:T(8,128)S(1)}, f32[40,64,128]{2,1,0:T(8,128)S(1)}, u32[]{:S(2)}, u32[]{:S(2)}) %collective-permute-start.21) | collective-permute-done | bytes 1310752 | tf_op jit(solution)/shard_map/ppermute | solution.py:366
  324.1 5.6 %collective-permute-start.22 = (f32[40,64,128]{2,1,0:T(8,128)}, f32[40,64,128]{2,1,0:T(8,128)}, u32[]{:S(2)}, u32[]{:S(2)}) collective-permute-start(f32[40,64,128]{2,1,0:T(8,128)} %collective-permute-done.20.refs_19_), channel_id=1, source_target_pairs={{0,2},{1,3},{2,4},{3,5},{4,6},{5,7},{8,10},{9,11},{10,12},{11,13},... | collective-permute-start | bytes 3932168 | tf_op jit(solution)/shard_map/ppermute | solution.py:366
  335.9 14.5 %collective-permute-done.18.refs_17_ = f32[40,64,128]{2,1,0:T(8,128)} collective-permute-done((f32[40,64,128]{2,1,0:T(8,128)}, f32[40,64,128]{2,1,0:T(8,128)}, u32[]{:S(2)}, u32[]{:S(2)}) %collective-permute-start.18) | collective-permute-done | bytes 1310752 | tf_op jit(solution)/shard_map/ppermute | solution.py:367
  351.1 4.7 %collective-permute-done.22.refs_23_ = f32[40,64,128]{2,1,0:T(8,128)} collective-permute-done((f32[40,64,128]{2,1,0:T(8,128)}, f32[40,64,128]{2,1,0:T(8,128)}, u32[]{:S(2)}, u32[]{:S(2)}) %collective-permute-start.22) | collective-permute-done | bytes 1310752 | tf_op jit(solution)/shard_map/ppermute | solution.py:366
  357.3 7.3 %collective-permute-done.3.refs_5_ = f32[40,128,128]{2,1,0:T(8,128)} collective-permute-done((f32[40,128,128]{2,1,0:T(8,128)}, f32[40,128,128]{2,1,0:T(8,128)}, u32[]{:S(2)}, u32[]{:S(2)}) %collective-permute-start.3) | collective-permute-done | bytes 2621472 | tf_op jit(solution)/shard_map/ppermute | solution.py:372
  365.9 5.7 %collective-permute-start.36 = (f32[2,24,64,128]{3,2,1,0:T(8,128)}, f32[2,24,64,128]{3,2,1,0:T(8,128)}, u32[]{:S(2)}, u32[]{:S(2)}) collective-permute-start(f32[2,24,64,128]{3,2,1,0:T(8,128)} %copy-done.7), channel_id=1, source_target_pairs={{0,2},{1,3},{2,4},{3,5},{4,6},{5,7},{8,10},{9,11},{10,12},{11,13},... | collective-permute-start | bytes 4718600 | tf_op jit(solution)/shard_map/ppermute | solution.py:366
  371.7 25.8 %shard_map.100 = (f32[128,40,128]{2,1,0:T(8,128)}, f32[128,40,128]{2,1,0:T(8,128)}) custom-call(s32[33]{0:T(128)} %concatenate.9.slot_ref, f32[40,32,128]{2,1,0:T(8,128)} %forward.5.refs_0_, f32[40,96,128]{2,1,0:T(8,128)} %forward.6.refs_1_, f32[40,128,128]{2,1,0:T(8,128)} %collective-permute-done.refs_2_, f32[40,32,128]{2,1,0:T(8,128)} %copy-done.21, ...), custom_call_target="tpu_custom_call" | custom-call | flops 8053063680 | bytes 39321600 | tf_op jit(solution)/shard_map/pallas_call | solution.py:247
  403.0 11.7 %shard_map.101.refs_15_ = f32[24,256,128]{2,1,0:T(8,128)} custom-call(s32[18]{0:T(128)} %concatenate.11.slot_ref, f32[24,128,128]{2,1,0:T(8,128)} %get-tuple-element.18.refs_0_, f32[24,128,128]{2,1,0:T(8,128)} %copy-done.2, f32[24,128,128]{2,1,0:T(8,128)} %collective-permute-done.24.refs_2_, f32[24,128,128]{2,1,0:T(8,128)} %collective-permute-done.25.refs_3_, ...), custom_call_target="tpu_custom_call" | custom-call | flops 3623878656 | bytes 17301504 | tf_op jit(solution)/shard_map/pallas_call | solution.py:247
  414.7 15.0 %collective-permute-done.26.refs_4_ = f32[24,128,128]{2,1,0:T(8,128)} collective-permute-done((f32[24,128,128]{2,1,0:T(8,128)}, f32[24,128,128]{2,1,0:T(8,128)}, u32[]{:S(2)}, u32[]{:S(2)}) %collective-permute-start.26) | collective-permute-done | bytes 1572896 | tf_op jit(solution)/shard_map/ppermute | solution.py:377
  429.7 16.8 %shard_map.102 = (f32[128,24,128]{2,1,0:T(8,128)}, f32[128,24,128]{2,1,0:T(8,128)}) custom-call(s32[23]{0:T(128)} %concatenate.10.slot_ref, f32[24,128,128]{2,1,0:T(8,128)} %get-tuple-element.18.refs_0_, f32[24,128,128]{2,1,0:T(8,128)} %copy-done.2, f32[24,128,128]{2,1,0:T(8,128)} %collective-permute-done.24.refs_2_, ...), custom_call_target="tpu_custom_call" | custom-call | flops 2415919104 | bytes 26738688 | tf_op jit(solution)/shard_map/pallas_call | solution.py:247
  446.6 3.6 collective-permute-done.38.refs_3_
  451.3 9.7 %inverse.1 = f32[128,128,128]{2,1,0:T(8,128)} custom-call(s32[1]{0:T(128)} %bitcast.core_ref, bf16[2,256,256]{2,1,0:T(8,128)(2,1)} %constant.88.clone.w_ref, f32[128,40,128]{2,1,0:T(8,128)} %get-tuple-element.17.refs_0_, f32[128,24,128]{2,1,0:T(8,128)} %get-tuple-element.22.refs_1_, f32[128,40,128]{2,1,0:T(8,128)} %collective-permute-done.37.refs_2_, ...), custom_call_target="tpu_custom_call" | custom-call | flops 3221225472 | bytes 16777216 | tf_op jit(solution)/shard_map/inverse/pallas_call | solution.py:288
  (118 shorter events, 52.4 us)
Async XLA Ops:
  18.4 33.3 %collective-permute-start.13 = (f32[40,64,128]{2,1,0:T(8,128)}, f32[40,64,128]{2,1,0:T(8,128)}, u32[]{:S(2)}, u32[]{:S(2)}) collective-permute-start(f32[40,64,128]{2,1,0:T(8,128)} %forward.8.refs_12_), channel_id=1, source_target_pairs={{2,0},{3,1},{4,2},{5,3},{6,4},{7,5},{10,8},{11,9},{12,10},{13,11},... | collective-permute-start | bytes 3932168 | tf_op jit(solution)/shard_map/ppermute | solution.py:367
  19.7 33.7 %collective-permute-start.11 = (f32[40,64,128]{2,1,0:T(8,128)}, f32[40,64,128]{2,1,0:T(8,128)}, u32[]{:S(2)}, u32[]{:S(2)}) collective-permute-start(f32[40,64,128]{2,1,0:T(8,128)} %forward.8.refs_12_), channel_id=1, source_target_pairs={{0,2},{1,3},{2,4},{3,5},{4,6},{5,7},{8,10},{9,11},{10,12},{11,13},... | collective-permute-start | bytes 3932168 | tf_op jit(solution)/shard_map/ppermute | solution.py:366
  36.8 93.4 %collective-permute-start.23 = (f32[24,128,128]{2,1,0:T(8,128)}, f32[24,128,128]{2,1,0:T(8,128)S(1)}, u32[]{:S(2)}, u32[]{:S(2)}) collective-permute-start(f32[24,128,128]{2,1,0:T(8,128)} %get-tuple-element.19), channel_id=1, source_target_pairs={{0,1},{1,0},{2,3},{3,2},{4,5},{5,4},{6,7},{7,6},{8,9},{9,8},{10,11... | collective-permute-start | bytes 4718600 | tf_op jit(solution)/shard_map/ppermute | solution.py:359
  37.0 96.6 %collective-permute-start.24 = (f32[24,128,128]{2,1,0:T(8,128)}, f32[24,128,128]{2,1,0:T(8,128)}, u32[]{:S(2)}, u32[]{:S(2)}) collective-permute-start(f32[24,128,128]{2,1,0:T(8,128)} %get-tuple-element.18.refs_0_), channel_id=1, source_target_pairs={{0,8},{8,24},{24,16},{16,0},{1,9},{9,25},{25,17},{17,1},{2,10},{10... | collective-permute-start | bytes 4718600 | tf_op jit(solution)/shard_map/ppermute | solution.py:372
  39.0 95.9 %collective-permute-start.29 = (f32[24,128,128]{2,1,0:T(8,128)}, f32[24,128,128]{2,1,0:T(8,128)}, u32[]{:S(2)}, u32[]{:S(2)}) collective-permute-start(f32[24,128,128]{2,1,0:T(8,128)} %get-tuple-element.18.refs_0_), channel_id=1, source_target_pairs={{8,0},{24,8},{16,24},{0,16},{9,1},{25,9},{17,25},{1,17},{10,2},{26... | collective-permute-start | bytes 4718600 | tf_op jit(solution)/shard_map/ppermute | solution.py:373
  51.7 87.8 %collective-permute-start.2 = (f32[40,96,128]{2,1,0:T(8,128)}, f32[40,96,128]{2,1,0:T(8,128)S(1)}, u32[]{:S(2)}, u32[]{:S(2)}) collective-permute-start(f32[40,96,128]{2,1,0:T(8,128)} %forward.6.refs_1_), channel_id=1, source_target_pairs={{0,8},{8,24},{24,16},{16,0},{1,9},{9,25},{25,17},{17,1},{2,10},{10... | collective-permute-start | bytes 5898248 | tf_op jit(solution)/shard_map/ppermute | solution.py:372
  53.4 76.8 %collective-permute-start.4 = (f32[40,32,128]{2,1,0:T(8,128)S(1)}, f32[40,32,128]{2,1,0:T(8,128)S(1)}, u32[]{:S(2)}, u32[]{:S(2)}) collective-permute-start(f32[40,32,128]{2,1,0:T(8,128)S(1)} %collective-permute-done.1.refs_3_), channel_id=1, source_target_pairs={{0,8},{8,24},{24,16},{16,0},{1,9},{9,25},{25,17},{17,1},{2,10},{10... | collective-permute-start | bytes 1966088 | tf_op jit(solution)/shard_map/ppermute | solution.py:377
  130.2 73.8 %collective-permute-start = (f32[40,128,128]{2,1,0:T(8,128)}, f32[40,128,128]{2,1,0:T(8,128)}, u32[]{:S(2)}, u32[]{:S(2)}) collective-permute-start(f32[40,128,128]{2,1,0:T(8,128)} %get-tuple-element.15), channel_id=1, source_target_pairs={{0,1},{1,0},{2,3},{3,2},{4,5},{5,4},{6,7},{7,6},{8,9},{9,8},{10,11... | collective-permute-start | bytes 7864328 | tf_op jit(solution)/shard_map/ppermute | solution.py:359
  130.2 45.4 %collective-permute-start.9 = (f32[40,96,128]{2,1,0:T(8,128)}, f32[40,96,128]{2,1,0:T(8,128)S(1)}, u32[]{:S(2)}, u32[]{:S(2)}) collective-permute-start(f32[40,96,128]{2,1,0:T(8,128)} %forward.6.refs_1_), channel_id=1, source_target_pairs={{8,0},{24,8},{16,24},{0,16},{9,1},{25,9},{17,25},{1,17},{10,2},{26... | collective-permute-start | bytes 5898248 | tf_op jit(solution)/shard_map/ppermute | solution.py:373
  133.6 44.8 %collective-permute-start.32 = (f32[2,24,64,128]{3,2,1,0:T(8,128)S(1)}, f32[2,24,64,128]{3,2,1,0:T(8,128)S(1)}, u32[]{:S(2)}, u32[]{:S(2)}) collective-permute-start(f32[2,24,64,128]{3,2,1,0:T(8,128)S(1)} %pad_maximum_fusion.refs_6_.refs_8_), channel_id=1, source_target_pairs={{2,0},{3,1},{4,2},{5,3},{6,4},{7,5},{10,8},{11,9},{12,10},{13,11},... | collective-permute-start | bytes 4718600 | tf_op jit(solution)/shard_map/ppermute | solution.py:367
  134.9 44.8 %collective-permute-start.31 = (f32[2,24,64,128]{3,2,1,0:T(8,128)S(1)}, f32[2,24,64,128]{3,2,1,0:T(8,128)S(1)}, u32[]{:S(2)}, u32[]{:S(2)}) collective-permute-start(f32[2,24,64,128]{3,2,1,0:T(8,128)S(1)} %pad_maximum_fusion.refs_6_.refs_8_), channel_id=1, source_target_pairs={{0,2},{1,3},{2,4},{3,5},{4,6},{5,7},{8,10},{9,11},{10,12},{11,13},... | collective-permute-start | bytes 4718600 | tf_op jit(solution)/shard_map/ppermute | solution.py:366
  139.6 61.3 %collective-permute-start.16 = (f32[40,64,128]{2,1,0:T(8,128)S(1)}, f32[40,64,128]{2,1,0:T(8,128)S(1)}, u32[]{:S(2)}, u32[]{:S(2)}) collective-permute-start(f32[40,64,128]{2,1,0:T(8,128)S(1)} %copy-done.14), channel_id=1, source_target_pairs={{2,0},{3,1},{4,2},{5,3},{6,4},{7,5},{10,8},{11,9},{12,10},{13,11},... | collective-permute-start | bytes 3932168 | tf_op jit(solution)/shard_map/ppermute | solution.py:367
  178.4 50.5 %collective-permute-start.14 = (f32[40,64,128]{2,1,0:T(8,128)}, f32[40,64,128]{2,1,0:T(8,128)S(1)}, u32[]{:S(2)}, u32[]{:S(2)}) collective-permute-start(f32[40,64,128]{2,1,0:T(8,128)} %collective-permute-done.13.refs_24_), channel_id=1, source_target_pairs={{2,0},{3,1},{4,2},{5,3},{6,4},{7,5},{10,8},{11,9},{12,10},{13,11},... | collective-permute-start | bytes 3932168 | tf_op jit(solution)/shard_map/ppermute | solution.py:367
  179.7 57.2 %collective-permute-start.27 = (f32[24,128,128]{2,1,0:T(8,128)S(1)}, f32[24,128,128]{2,1,0:T(8,128)S(1)}, u32[]{:S(2)}, u32[]{:S(2)}) collective-permute-start(f32[24,128,128]{2,1,0:T(8,128)S(1)} %collective-permute-done.23.refs_1_), channel_id=1, source_target_pairs={{8,0},{24,8},{16,24},{0,16},{9,1},{25,9},{17,25},{1,17},{10,2},{26... | collective-permute-start | bytes 4718600 | tf_op jit(solution)/shard_map/ppermute | solution.py:373
  200.9 34.8 %collective-permute-start.19 = (f32[40,64,128]{2,1,0:T(8,128)}, f32[40,64,128]{2,1,0:T(8,128)S(1)}, u32[]{:S(2)}, u32[]{:S(2)}) collective-permute-start(f32[40,64,128]{2,1,0:T(8,128)} %collective-permute-done.11.refs_14_), channel_id=1, source_target_pairs={{0,2},{1,3},{2,4},{3,5},{4,6},{5,7},{8,10},{9,11},{10,12},{11,13},... | collective-permute-start | bytes 3932168 | tf_op jit(solution)/shard_map/ppermute | solution.py:366
  204.0 94.8 %collective-permute-start.6 = (f32[40,128,128]{2,1,0:T(8,128)}, f32[40,128,128]{2,1,0:T(8,128)}, u32[]{:S(2)}, u32[]{:S(2)}) collective-permute-start(f32[40,128,128]{2,1,0:T(8,128)} %collective-permute-done.refs_2_), channel_id=1, source_target_pairs={{8,0},{24,8},{16,24},{0,16},{9,1},{25,9},{17,25},{1,17},{10,2},{26... | collective-permute-start | bytes 7864328 | tf_op jit(solution)/shard_map/ppermute | solution.py:373
  207.5 55.2 %collective-permute-start.33 = (f32[2,24,64,128]{3,2,1,0:T(8,128)S(1)}, f32[2,24,64,128]{3,2,1,0:T(8,128)S(1)}, u32[]{:S(2)}, u32[]{:S(2)}) collective-permute-start(f32[2,24,64,128]{3,2,1,0:T(8,128)S(1)} %collective-permute-done.32.refs_10_.refs_14_), channel_id=1, source_target_pairs={{2,0},{3,1},{4,2},{5,3},{6,4},{7,5},{10,8},{11,9},{12,10},{13,11},... | collective-permute-start | bytes 4718600 | tf_op jit(solution)/shard_map/ppermute | solution.py:367
  229.0 40.3 %collective-permute-start.35 = (f32[2,24,64,128]{3,2,1,0:T(8,128)S(1)}, f32[2,24,64,128]{3,2,1,0:T(8,128)S(1)}, u32[]{:S(2)}, u32[]{:S(2)}) collective-permute-start(f32[2,24,64,128]{3,2,1,0:T(8,128)S(1)} %collective-permute-done.31.refs_7_.refs_9_), channel_id=1, source_target_pairs={{0,2},{1,3},{2,4},{3,5},{4,6},{5,7},{8,10},{9,11},{10,12},{11,13},... | collective-permute-start | bytes 4718600 | tf_op jit(solution)/shard_map/ppermute | solution.py:366
  235.6 55.2 %collective-permute-start.17 = (f32[40,64,128]{2,1,0:T(8,128)S(1)}, f32[40,64,128]{2,1,0:T(8,128)}, u32[]{:S(2)}, u32[]{:S(2)}) collective-permute-start(f32[40,64,128]{2,1,0:T(8,128)S(1)} %collective-permute-done.16.refs_25_), channel_id=1, source_target_pairs={{2,0},{3,1},{4,2},{5,3},{6,4},{7,5},{10,8},{11,9},{12,10},{13,11},... | collective-permute-start | bytes 3932168 | tf_op jit(solution)/shard_map/ppermute | solution.py:367
  237.0 60.4 %collective-permute-start.20 = (f32[40,64,128]{2,1,0:T(8,128)S(1)}, f32[40,64,128]{2,1,0:T(8,128)}, u32[]{:S(2)}, u32[]{:S(2)}) collective-permute-start(f32[40,64,128]{2,1,0:T(8,128)S(1)} %collective-permute-done.12.refs_15_), channel_id=1, source_target_pairs={{0,2},{1,3},{2,4},{3,5},{4,6},{5,7},{8,10},{9,11},{10,12},{11,13},... | collective-permute-start | bytes 3932168 | tf_op jit(solution)/shard_map/ppermute | solution.py:366
  262.7 67.0 %collective-permute-start.5 = (f32[40,96,128]{2,1,0:T(8,128)S(1)}, f32[40,96,128]{2,1,0:T(8,128)S(1)}, u32[]{:S(2)}, u32[]{:S(2)}) collective-permute-start(f32[40,96,128]{2,1,0:T(8,128)S(1)} %collective-permute-done.2.refs_4_), channel_id=1, source_target_pairs={{0,8},{8,24},{24,16},{16,0},{1,9},{9,25},{25,17},{17,1},{2,10},{10... | collective-permute-start | bytes 5898248 | tf_op jit(solution)/shard_map/ppermute | solution.py:377
  269.2 48.8 %collective-permute-start.15 = (f32[40,64,128]{2,1,0:T(8,128)S(1)}, f32[40,64,128]{2,1,0:T(8,128)S(1)}, u32[]{:S(2)}, u32[]{:S(2)}) collective-permute-start(f32[40,64,128]{2,1,0:T(8,128)S(1)} %collective-permute-done.14.refs_20_), channel_id=1, source_target_pairs={{2,0},{3,1},{4,2},{5,3},{6,4},{7,5},{10,8},{11,9},{12,10},{13,11},... | collective-permute-start | bytes 3932168 | tf_op jit(solution)/shard_map/ppermute | solution.py:367
  290.8 33.2 %collective-permute-start.21 = (f32[40,64,128]{2,1,0:T(8,128)S(1)}, f32[40,64,128]{2,1,0:T(8,128)S(1)}, u32[]{:S(2)}, u32[]{:S(2)}) collective-permute-start(f32[40,64,128]{2,1,0:T(8,128)S(1)} %collective-permute-done.19.refs_18_), channel_id=1, source_target_pairs={{0,2},{1,3},{2,4},{3,5},{4,6},{5,7},{8,10},{9,11},{10,12},{11,13},... | collective-permute-start | bytes 3932168 | tf_op jit(solution)/shard_map/ppermute | solution.py:366
  297.3 67.3 %collective-permute-start.3 = (f32[40,128,128]{2,1,0:T(8,128)}, f32[40,128,128]{2,1,0:T(8,128)}, u32[]{:S(2)}, u32[]{:S(2)}) collective-permute-start(f32[40,128,128]{2,1,0:T(8,128)} %collective-permute-done.refs_2_), channel_id=1, source_target_pairs={{0,8},{8,24},{24,16},{16,0},{1,9},{9,25},{25,17},{17,1},{2,10},{10... | collective-permute-start | bytes 7864328 | tf_op jit(solution)/shard_map/ppermute | solution.py:372
  298.8 67.1 %collective-permute-start.7 = (f32[40,128,128]{2,1,0:T(8,128)}, f32[40,128,128]{2,1,0:T(8,128)}, u32[]{:S(2)}, u32[]{:S(2)}) collective-permute-start(f32[40,128,128]{2,1,0:T(8,128)} %collective-permute-done.6.refs_11_), channel_id=1, source_target_pairs={{8,0},{24,8},{16,24},{0,16},{9,1},{25,9},{17,25},{1,17},{10,2},{26... | collective-permute-start | bytes 7864328 | tf_op jit(solution)/shard_map/ppermute | solution.py:378
  318.0 32.3 %collective-permute-start.18 = (f32[40,64,128]{2,1,0:T(8,128)}, f32[40,64,128]{2,1,0:T(8,128)}, u32[]{:S(2)}, u32[]{:S(2)}) collective-permute-start(f32[40,64,128]{2,1,0:T(8,128)} %collective-permute-done.17.refs_21_), channel_id=1, source_target_pairs={{2,0},{3,1},{4,2},{5,3},{6,4},{7,5},{10,8},{11,9},{12,10},{13,11},... | collective-permute-start | bytes 3932168 | tf_op jit(solution)/shard_map/ppermute | solution.py:367
  331.1 67.3 %collective-permute-start.25 = (f32[24,128,128]{2,1,0:T(8,128)S(1)}, f32[24,128,128]{2,1,0:T(8,128)}, u32[]{:S(2)}, u32[]{:S(2)}) collective-permute-start(f32[24,128,128]{2,1,0:T(8,128)S(1)} %collective-permute-done.23.refs_1_), channel_id=1, source_target_pairs={{0,8},{8,24},{24,16},{16,0},{1,9},{9,25},{25,17},{17,1},{2,10},{10... | collective-permute-start | bytes 4718600 | tf_op jit(solution)/shard_map/ppermute | solution.py:372
  350.3 79.4 %collective-permute-start.26 = (f32[24,128,128]{2,1,0:T(8,128)}, f32[24,128,128]{2,1,0:T(8,128)}, u32[]{:S(2)}, u32[]{:S(2)}) collective-permute-start(f32[24,128,128]{2,1,0:T(8,128)} %collective-permute-done.24.refs_2_), channel_id=1, source_target_pairs={{0,8},{8,24},{24,16},{16,0},{1,9},{9,25},{25,17},{17,1},{2,10},{10... | collective-permute-start | bytes 4718600 | tf_op jit(solution)/shard_map/ppermute | solution.py:377
  355.8 73.9 %collective-permute-start.28 = (f32[24,128,128]{2,1,0:T(8,128)}, f32[24,128,128]{2,1,0:T(8,128)}, u32[]{:S(2)}, u32[]{:S(2)}) collective-permute-start(f32[24,128,128]{2,1,0:T(8,128)} %copy-done.5), channel_id=1, source_target_pairs={{8,0},{24,8},{16,24},{0,16},{9,1},{25,9},{17,25},{1,17},{10,2},{26... | collective-permute-start | bytes 4718600 | tf_op jit(solution)/shard_map/ppermute | solution.py:378
  364.6 65.1 %collective-permute-start.34 = (f32[2,24,64,128]{3,2,1,0:T(8,128)}, f32[2,24,64,128]{3,2,1,0:T(8,128)}, u32[]{:S(2)}, u32[]{:S(2)}) collective-permute-start(f32[2,24,64,128]{3,2,1,0:T(8,128)} %copy-done.6), channel_id=1, source_target_pairs={{2,0},{3,1},{4,2},{5,3},{6,4},{7,5},{10,8},{11,9},{12,10},{13,11},... | collective-permute-start | bytes 4718600 | tf_op jit(solution)/shard_map/ppermute | solution.py:367
  365.9 63.8 %collective-permute-start.36 = (f32[2,24,64,128]{3,2,1,0:T(8,128)}, f32[2,24,64,128]{3,2,1,0:T(8,128)}, u32[]{:S(2)}, u32[]{:S(2)}) collective-permute-start(f32[2,24,64,128]{3,2,1,0:T(8,128)} %copy-done.7), channel_id=1, source_target_pairs={{0,2},{1,3},{2,4},{3,5},{4,6},{5,7},{8,10},{9,11},{10,12},{11,13},... | collective-permute-start | bytes 4718600 | tf_op jit(solution)/shard_map/ppermute | solution.py:366
  398.3 51.8 %collective-permute-start.37 = (f32[128,40,128]{2,1,0:T(8,128)}, f32[128,40,128]{2,1,0:T(8,128)}, u32[]{:S(2)}, u32[]{:S(2)}) collective-permute-start(f32[128,40,128]{2,1,0:T(8,128)} %get-tuple-element.23), channel_id=1, source_target_pairs={{0,1},{1,0},{2,3},{3,2},{4,5},{5,4},{6,7},{7,6},{8,9},{9,8},{10,11... | collective-permute-start | bytes 7864328 | tf_op jit(solution)/shard_map/ppermute | solution.py:384
  (31 other events, 2201.2 us)

commit v3 on v2

--- a/solution.py
+++ b/solution.py
@@ -12,7 +12,9 @@
 
 NT = 128
 NF = 64
+SPLIT = (1,)
 SHARES = (20, 12)
+GRANT = 53 << 20
 F32, BF16 = jnp.float32, jnp.bfloat16
 
 
@@ -121,7 +123,7 @@
     rows = lhs.shape[1] // 4
     half, cols = next(iter(g_refs.values())).shape[1:]
     core, chosen, far = (slot_ref[levels + i] for i in range(3))
-    step, steps = pl.program_id(0), pl.num_programs(0)
+    step, each = pl.program_id(0), 4 // count
 
     def put_g(b, slot, h, half_of, g):
         high, low = split(g)
@@ -131,30 +133,35 @@
         for i, value in enumerate((high, high, low)):
             rhs[b % 2, pl.ds(at + i * depth, half), to] = value
 
-    def put_d(b, place, a):
-        for at, ref in d_refs[a]:
+    def put_d(b, place, which):
+        for i, (at, ref) in enumerate(d_refs[which[0]]):
             for half_of in range(2):
-                high, low = split(ref[2 * b + half_of])
+                value = ref[2 * b + half_of]
+                for a in which[1:]:
+                    value = jnp.where(chosen == a, d_refs[a][i][1][2 * b + half_of], value)
+                high, low = split(value)
                 first = 2 * rows * half_of + at
-                for i, value in enumerate((high, low, high)):
-                    to = slice((3 * place + i) * depth, (3 * place + i + 1) * depth)
-                    lhs[b % 2, first : first + ref.shape[1], to] = value
+                for j, piece in enumerate((high, low, high)):
+                    to = slice((3 * place + j) * depth, (3 * place + j + 1) * depth)
+                    lhs[b % 2, first : first + ref.shape[1], to] = piece
 
     for b in range(count):
         for h in range(2):
             for half_of in range(2):
                 row = 2 * b + half_of
-                for s, pair in enumerate(sides(part, levels)):
-                    put_g(b, slot_ref[s], h, half_of, sum(g_refs[way, hop, h][row] for way, hop in pair))
+                blocks = [sum(g_refs[way, hop, h][row] for way, hop in pair) for pair in sides(part, levels)]
                 if part == LATE:
+                    met = blocks[0]
+                    for s in range(1, levels):
+                        met = jnp.where(slot_ref[s] == 0, blocks[s], met)
                     last = g_refs["up", levels - 1, h][row] + g_refs["down", levels - 1, h][row]
+                    put_g(b, 0, h, half_of, met)
                     put_g(b, 1, h, half_of, jnp.where(far > 0, last, 0.0))
+                else:
+                    for s, block in enumerate(blocks):
+                        put_g(b, slot_ref[s], h, half_of, block)
         for place, which in enumerate(places):
-            if len(which) == 1:
-                put_d(b, place, which[0])
-            else:
-                for a in which:
-                    pl.when(chosen == a)(functools.partial(put_d, b, place, a))
+            put_d(b, place, which)
         deep = 3 * depth * len(places)
         p = jnp.dot(lhs[b % 2, :, :deep], rhs[b % 2, :deep, :], preferred_element_type=F32)
         real = p[: 2 * rows, :cols] - p[2 * rows :, cols:]
@@ -165,12 +172,12 @@
         if part == LATE:
             real, imaginary = real + rest[0][2 * b], imaginary + rest[0][2 * b + 1]
         held = rest[-3]
-        row = 2 * (step * count + b)
+        row = 2 * (step % each * count + b)
         held[row], held[row + 1] = real, imaginary
 
     if part != EARLY:
 
-        @pl.when(step == steps - 1)
+        @pl.when(step % each == each - 1)
         def _():
             out_a, out_b, held = rest[-5:-2]
             for c in range(held.shape[0]):
@@ -178,53 +185,57 @@
                 out_b[:, c, :] = held[c, rows:]
 
 
-def product(part, me, d, g, so_far=None):
+def numbers(part, me, d, g):
     slot, core, z = me
     levels = slot.shape[0]
     around = len(d)
     diag = around // 2
-    depth = d[0][0].shape[2]
-    n = d[0][0].shape[0]
-    rows = sum(x.shape[1] for x in d[0]) // 2
-    _, cols = g["own", 0][0].shape[-2:]
-    step = 4
-
-    far_s = jnp.where(z == 0, 1, levels - 1)
-    far_a = slot[far_s]
+    far_a = slot[jnp.where(z == 0, 1, levels - 1)]
     far = ((z == 0) | (z == levels - 1)) & (far_a != diag)
     chosen = jnp.where(far, far_a, 0)
     others = [a for a in range(around) if a != diag]
     if part == ALL:
         places, to = [[a] for a in range(around)], slot
     elif part == EARLY:
-        index = np.array([others.index(a) if a in others else len(others) for a in range(around)])
-        places, to = [[a] for a in others], jnp.asarray(index)[slot]
+        places, to = [[a] for a in others], jnp.where(slot == diag, len(others), slot - (slot > diag))
     else:
         places, to = [[diag], others], jnp.where(slot == diag, 0, 2)
-    scalars = [to, jnp.stack([core, chosen, far.astype(jnp.int32)])]
-
-    operands, d_keys, g_keys, needed = [], [], [], []
+    needed = []
+    for a in sorted(set(sum(places, []))):
+        needed += [chosen == a if part == LATE and a != diag else True] * d[a]
+    for s, pair in enumerate(sides(part, levels)):
+        for way, hop in pair:
+            there = {"own": True, "up": z >= hop, "down": z + hop < levels}[way]
+            if part == LATE:
+                there = there & ((slot[s] == diag) | (hop == levels - 1))
+            needed += [there] * g
+    needed.append(True)
+    scalars = [core, chosen, far] + needed
+    scalars = [to.astype(jnp.int32), jnp.stack([jnp.asarray(x).astype(jnp.int32) for x in scalars])]
+    return places, jnp.concatenate(scalars)
+
+
+def product(part, places, scalars, d, g, so_far=None):
+    levels = 1 + max(hop for _, hop in g)
+    depth = d[0][0].shape[2]
+    n = d[0][0].shape[0]
+    rows = sum(x.shape[1] for x in d[0]) // 2
+    _, cols = g["own", 0][0].shape[-2:]
+    step = 4
+    operands, d_keys, g_keys = [], [], []
     for a in sorted(set(sum(places, []))):
         at = 0
         for x in d[a]:
             d_keys.append((a, at))
             operands.append(x)
-            needed.append(jnp.where(chosen == a, 1, 0) if part == LATE and a != diag else 1)
             at += x.shape[1]
-    for s, pair in enumerate(sides(part, levels)):
+    for pair in sides(part, levels):
         for way, hop in pair:
-            there = {"own": True, "up": z >= hop, "down": z + hop < levels}[way]
-            if part == LATE:
-                there = there & ((slot[s] == diag) | (hop == levels - 1))
             for h, x in enumerate(g[way, hop]):
                 g_keys.append((way, hop, h if len(g[way, hop]) == 2 else None))
                 operands.append(x)
-                needed.append(jnp.where(there, 1, 0))
     if so_far is not None:
         operands.append(so_far)
-        needed.append(1)
-    scalars.append(jnp.stack([jnp.asarray(x, jnp.int32) for x in needed]))
-    scalars = jnp.concatenate([x.astype(jnp.int32) for x in scalars])
     first = levels + 3
 
     def spec(i, x):
@@ -242,8 +253,8 @@
         out_specs = pl.BlockSpec((step, 2 * rows, cols), lambda i, c: (i, 0, 0))
     else:
         out = [jax.ShapeDtypeStruct((rows, n, cols), F32)] * 2
-        out_specs = [pl.BlockSpec((rows, n, cols), lambda i, c: (0, 0, 0))] * 2
-        scratch = [pltpu.VMEM((n, 2 * rows, cols), F32)] + scratch
+        out_specs = [pl.BlockSpec((rows, 8, cols), lambda i, c: (0, i * step // 8, 0))] * 2
+        scratch = [pltpu.VMEM((8, 2 * rows, cols), F32)] + scratch
     return pl.pallas_call(
         functools.partial(product_kernel, part, levels, places, d_keys, g_keys),
         grid_spec=pltpu.PrefetchScalarGridSpec(
@@ -254,6 +265,7 @@
             scratch_shapes=scratch,
         ),
         out_shape=out,
+        compiler_params=pltpu.CompilerParams(vmem_limit_bytes=GRANT if part == LATE else None),
         cost_estimate=pl.CostEstimate(
             flops=n // 2 * 2 * 4 * rows * 3 * len(places) * depth * 2 * cols,
             bytes_accessed=4 * sum(x.size for x in operands),
@@ -262,8 +274,8 @@
     )(scalars, *operands)
 
 
-def inverse_kernel(core_ref, w_ref, *refs):
-    x_refs, out = refs[:-1], refs[-1]
+def inverse_kernel(count, core_ref, w_ref, *refs):
+    x_refs, out = refs[:count], refs[-1]
     group = 8
 
     def some(q, carry):
@@ -272,34 +284,38 @@
             high, low = split(jnp.concatenate([x[i] for x in x_refs], axis=0))
             x = jnp.concatenate([high, low], axis=0)
             both = lax.dot_general(x, w_ref[0], (((0,), (0,)), ((), ())), preferred_element_type=F32)
-            out[i] = both[:, :NT] + both[:, NT:]
+            res = both[:, :NT] + both[:, NT:]
+            out[i] = res if len(refs) == count + 1 else res + refs[count][i]
         return carry
 
     lax.fori_loop(0, out.shape[0] // group, some, 0)
 
 
-def inverse(ms, core):
+def inverse(ms, core, cuts, so_far=None):
     rows, _, cols = ms[0].shape
-    high, low = parts(by_core(tables()[1]))
+    table = by_core(tables()[1])
+    high, low = parts(np.concatenate([table[:, a:b] for a, b in cuts], axis=1))
+    operands = list(ms) + ([] if so_far is None else [so_far])
     w = np.concatenate(
         [np.concatenate([high, low], axis=2), np.concatenate([high, np.zeros_like(low)], axis=2)], axis=1
     )
     step = 32
     return pl.pallas_call(
-        inverse_kernel,
+        functools.partial(inverse_kernel, len(ms)),
         grid_spec=pltpu.PrefetchScalarGridSpec(
             num_scalar_prefetch=1,
             grid=(rows // step,),
             in_specs=[pl.BlockSpec((1,) + w.shape[1:], lambda i, c: (c[0], 0, 0))]
-            + [pl.BlockSpec((step,) + x.shape[1:], lambda i, c: (i, 0, 0)) for x in ms],
+            + [pl.BlockSpec((step,) + x.shape[1:], lambda i, c: (i, 0, 0)) for x in operands],
             out_specs=pl.BlockSpec((step, cols, NT), lambda i, c: (i, 0, 0)),
         ),
         out_shape=jax.ShapeDtypeStruct((rows, cols, NT), F32),
+        compiler_params=pltpu.CompilerParams(vmem_limit_bytes=GRANT),
         cost_estimate=pl.CostEstimate(
             flops=12 * rows * cols * NT * NT, bytes_accessed=8 * rows * cols * NT, transcendentals=0
         ),
         name="inverse",
-    )(core, jnp.asarray(w), *ms)
+    )(core, jnp.asarray(w), *operands)
 
 
 def plain(recorded, panels):
@@ -358,11 +374,17 @@
         g_own = [g_parts[c], lax.ppermute(g_parts[chunks + c], "src", partner)]
         d_swapped = lax.ppermute(d_parts[chunks + c], "src", partner)
         d_own = [d_parts[c], d_swapped] if c else head + [d_parts[c], d_swapped]
+        calls = (EARLY, LATE) if c in SPLIT else (ALL,)
+        counts = {a: len(d_own) for a in range(around)}
+        plans = [numbers(part, me, counts, 1 if c else 2) for part in calls]
         if c:
             g_own = [jnp.stack(g_own)]
         g = {("own", 0): g_own}
         up, down = g_own, g_own
         for s in range(1, levels):
+            if s == 2:
+                made, up[0] = lax.optimization_barrier(([x[1] for x in plans], up[0]))
+                plans = [(x[0], y) for x, y in zip(plans, made)]
             up = [lax.ppermute(x, "src", upward) for x in up]
             down = [lax.ppermute(x, "src", downward) for x in down]
             g["up", s], g["down", s] = up, down
@@ -376,13 +398,12 @@
         mine = len(d_own) - 1
         d[last] = [lax.ppermute(x, "freq", clockwise) for x in right[:mine]]
         d[last].append(lax.ppermute(left[mine], "freq", counter))
-        if c < chunks - 1:
-            m = product(ALL, me, d, g)
-        else:
-            m = product(EARLY, me, d, g)
-            m = product(LATE, me, d, g, m)
+        m = None
+        for part, (places, scalars) in zip(calls, plans):
+            m = product(part, places, scalars, d, g, m)
         ms.append([m[0], lax.ppermute(m[1], "src", partner)])
-    return inverse([m[0] for m in ms] + [m[1] for m in ms], core_at)
+    acc = inverse(ms[0], core_at, [cuts[0], cuts[chunks]])
+    return inverse(ms[1], core_at, [cuts[1], cuts[chunks + 1]], acc)
 
 
 def solution(mesh):

time: 462 us -> 410 us (0.89)
  waiting for transfers between devices: 279 us -> 225 us
    ppermute x3, waiting for transfers between devices: 90.3 us -> 5.33 us  [local(): d[last] = [lax.ppermute(x, 'freq', clockwise) for x in right[:mine]]]
    ppermute x5, waiting for transfers between devices: 8.21 us -> 50.9 us  [local(): right = [lax.ppermute(x, 'freq', clockwise) for x in right]]
    ppermute x9, waiting for transfers between devices: 118 us -> 99.2 us  [local(): down = [lax.ppermute(x, 'src', downward) for x in down]]
    pallas_call x1 -> x2, Pallas kernels: 9.68 us -> 19.5 us  [inverse(): pl.pallas_call(functools.partial(inverse_kernel, len(ms)), grid_spec=pltp...]
    ppermute x5, waiting for transfers between devices: 34.7 us -> 42.5 us  [local(): left = [lax.ppermute(x, 'freq', counter) for x in left]]
    pallas_call x3, Pallas kernels: 54.3 us -> 49.2 us  [product(): pl.pallas_call(functools.partial(product_kernel, part, levels, places, d_...]
  transfers between devices with their start and end apart: 39 -> 39, of which waited for: 19 -> 16; matrix products, arithmetic and copies ran while one was open for 1% -> 1% of each run, Pallas kernels for 18% -> 21%
where the time goes in v3:
time: 410 us; the launch traced here: 409 us
  waiting for transfers between devices  225 us (55%)
  Pallas kernels  101 us (25%)
  starting transfers between devices  70.4 us (17%)
  local copies, waits for them, and re-layouts  6.04 us (1%)
    ppermute x9, waiting for transfers between devices, local(): down = [lax.ppermute(x, 'src', downward) for x in down]  99.2 us
    ppermute x5, waiting for transfers between devices, local(): right = [lax.ppermute(x, 'freq', clockwise) for x in right]  50.9 us
    pallas_call x3, Pallas kernels, product(): pl.pallas_call(functools.partial(product_kernel, part, levels, places, d_...  49.2 us
    ppermute x5, waiting for transfers between devices, local(): left = [lax.ppermute(x, 'freq', counter) for x in left]  42.5 us
    ppermute x9, starting transfers between devices, local(): up = [lax.ppermute(x, 'src', upward) for x in up]  41.7 us
    pallas_call x5, Pallas kernels, forward(): pl.pallas_call(functools.partial(forward_kernel, counts), grid_spec=pltpu...  32.7 us
    ppermute x9, waiting for transfers between devices, local(): up = [lax.ppermute(x, 'src', upward) for x in up]  27.1 us
    pallas_call x2, Pallas kernels, inverse(): pl.pallas_call(functools.partial(inverse_kernel, len(ms)), grid_spec=pltp...  19.5 us
  transfers between devices with their start and end apart: 39, of which 16 were waited for; matrix products, arithmetic and copies ran while one was open for 1% of the time, Pallas kernels for 21%

profile of v3, /device:TPU:0, one launch (start us, length us, event | category | flops | bytes accessed | tf_op | source)
XLA Modules:
  0.0 408.7 jit_solution(17587531958070955289)
XLA Ops:
  0.0 6.5 %forward.5 = (f32[24,64,128]{2,1,0:T(8,128)}, f32[40,64,128]{2,1,0:T(8,128)}, f32[24,64,128]{2,1,0:T(8,128)}) custom-call(s32[1]{0:T(128)} %bitcast.core_ref, bf16[2,176,256]{2,1,0:T(8,128)(2,1)} %constant.82.clone.w_ref, f32[64,128,128]{2,1,0:T(8,128)} %x_ref.7), custom_call_target="tpu_custom_call" | custom-call | flops 1610612736 | bytes 8388608 | tf_op jit(solution)/shard_map/forward/pallas_call | solution.py:84
  7.0 3.3 forward.8.refs_0_
  12.8 5.5 %forward.7.refs_12_ = f32[40,64,128]{2,1,0:T(8,128)} custom-call(s32[1]{0:T(128)} %bitcast.core_ref, bf16[2,80,256]{2,1,0:T(8,128)(2,1)} %constant.81.clone.w_ref, f32[64,128,128]{2,1,0:T(8,128)} %x_ref.7), custom_call_target="tpu_custom_call" | custom-call | flops 1610612736 | bytes 8388608 | tf_op jit(solution)/shard_map/forward/pallas_call | solution.py:84
  18.3 4.5 %collective-permute-start.15 = (f32[40,64,128]{2,1,0:T(8,128)}, f32[40,64,128]{2,1,0:T(8,128)}, u32[]{:S(2)}, u32[]{:S(2)}) collective-permute-start(f32[40,64,128]{2,1,0:T(8,128)} %forward.7.refs_12_), channel_id=1, source_target_pairs={{0,2},{1,3},{2,4},{3,5},{4,6},{5,7},{8,10},{9,11},{10,12},{11,13},... | collective-permute-start | bytes 3932168 | tf_op jit(solution)/shard_map/ppermute | solution.py:388
  23.4 10.4 %forward.6 = (f32[24,128,128]{2,1,0:T(8,128)}, f32[40,128,128]{2,1,0:T(8,128)}, f32[24,128,128]{2,1,0:T(8,128)}) custom-call(s32[1]{0:T(128)} %bitcast.core_ref, bf16[2,176,256]{2,1,0:T(8,128)(2,1)} %constant.82.clone.w_ref, f32[128,128,128]{2,1,0:T(8,128)} %x_ref.9), custom_call_target="tpu_custom_call" | custom-call | flops 3221225472 | bytes 16777216 | tf_op jit(solution)/shard_map/forward/pallas_call | solution.py:84
  34.3 5.2 %collective-permute-done.24.refs_9_ = f32[40,32,128]{2,1,0:T(8,128)S(1)} collective-permute-done((f32[40,32,128]{2,1,0:T(8,128)S(1)}, f32[40,32,128]{2,1,0:T(8,128)S(1)}, u32[]{:S(2)}, u32[]{:S(2)}) %collective-permute-start.24) | collective-permute-done | bytes 655392 | tf_op jit(solution)/shard_map/ppermute | solution.py:395
  42.2 8.3 %collective-permute-done.15.refs_14_ = f32[40,64,128]{2,1,0:T(8,128)} collective-permute-done((f32[40,64,128]{2,1,0:T(8,128)}, f32[40,64,128]{2,1,0:T(8,128)}, u32[]{:S(2)}, u32[]{:S(2)}) %collective-permute-start.15) | collective-permute-done | bytes 1310752 | tf_op jit(solution)/shard_map/ppermute | solution.py:388
  52.0 5.3 %collective-permute-done.20.refs_6_ = f32[40,32,128]{2,1,0:T(8,128)} collective-permute-done((f32[40,32,128]{2,1,0:T(8,128)}, f32[40,32,128]{2,1,0:T(8,128)}, u32[]{:S(2)}, u32[]{:S(2)}) %collective-permute-start.20) | collective-permute-done | bytes 655392 | tf_op jit(solution)/shard_map/ppermute | solution.py:399
  57.9 7.0 %forward.9.refs_1_ = f32[40,96,128]{2,1,0:T(8,128)} custom-call(s32[1]{0:T(128)} %bitcast.core_ref, bf16[2,80,256]{2,1,0:T(8,128)(2,1)} %constant.81.clone.w_ref, f32[128,128,128]{2,1,0:T(8,128)} %x_ref.9), custom_call_target="tpu_custom_call" | custom-call | flops 2415919104 | bytes 12582912 | tf_op jit(solution)/shard_map/forward/pallas_call | solution.py:84
  66.4 6.1 %collective-permute-done.28.refs_24_ = f32[40,64,128]{2,1,0:T(8,128)S(1)} collective-permute-done((f32[40,64,128]{2,1,0:T(8,128)}, f32[40,64,128]{2,1,0:T(8,128)S(1)}, u32[]{:S(2)}, u32[]{:S(2)}) %collective-permute-start.28) | collective-permute-done | bytes 1310752 | tf_op jit(solution)/shard_map/ppermute | solution.py:389
  75.2 15.8 %collective-permute-done.3.refs_2_ = f32[24,128,128]{2,1,0:T(8,128)} collective-permute-done((f32[24,128,128]{2,1,0:T(8,128)}, f32[24,128,128]{2,1,0:T(8,128)}, u32[]{:S(2)}, u32[]{:S(2)}) %collective-permute-start.3) | collective-permute-done | bytes 1572896 | tf_op jit(solution)/shard_map/ppermute | solution.py:394
  91.0 2.8 collective-permute-start.1
  96.2 35.1 %collective-permute-done.18.refs_4_ = f32[40,96,128]{2,1,0:T(8,128)} collective-permute-done((f32[40,96,128]{2,1,0:T(8,128)}, f32[40,96,128]{2,1,0:T(8,128)}, u32[]{:S(2)}, u32[]{:S(2)}) %collective-permute-start.18) | collective-permute-done | bytes 1966112 | tf_op jit(solution)/shard_map/ppermute | solution.py:394
  131.3 3.6 collective-permute-start.27
  140.7 6.3 %collective-permute-start.34 = (f32[40,64,128]{2,1,0:T(8,128)}, f32[40,64,128]{2,1,0:T(8,128)}, u32[]{:S(2)}, u32[]{:S(2)}) collective-permute-start(f32[40,64,128]{2,1,0:T(8,128)} %collective-permute-done.15.refs_14_), channel_id=1, source_target_pairs={{0,2},{1,3},{2,4},{3,5},{4,6},{5,7},{8,10},{9,11},{10,12},{11,13},... | collective-permute-start | bytes 3932168 | tf_op jit(solution)/shard_map/ppermute | solution.py:388
  147.5 15.8 %collective-permute-done.27.refs_15_ = f32[40,64,128]{2,1,0:T(8,128)} collective-permute-done((f32[40,64,128]{2,1,0:T(8,128)}, f32[40,64,128]{2,1,0:T(8,128)}, u32[]{:S(2)}, u32[]{:S(2)}) %collective-permute-start.27) | collective-permute-done | bytes 1310752 | tf_op jit(solution)/shard_map/ppermute | solution.py:388
  163.9 4.9 %collective-permute-done.29.refs_20_ = f32[40,64,128]{2,1,0:T(8,128)} collective-permute-done((f32[40,64,128]{2,1,0:T(8,128)}, f32[40,64,128]{2,1,0:T(8,128)}, u32[]{:S(2)}, u32[]{:S(2)}) %collective-permute-start.29) | collective-permute-done | bytes 1310752 | tf_op jit(solution)/shard_map/ppermute | solution.py:389
  173.6 21.2 %collective-permute-done.31.refs_25_ = f32[40,64,128]{2,1,0:T(8,128)} collective-permute-done((f32[40,64,128]{2,1,0:T(8,128)}, f32[40,64,128]{2,1,0:T(8,128)}, u32[]{:S(2)}, u32[]{:S(2)}) %collective-permute-start.31) | collective-permute-done | bytes 1310752 | tf_op jit(solution)/shard_map/ppermute | solution.py:389
  196.2 5.7 %collective-permute-start.12 = (f32[2,24,64,128]{3,2,1,0:T(8,128)}, f32[2,24,64,128]{3,2,1,0:T(8,128)}, u32[]{:S(2)}, u32[]{:S(2)}) collective-permute-start(f32[2,24,64,128]{3,2,1,0:T(8,128)} %collective-permute-done.1.refs_7_.refs_9_), channel_id=1, source_target_pairs={{0,2},{1,3},{2,4},{3,5},{4,6},{5,7},{8,10},{9,11},{10,12},{11,13},... | collective-permute-start | bytes 4718600 | tf_op jit(solution)/shard_map/ppermute | solution.py:388
  201.9 36.3 %collective-permute-done.6.refs_5_.refs_7_ = f32[24,128,128]{2,1,0:T(8,128)} collective-permute-done((f32[24,128,128]{2,1,0:T(8,128)S(1)}, f32[24,128,128]{2,1,0:T(8,128)}, u32[]{:S(2)}, u32[]{:S(2)}) %collective-permute-start.6) | collective-permute-done | bytes 1572896 | tf_op jit(solution)/shard_map/ppermute | solution.py:395
  242.3 5.3 %collective-permute-start.35 = (f32[40,64,128]{2,1,0:T(8,128)}, f32[40,64,128]{2,1,0:T(8,128)S(1)}, u32[]{:S(2)}, u32[]{:S(2)}) collective-permute-start(f32[40,64,128]{2,1,0:T(8,128)} %collective-permute-done.27.refs_15_), channel_id=1, source_target_pairs={{0,2},{1,3},{2,4},{3,5},{4,6},{5,7},{8,10},{9,11},{10,12},{11,13},... | collective-permute-start | bytes 3932168 | tf_op jit(solution)/shard_map/ppermute | solution.py:388
  248.2 23.7 %collective-permute-done.30.refs_16_ = f32[40,64,128]{2,1,0:T(8,128)S(1)} collective-permute-done((f32[40,64,128]{2,1,0:T(8,128)}, f32[40,64,128]{2,1,0:T(8,128)S(1)}, u32[]{:S(2)}, u32[]{:S(2)}) %collective-permute-start.30) | collective-permute-done | bytes 1310752 | tf_op jit(solution)/shard_map/ppermute | solution.py:389
  271.9 2.7 collective-permute-start.36
  274.6 22.0 %collective-permute-done.32.refs_21_ = f32[40,64,128]{2,1,0:T(8,128)S(1)} collective-permute-done((f32[40,64,128]{2,1,0:T(8,128)}, f32[40,64,128]{2,1,0:T(8,128)S(1)}, u32[]{:S(2)}, u32[]{:S(2)}) %collective-permute-start.32) | collective-permute-done | bytes 1310752 | tf_op jit(solution)/shard_map/ppermute | solution.py:389
  297.9 4.6 %collective-permute-start.37 = (f32[40,64,128]{2,1,0:T(8,128)S(1)}, f32[40,64,128]{2,1,0:T(8,128)S(1)}, u32[]{:S(2)}, u32[]{:S(2)}) collective-permute-start(f32[40,64,128]{2,1,0:T(8,128)S(1)} %collective-permute-done.35.refs_19_), channel_id=1, source_target_pairs={{0,2},{1,3},{2,4},{3,5},{4,6},{5,7},{8,10},{9,11},{10,12},{11,13},... | collective-permute-start | bytes 3932168 | tf_op jit(solution)/shard_map/ppermute | solution.py:388
  304.7 21.2 %collective-permute-done.33.refs_17_ = f32[40,64,128]{2,1,0:T(8,128)S(1)} collective-permute-done((f32[40,64,128]{2,1,0:T(8,128)S(1)}, f32[40,64,128]{2,1,0:T(8,128)S(1)}, u32[]{:S(2)}, u32[]{:S(2)}) %collective-permute-start.33) | collective-permute-done | bytes 1310752 | tf_op jit(solution)/shard_map/ppermute | solution.py:389
  330.4 6.2 %collective-permute-start.13 = (f32[2,24,64,128]{3,2,1,0:T(8,128)}, f32[2,24,64,128]{3,2,1,0:T(8,128)}, u32[]{:S(2)}, u32[]{:S(2)}) collective-permute-start(f32[2,24,64,128]{3,2,1,0:T(8,128)} %collective-permute-done.12.refs_8_.refs_11_), channel_id=1, source_target_pairs={{0,2},{1,3},{2,4},{3,5},{4,6},{5,7},{8,10},{9,11},{10,12},{11,13},... | collective-permute-start | bytes 4718600 | tf_op jit(solution)/shard_map/ppermute | solution.py:388
  336.5 24.3 %shard_map.102 = (f32[128,40,128]{2,1,0:T(8,128)}, f32[128,40,128]{2,1,0:T(8,128)}) custom-call(s32[34]{0:T(128)} %concatenate.11.slot_ref, f32[40,32,128]{2,1,0:T(8,128)} %forward.8.refs_0_, f32[40,96,128]{2,1,0:T(8,128)} %forward.9.refs_1_, f32[40,128,128]{2,1,0:T(8,128)} %collective-permute-done.16.refs_2_, ...), custom_call_target="tpu_custom_call" | custom-call | flops 8053063680 | bytes 39321600 | tf_op jit(solution)/shard_map/pallas_call | solution.py:258
  361.0 11.6 %shard_map.100.refs_15_ = f32[24,256,128]{2,1,0:T(8,128)} custom-call(s32[19]{0:T(128)} %concatenate.9.slot_ref, f32[24,128,128]{2,1,0:T(8,128)} %get-tuple-element.23.refs_0_, f32[24,128,128]{2,1,0:T(8,128)} %copy-done.4, f32[24,128,128]{2,1,0:T(8,128)} %collective-permute-done.3.refs_2_, f32[24,128,128]{2,1,0:T(8,128)} %collective-permute-done.4.refs_3_, ...), custom_call_target="tpu_custom_call" | custom-call | flops 3623878656 | bytes 17301504 | tf_op jit(solution)/shard_map/pallas_call | solution.py:258
  372.7 13.2 %shard_map.101 = (f32[128,24,128]{2,1,0:T(8,128)}, f32[128,24,128]{2,1,0:T(8,128)}) custom-call(s32[23]{0:T(128)S(1)} %concatenate.10.slot_ref, f32[24,128,128]{2,1,0:T(8,128)} %get-tuple-element.23.refs_0_, f32[24,128,128]{2,1,0:T(8,128)} %copy-done.4, f32[24,128,128]{2,1,0:T(8,128)} %collective-permute-done.3.refs_2_, ...), custom_call_target="tpu_custom_call" | custom-call | flops 2415919104 | bytes 26738688 | tf_op jit(solution)/shard_map/pallas_call | solution.py:258
  388.0 9.1 %inverse.2.refs_2_ = f32[128,128,128]{2,1,0:T(8,128)} custom-call(s32[1]{0:T(128)} %bitcast.core_ref, bf16[2,160,256]{2,1,0:T(8,128)(2,1)S(1)} %copy-done, f32[128,40,128]{2,1,0:T(8,128)} %get-tuple-element.33.refs_0_, f32[128,40,128]{2,1,0:T(8,128)} %copy-done.5), custom_call_target="tpu_custom_call" | custom-call | flops 3221225472 | bytes 16777216 | tf_op jit(solution)/shard_map/inverse/pallas_call | solution.py:303
  398.2 10.4 %inverse.3 = f32[128,128,128]{2,1,0:T(8,128)} custom-call(s32[1]{0:T(128)} %bitcast.core_ref, bf16[2,96,256]{2,1,0:T(8,128)(2,1)S(1)} %copy-done.1, f32[128,24,128]{2,1,0:T(8,128)} %get-tuple-element.27.refs_0_, f32[128,24,128]{2,1,0:T(8,128)} %copy-done.7, f32[128,128,128]{2,1,0:T(8,128)} %inverse.2.refs_2_), custom_call_target="tpu_custom_call" | custom-call | flops 3221225472 | bytes 16777216 | tf_op jit(solution)/shard_map/inverse/pallas_call | solution.py:303
  (101 shorter events, 40.6 us)
Async XLA Ops:
  6.5 34.4 %collective-permute-start = (f32[24,64,128]{2,1,0:T(8,128)}, f32[24,64,128]{2,1,0:T(8,128)}, u32[]{:S(2)}, u32[]{:S(2)}) collective-permute-start(f32[24,64,128]{2,1,0:T(8,128)} %get-tuple-element.21), channel_id=1, source_target_pairs={{0,1},{1,0},{2,3},{3,2},{4,5},{5,4},{6,7},{7,6},{8,9},{9,8},{10,11... | collective-permute-start | bytes 2359304 | tf_op jit(solution)/shard_map/ppermute | solution.py:374
  18.3 32.2 %collective-permute-start.15 = (f32[40,64,128]{2,1,0:T(8,128)}, f32[40,64,128]{2,1,0:T(8,128)}, u32[]{:S(2)}, u32[]{:S(2)}) collective-permute-start(f32[40,64,128]{2,1,0:T(8,128)} %forward.7.refs_12_), channel_id=1, source_target_pairs={{0,2},{1,3},{2,4},{3,5},{4,6},{5,7},{8,10},{9,11},{10,12},{11,13},... | collective-permute-start | bytes 3932168 | tf_op jit(solution)/shard_map/ppermute | solution.py:388
  23.4 41.5 %collective-permute-start.26 = (f32[40,64,128]{2,1,0:T(8,128)}, f32[40,64,128]{2,1,0:T(8,128)}, u32[]{:S(2)}, u32[]{:S(2)}) collective-permute-start(f32[40,64,128]{2,1,0:T(8,128)} %get-tuple-element.31), channel_id=1, source_target_pairs={{0,1},{1,0},{2,3},{3,2},{4,5},{5,4},{6,7},{7,6},{8,9},{9,8},{10,11... | collective-permute-start | bytes 3932168 | tf_op jit(solution)/shard_map/ppermute | solution.py:374
  33.8 39.3 %collective-permute-start.2 = (f32[24,128,128]{2,1,0:T(8,128)}, f32[24,128,128]{2,1,0:T(8,128)S(1)}, u32[]{:S(2)}, u32[]{:S(2)}) collective-permute-start(f32[24,128,128]{2,1,0:T(8,128)} %get-tuple-element.24), channel_id=1, source_target_pairs={{0,1},{1,0},{2,3},{3,2},{4,5},{5,4},{6,7},{7,6},{8,9},{9,8},{10,11... | collective-permute-start | bytes 4718600 | tf_op jit(solution)/shard_map/ppermute | solution.py:375
  40.9 31.6 %collective-permute-start.28 = (f32[40,64,128]{2,1,0:T(8,128)}, f32[40,64,128]{2,1,0:T(8,128)S(1)}, u32[]{:S(2)}, u32[]{:S(2)}) collective-permute-start(f32[40,64,128]{2,1,0:T(8,128)} %forward.7.refs_12_), channel_id=1, source_target_pairs={{2,0},{3,1},{4,2},{5,3},{6,4},{7,5},{10,8},{11,9},{12,10},{13,11},... | collective-permute-start | bytes 3932168 | tf_op jit(solution)/shard_map/ppermute | solution.py:389
  50.5 40.6 %collective-permute-start.3 = (f32[24,128,128]{2,1,0:T(8,128)}, f32[24,128,128]{2,1,0:T(8,128)}, u32[]{:S(2)}, u32[]{:S(2)}) collective-permute-start(f32[24,128,128]{2,1,0:T(8,128)} %get-tuple-element.23.refs_0_), channel_id=1, source_target_pairs={{0,8},{8,24},{24,16},{16,0},{1,9},{9,25},{25,17},{17,1},{2,10},{10... | collective-permute-start | bytes 4718600 | tf_op jit(solution)/shard_map/ppermute | solution.py:394
  57.3 37.6 %collective-permute-start.8 = (f32[24,128,128]{2,1,0:T(8,128)}, f32[24,128,128]{2,1,0:T(8,128)}, u32[]{:S(2)}, u32[]{:S(2)}) collective-permute-start(f32[24,128,128]{2,1,0:T(8,128)} %get-tuple-element.23.refs_0_), channel_id=1, source_target_pairs={{8,0},{24,8},{16,24},{0,16},{9,1},{25,9},{17,25},{1,17},{10,2},{26... | collective-permute-start | bytes 4718600 | tf_op jit(solution)/shard_map/ppermute | solution.py:395
  64.9 66.4 %collective-permute-start.18 = (f32[40,96,128]{2,1,0:T(8,128)}, f32[40,96,128]{2,1,0:T(8,128)}, u32[]{:S(2)}, u32[]{:S(2)}) collective-permute-start(f32[40,96,128]{2,1,0:T(8,128)} %forward.9.refs_1_), channel_id=1, source_target_pairs={{0,8},{8,24},{24,16},{16,0},{1,9},{9,25},{25,17},{17,1},{2,10},{10... | collective-permute-start | bytes 5898248 | tf_op jit(solution)/shard_map/ppermute | solution.py:394
  72.5 62.4 %collective-permute-start.25 = (f32[40,96,128]{2,1,0:T(8,128)}, f32[40,96,128]{2,1,0:T(8,128)}, u32[]{:S(2)}, u32[]{:S(2)}) collective-permute-start(f32[40,96,128]{2,1,0:T(8,128)} %forward.9.refs_1_), channel_id=1, source_target_pairs={{8,0},{24,8},{16,24},{0,16},{9,1},{25,9},{17,25},{1,17},{10,2},{26... | collective-permute-start | bytes 5898248 | tf_op jit(solution)/shard_map/ppermute | solution.py:395
  73.0 74.0 %collective-permute-start.16 = (f32[40,128,128]{2,1,0:T(8,128)}, f32[40,128,128]{2,1,0:T(8,128)}, u32[]{:S(2)}, u32[]{:S(2)}) collective-permute-start(f32[40,128,128]{2,1,0:T(8,128)} %get-tuple-element.30), channel_id=1, source_target_pairs={{0,1},{1,0},{2,3},{3,2},{4,5},{5,4},{6,7},{7,6},{8,9},{9,8},{10,11... | collective-permute-start | bytes 7864328 | tf_op jit(solution)/shard_map/ppermute | solution.py:375
  91.0 48.4 %collective-permute-start.1 = (f32[2,24,64,128]{3,2,1,0:T(8,128)S(1)}, f32[2,24,64,128]{3,2,1,0:T(8,128)}, u32[]{:S(2)}, u32[]{:S(2)}) collective-permute-start(f32[2,24,64,128]{3,2,1,0:T(8,128)S(1)} %pad_maximum_fusion.refs_6_.refs_8_), channel_id=1, source_target_pairs={{0,2},{1,3},{2,4},{3,5},{4,6},{5,7},{8,10},{9,11},{10,12},{11,13},... | collective-permute-start | bytes 4718600 | tf_op jit(solution)/shard_map/ppermute | solution.py:388
  94.9 45.8 %collective-permute-start.9 = (f32[2,24,64,128]{3,2,1,0:T(8,128)S(1)}, f32[2,24,64,128]{3,2,1,0:T(8,128)}, u32[]{:S(2)}, u32[]{:S(2)}) collective-permute-start(f32[2,24,64,128]{3,2,1,0:T(8,128)S(1)} %pad_maximum_fusion.refs_6_.refs_8_), channel_id=1, source_target_pairs={{2,0},{3,1},{4,2},{5,3},{6,4},{7,5},{10,8},{11,9},{12,10},{13,11},... | collective-permute-start | bytes 4718600 | tf_op jit(solution)/shard_map/ppermute | solution.py:389
  131.3 32.0 %collective-permute-start.27 = (f32[40,64,128]{2,1,0:T(8,128)}, f32[40,64,128]{2,1,0:T(8,128)}, u32[]{:S(2)}, u32[]{:S(2)}) collective-permute-start(f32[40,64,128]{2,1,0:T(8,128)} %collective-permute-done.26.refs_13_), channel_id=1, source_target_pairs={{0,2},{1,3},{2,4},{3,5},{4,6},{5,7},{8,10},{9,11},{10,12},{11,13},... | collective-permute-start | bytes 3932168 | tf_op jit(solution)/shard_map/ppermute | solution.py:388
  134.9 33.9 %collective-permute-start.29 = (f32[40,64,128]{2,1,0:T(8,128)}, f32[40,64,128]{2,1,0:T(8,128)}, u32[]{:S(2)}, u32[]{:S(2)}) collective-permute-start(f32[40,64,128]{2,1,0:T(8,128)} %copy-done.8), channel_id=1, source_target_pairs={{2,0},{3,1},{4,2},{5,3},{6,4},{7,5},{10,8},{11,9},{12,10},{13,11},... | collective-permute-start | bytes 3932168 | tf_op jit(solution)/shard_map/ppermute | solution.py:389
  139.4 55.5 %collective-permute-start.31 = (f32[40,64,128]{2,1,0:T(8,128)}, f32[40,64,128]{2,1,0:T(8,128)}, u32[]{:S(2)}, u32[]{:S(2)}) collective-permute-start(f32[40,64,128]{2,1,0:T(8,128)} %collective-permute-done.26.refs_13_), channel_id=1, source_target_pairs={{2,0},{3,1},{4,2},{5,3},{6,4},{7,5},{10,8},{11,9},{12,10},{13,11},... | collective-permute-start | bytes 3932168 | tf_op jit(solution)/shard_map/ppermute | solution.py:389
  140.7 55.5 %collective-permute-start.34 = (f32[40,64,128]{2,1,0:T(8,128)}, f32[40,64,128]{2,1,0:T(8,128)}, u32[]{:S(2)}, u32[]{:S(2)}) collective-permute-start(f32[40,64,128]{2,1,0:T(8,128)} %collective-permute-done.15.refs_14_), channel_id=1, source_target_pairs={{0,2},{1,3},{2,4},{3,5},{4,6},{5,7},{8,10},{9,11},{10,12},{11,13},... | collective-permute-start | bytes 3932168 | tf_op jit(solution)/shard_map/ppermute | solution.py:388
  147.0 100.6 %collective-permute-start.22 = (f32[40,128,128]{2,1,0:T(8,128)}, f32[40,128,128]{2,1,0:T(8,128)}, u32[]{:S(2)}, u32[]{:S(2)}) collective-permute-start(f32[40,128,128]{2,1,0:T(8,128)} %collective-permute-done.16.refs_2_), channel_id=1, source_target_pairs={{8,0},{24,8},{16,24},{0,16},{9,1},{25,9},{17,25},{1,17},{10,2},{26... | collective-permute-start | bytes 7864328 | tf_op jit(solution)/shard_map/ppermute | solution.py:395
  163.3 74.8 %collective-permute-start.6 = (f32[24,128,128]{2,1,0:T(8,128)S(1)}, f32[24,128,128]{2,1,0:T(8,128)}, u32[]{:S(2)}, u32[]{:S(2)}) collective-permute-start(f32[24,128,128]{2,1,0:T(8,128)S(1)} %collective-permute-done.2.refs_1_), channel_id=1, source_target_pairs={{8,0},{24,8},{16,24},{0,16},{9,1},{25,9},{17,25},{1,17},{10,2},{26... | collective-permute-start | bytes 4718600 | tf_op jit(solution)/shard_map/ppermute | solution.py:395
  168.8 73.5 %collective-permute-start.21 = (f32[40,96,128]{2,1,0:T(8,128)}, f32[40,96,128]{2,1,0:T(8,128)}, u32[]{:S(2)}, u32[]{:S(2)}) collective-permute-start(f32[40,96,128]{2,1,0:T(8,128)} %collective-permute-done.18.refs_4_), channel_id=1, source_target_pairs={{0,8},{8,24},{24,16},{16,0},{1,9},{9,25},{25,17},{17,1},{2,10},{10... | collective-permute-start | bytes 5898248 | tf_op jit(solution)/shard_map/ppermute | solution.py:399
  194.9 44.6 %collective-permute-start.10 = (f32[2,24,64,128]{3,2,1,0:T(8,128)}, f32[2,24,64,128]{3,2,1,0:T(8,128)}, u32[]{:S(2)}, u32[]{:S(2)}) collective-permute-start(f32[2,24,64,128]{3,2,1,0:T(8,128)} %collective-permute-done.9.refs_10_.refs_14_), channel_id=1, source_target_pairs={{2,0},{3,1},{4,2},{5,3},{6,4},{7,5},{10,8},{11,9},{12,10},{13,11},... | collective-permute-start | bytes 4718600 | tf_op jit(solution)/shard_map/ppermute | solution.py:389
  196.2 44.9 %collective-permute-start.12 = (f32[2,24,64,128]{3,2,1,0:T(8,128)}, f32[2,24,64,128]{3,2,1,0:T(8,128)}, u32[]{:S(2)}, u32[]{:S(2)}) collective-permute-start(f32[2,24,64,128]{3,2,1,0:T(8,128)} %collective-permute-done.1.refs_7_.refs_9_), channel_id=1, source_target_pairs={{0,2},{1,3},{2,4},{3,5},{4,6},{5,7},{8,10},{9,11},{10,12},{11,13},... | collective-permute-start | bytes 4718600 | tf_op jit(solution)/shard_map/ppermute | solution.py:388
  238.2 33.7 %collective-permute-start.30 = (f32[40,64,128]{2,1,0:T(8,128)}, f32[40,64,128]{2,1,0:T(8,128)S(1)}, u32[]{:S(2)}, u32[]{:S(2)}) collective-permute-start(f32[40,64,128]{2,1,0:T(8,128)} %collective-permute-done.29.refs_20_), channel_id=1, source_target_pairs={{2,0},{3,1},{4,2},{5,3},{6,4},{7,5},{10,8},{11,9},{12,10},{13,11},... | collective-permute-start | bytes 3932168 | tf_op jit(solution)/shard_map/ppermute | solution.py:389
  239.5 64.6 %collective-permute-start.19 = (f32[40,128,128]{2,1,0:T(8,128)}, f32[40,128,128]{2,1,0:T(8,128)}, u32[]{:S(2)}, u32[]{:S(2)}) collective-permute-start(f32[40,128,128]{2,1,0:T(8,128)} %collective-permute-done.16.refs_2_), channel_id=1, source_target_pairs={{0,8},{8,24},{24,16},{16,0},{1,9},{9,25},{25,17},{17,1},{2,10},{10... | collective-permute-start | bytes 7864328 | tf_op jit(solution)/shard_map/ppermute | solution.py:394
  241.0 55.5 %collective-permute-start.32 = (f32[40,64,128]{2,1,0:T(8,128)}, f32[40,64,128]{2,1,0:T(8,128)S(1)}, u32[]{:S(2)}, u32[]{:S(2)}) collective-permute-start(f32[40,64,128]{2,1,0:T(8,128)} %collective-permute-done.31.refs_25_), channel_id=1, source_target_pairs={{2,0},{3,1},{4,2},{5,3},{6,4},{7,5},{10,8},{11,9},{12,10},{13,11},... | collective-permute-start | bytes 3932168 | tf_op jit(solution)/shard_map/ppermute | solution.py:389
  242.3 55.5 %collective-permute-start.35 = (f32[40,64,128]{2,1,0:T(8,128)}, f32[40,64,128]{2,1,0:T(8,128)S(1)}, u32[]{:S(2)}, u32[]{:S(2)}) collective-permute-start(f32[40,64,128]{2,1,0:T(8,128)} %collective-permute-done.27.refs_15_), channel_id=1, source_target_pairs={{0,2},{1,3},{2,4},{3,5},{4,6},{5,7},{8,10},{9,11},{10,12},{11,13},... | collective-permute-start | bytes 3932168 | tf_op jit(solution)/shard_map/ppermute | solution.py:388
  247.6 82.7 %collective-permute-start.23 = (f32[40,128,128]{2,1,0:T(8,128)}, f32[40,128,128]{2,1,0:T(8,128)}, u32[]{:S(2)}, u32[]{:S(2)}) collective-permute-start(f32[40,128,128]{2,1,0:T(8,128)} %collective-permute-done.22.refs_11_), channel_id=1, source_target_pairs={{8,0},{24,8},{16,24},{0,16},{9,1},{25,9},{17,25},{1,17},{10,2},{26... | collective-permute-start | bytes 7864328 | tf_op jit(solution)/shard_map/ppermute | solution.py:400
  297.9 31.2 %collective-permute-start.37 = (f32[40,64,128]{2,1,0:T(8,128)S(1)}, f32[40,64,128]{2,1,0:T(8,128)S(1)}, u32[]{:S(2)}, u32[]{:S(2)}) collective-permute-start(f32[40,64,128]{2,1,0:T(8,128)S(1)} %collective-permute-done.35.refs_19_), channel_id=1, source_target_pairs={{0,2},{1,3},{2,4},{3,5},{4,6},{5,7},{8,10},{9,11},{10,12},{11,13},... | collective-permute-start | bytes 3932168 | tf_op jit(solution)/shard_map/ppermute | solution.py:388
  303.0 57.9 %collective-permute-start.4 = (f32[24,128,128]{2,1,0:T(8,128)S(1)}, f32[24,128,128]{2,1,0:T(8,128)}, u32[]{:S(2)}, u32[]{:S(2)}) collective-permute-start(f32[24,128,128]{2,1,0:T(8,128)S(1)} %collective-permute-done.2.refs_1_), channel_id=1, source_target_pairs={{0,8},{8,24},{24,16},{16,0},{1,9},{9,25},{25,17},{17,1},{2,10},{10... | collective-permute-start | bytes 4718600 | tf_op jit(solution)/shard_map/ppermute | solution.py:394
  304.1 68.5 %collective-permute-start.5 = (f32[24,128,128]{2,1,0:T(8,128)}, f32[24,128,128]{2,1,0:T(8,128)}, u32[]{:S(2)}, u32[]{:S(2)}) collective-permute-start(f32[24,128,128]{2,1,0:T(8,128)} %collective-permute-done.3.refs_2_), channel_id=1, source_target_pairs={{0,8},{8,24},{24,16},{16,0},{1,9},{9,25},{25,17},{17,1},{2,10},{10... | collective-permute-start | bytes 4718600 | tf_op jit(solution)/shard_map/ppermute | solution.py:399
  325.9 46.7 %collective-permute-start.7 = (f32[24,128,128]{2,1,0:T(8,128)}, f32[24,128,128]{2,1,0:T(8,128)}, u32[]{:S(2)}, u32[]{:S(2)}) collective-permute-start(f32[24,128,128]{2,1,0:T(8,128)} %collective-permute-done.6.refs_5_.refs_7_), channel_id=1, source_target_pairs={{8,0},{24,8},{16,24},{0,16},{9,1},{25,9},{17,25},{1,17},{10,2},{26... | collective-permute-start | bytes 4718600 | tf_op jit(solution)/shard_map/ppermute | solution.py:400
  329.1 43.6 %collective-permute-start.11 = (f32[2,24,64,128]{3,2,1,0:T(8,128)}, f32[2,24,64,128]{3,2,1,0:T(8,128)}, u32[]{:S(2)}, u32[]{:S(2)}) collective-permute-start(f32[2,24,64,128]{3,2,1,0:T(8,128)} %collective-permute-done.10.refs_9_.refs_12_), channel_id=1, source_target_pairs={{2,0},{3,1},{4,2},{5,3},{6,4},{7,5},{10,8},{11,9},{12,10},{13,11},... | collective-permute-start | bytes 4718600 | tf_op jit(solution)/shard_map/ppermute | solution.py:389
  330.4 42.3 %collective-permute-start.13 = (f32[2,24,64,128]{3,2,1,0:T(8,128)}, f32[2,24,64,128]{3,2,1,0:T(8,128)}, u32[]{:S(2)}, u32[]{:S(2)}) collective-permute-start(f32[2,24,64,128]{3,2,1,0:T(8,128)} %collective-permute-done.12.refs_8_.refs_11_), channel_id=1, source_target_pairs={{0,2},{1,3},{2,4},{3,5},{4,6},{5,7},{8,10},{9,11},{10,12},{11,13},... | collective-permute-start | bytes 4718600 | tf_op jit(solution)/shard_map/ppermute | solution.py:388
  (23 other events, 876.3 us)

commit v4 on v3

--- a/solution.py
+++ b/solution.py
@@ -12,9 +12,9 @@
 
 NT = 128
 NF = 64
-SPLIT = (1,)
+SPLIT = (0, 1)
 SHARES = (20, 12)
-GRANT = 53 << 20
+GRANT = 50 << 20
 F32, BF16 = jnp.float32, jnp.bfloat16
 
 
@@ -295,7 +295,7 @@
     rows, _, cols = ms[0].shape
     table = by_core(tables()[1])
     high, low = parts(np.concatenate([table[:, a:b] for a, b in cuts], axis=1))
-    operands = list(ms) + ([] if so_far is None else [so_far])
+    operands = list(ms) + ([] if so_far is None else [pltpu.with_memory_space_constraint(so_far, pltpu.VMEM)])
     w = np.concatenate(
         [np.concatenate([high, low], axis=2), np.concatenate([high, np.zeros_like(low)], axis=2)], axis=1
     )
@@ -309,8 +309,8 @@
             + [pl.BlockSpec((step,) + x.shape[1:], lambda i, c: (i, 0, 0)) for x in operands],
             out_specs=pl.BlockSpec((step, cols, NT), lambda i, c: (i, 0, 0)),
         ),
-        out_shape=jax.ShapeDtypeStruct((rows, cols, NT), F32),
-        compiler_params=pltpu.CompilerParams(vmem_limit_bytes=GRANT),
+        out_shape=(pltpu.VMEM if so_far is None else jax.ShapeDtypeStruct)((rows, cols, NT), F32),
+        compiler_params=pltpu.CompilerParams(vmem_limit_bytes=GRANT - (12 << 20)),
         cost_estimate=pl.CostEstimate(
             flops=12 * rows * cols * NT * NT, bytes_accessed=8 * rows * cols * NT, transcendentals=0
         ),

time: 410 us -> 416 us (1.015)
  starting transfers between devices: 70.4 us -> 80.5 us
  waiting for transfers between devices: 225 us -> 216 us
  Pallas kernels: 101 us -> 107 us
    pallas_call x3 -> x4, Pallas kernels: 49.2 us -> 61.3 us  [product(): pl.pallas_call(functools.partial(product_kernel, part, levels, places, d_...]
    pallas_call x2, Pallas kernels: 19.5 us -> 12.6 us  [inverse(): pl.pallas_call(functools.partial(inverse_kernel, len(ms)), grid_spec=pltp...]
    ppermute x3, waiting for transfers between devices: 5.33 us -> 0.01 us  [local(): d[last] = [lax.ppermute(x, 'freq', clockwise) for x in right[:mine]]]
    ppermute x9, starting transfers between devices: 41.7 us -> 46.8 us  [local(): up = [lax.ppermute(x, 'src', upward) for x in up]]
  transfers between devices with their start and end apart: 39 -> 39, of which waited for: 16 -> 12; matrix products, arithmetic and copies ran while one was open for 1% -> 1% of each run, Pallas kernels for 21% -> 23%
where the time goes in v4:
time: 416 us; the launch traced here: 414 us
  waiting for transfers between devices  216 us (52%)
  Pallas kernels  107 us (26%)
  starting transfers between devices  80.5 us (19%)
  local copies, waits for them, and re-layouts  5.87 us (1%)
  between operations  4.31 us (1%)
    ppermute x9, waiting for transfers between devices, local(): down = [lax.ppermute(x, 'src', downward) for x in down]  97.6 us
    pallas_call x4, Pallas kernels, product(): pl.pallas_call(functools.partial(product_kernel, part, levels, places, d_...  61.3 us
    ppermute x5, waiting for transfers between devices, local(): right = [lax.ppermute(x, 'freq', clockwise) for x in right]  52.5 us
    ppermute x9, starting transfers between devices, local(): up = [lax.ppermute(x, 'src', upward) for x in up]  46.8 us
    ppermute x5, waiting for transfers between devices, local(): left = [lax.ppermute(x, 'freq', counter) for x in left]  38.4 us
    pallas_call x5, Pallas kernels, forward(): pl.pallas_call(functools.partial(forward_kernel, counts), grid_spec=pltpu...  32.8 us
    ppermute x9, waiting for transfers between devices, local(): up = [lax.ppermute(x, 'src', upward) for x in up]  27.1 us
    pallas_call x2, Pallas kernels, inverse(): pl.pallas_call(functools.partial(inverse_kernel, len(ms)), grid_spec=pltp...  12.6 us
  transfers between devices with their start and end apart: 39, of which 12 were waited for; matrix products, arithmetic and copies ran while one was open for 1% of the time, Pallas kernels for 23%

profile of v4, /device:TPU:0, one launch (start us, length us, event | category | flops | bytes accessed | tf_op | source)
XLA Modules:
  0.0 414.4 jit_solution(16931065672913771785)
XLA Ops:
  0.0 3.3 forward.8.refs_0_
  3.3 3.0 collective-permute-start.17
  6.3 6.5 %forward.5 = (f32[24,64,128]{2,1,0:T(8,128)}, f32[40,64,128]{2,1,0:T(8,128)}, f32[24,64,128]{2,1,0:T(8,128)}) custom-call(s32[1]{0:T(128)} %bitcast.core_ref, bf16[2,176,256]{2,1,0:T(8,128)(2,1)} %constant.82.clone.w_ref, f32[64,128,128]{2,1,0:T(8,128)} %x_ref.7), custom_call_target="tpu_custom_call" | custom-call | flops 1610612736 | bytes 8388608 | tf_op jit(solution)/shard_map/forward/pallas_call | solution.py:84
  12.8 5.5 %forward.7.refs_9_.refs_12_ = f32[40,64,128]{2,1,0:T(8,128)} custom-call(s32[1]{0:T(128)} %bitcast.core_ref, bf16[2,80,256]{2,1,0:T(8,128)(2,1)} %constant.81.clone.w_ref, f32[64,128,128]{2,1,0:T(8,128)} %x_ref.7), custom_call_target="tpu_custom_call" | custom-call | flops 1610612736 | bytes 8388608 | tf_op jit(solution)/shard_map/forward/pallas_call | solution.py:84
  18.3 5.1 %collective-permute-start.15 = (f32[40,64,128]{2,1,0:T(8,128)}, f32[40,64,128]{2,1,0:T(8,128)}, u32[]{:S(2)}, u32[]{:S(2)}) collective-permute-start(f32[40,64,128]{2,1,0:T(8,128)} %forward.7.refs_9_.refs_12_), channel_id=1, source_target_pairs={{0,2},{1,3},{2,4},{3,5},{4,6},{5,7},{8,10},{9,11},{10,12},{11,13},... | collective-permute-start | bytes 3932168 | tf_op jit(solution)/shard_map/ppermute | solution.py:388
  23.6 10.4 %forward.6 = (f32[24,128,128]{2,1,0:T(8,128)}, f32[40,128,128]{2,1,0:T(8,128)}, f32[24,128,128]{2,1,0:T(8,128)}) custom-call(s32[1]{0:T(128)} %bitcast.core_ref, bf16[2,176,256]{2,1,0:T(8,128)(2,1)} %constant.82.clone.w_ref, f32[128,128,128]{2,1,0:T(8,128)} %x_ref.9), custom_call_target="tpu_custom_call" | custom-call | flops 3221225472 | bytes 16777216 | tf_op jit(solution)/shard_map/forward/pallas_call | solution.py:84
  37.3 14.0 %collective-permute-done.15.refs_11_.refs_14_ = f32[40,64,128]{2,1,0:T(8,128)} collective-permute-done((f32[40,64,128]{2,1,0:T(8,128)}, f32[40,64,128]{2,1,0:T(8,128)}, u32[]{:S(2)}, u32[]{:S(2)}) %collective-permute-start.15) | collective-permute-done | bytes 1310752 | tf_op jit(solution)/shard_map/ppermute | solution.py:388
  55.0 7.0 %forward.9.refs_1_ = f32[40,96,128]{2,1,0:T(8,128)} custom-call(s32[1]{0:T(128)} %bitcast.core_ref, bf16[2,80,256]{2,1,0:T(8,128)(2,1)} %constant.81.clone.w_ref, f32[128,128,128]{2,1,0:T(8,128)} %x_ref.9), custom_call_target="tpu_custom_call" | custom-call | flops 2415919104 | bytes 12582912 | tf_op jit(solution)/shard_map/forward/pallas_call | solution.py:84
  62.7 4.6 %collective-permute-done.28.refs_17_.refs_24_ = f32[40,64,128]{2,1,0:T(8,128)} collective-permute-done((f32[40,64,128]{2,1,0:T(8,128)S(1)}, f32[40,64,128]{2,1,0:T(8,128)}, u32[]{:S(2)}, u32[]{:S(2)}) %collective-permute-start.28) | collective-permute-done | bytes 1310752 | tf_op jit(solution)/shard_map/ppermute | solution.py:389
  70.3 18.5 %collective-permute-done.3.refs_2_ = f32[24,128,128]{2,1,0:T(8,128)} collective-permute-done((f32[24,128,128]{2,1,0:T(8,128)}, f32[24,128,128]{2,1,0:T(8,128)}, u32[]{:S(2)}, u32[]{:S(2)}) %collective-permute-start.3) | collective-permute-done | bytes 1572896 | tf_op jit(solution)/shard_map/ppermute | solution.py:394
  88.8 5.5 %collective-permute-start.1 = (f32[2,24,64,128]{3,2,1,0:T(8,128)S(1)}, f32[2,24,64,128]{3,2,1,0:T(8,128)}, u32[]{:S(2)}, u32[]{:S(2)}) collective-permute-start(f32[2,24,64,128]{3,2,1,0:T(8,128)S(1)} %pad_maximum_fusion.refs_6_.refs_8_), channel_id=1, source_target_pairs={{0,2},{1,3},{2,4},{3,5},{4,6},{5,7},{8,10},{9,11},{10,12},{11,13},... | collective-permute-start | bytes 4718600 | tf_op jit(solution)/shard_map/ppermute | solution.py:388
  95.7 33.9 %collective-permute-done.18.refs_4_ = f32[40,96,128]{2,1,0:T(8,128)} collective-permute-done((f32[40,96,128]{2,1,0:T(8,128)}, f32[40,96,128]{2,1,0:T(8,128)}, u32[]{:S(2)}, u32[]{:S(2)}) %collective-permute-start.18) | collective-permute-done | bytes 1966112 | tf_op jit(solution)/shard_map/ppermute | solution.py:394
  129.6 5.4 %collective-permute-start.27 = (f32[40,64,128]{2,1,0:T(8,128)}, f32[40,64,128]{2,1,0:T(8,128)}, u32[]{:S(2)}, u32[]{:S(2)}) collective-permute-start(f32[40,64,128]{2,1,0:T(8,128)} %collective-permute-done.26.refs_10_.refs_13_), channel_id=1, source_target_pairs={{0,2},{1,3},{2,4},{3,5},{4,6},{5,7},{8,10},{9,11},{10,12},{11,13},... | collective-permute-start | bytes 3932168 | tf_op jit(solution)/shard_map/ppermute | solution.py:388
  143.6 6.3 %collective-permute-start.34 = (f32[40,64,128]{2,1,0:T(8,128)}, f32[40,64,128]{2,1,0:T(8,128)}, u32[]{:S(2)}, u32[]{:S(2)}) collective-permute-start(f32[40,64,128]{2,1,0:T(8,128)} %collective-permute-done.15.refs_11_.refs_14_), channel_id=1, source_target_pairs={{0,2},{1,3},{2,4},{3,5},{4,6},{5,7},{8,10},{9,11},{10,12},{11,13},... | collective-permute-start | bytes 3932168 | tf_op jit(solution)/shard_map/ppermute | solution.py:388
  151.4 12.1 %collective-permute-done.27.refs_12_.refs_15_ = f32[40,64,128]{2,1,0:T(8,128)} collective-permute-done((f32[40,64,128]{2,1,0:T(8,128)}, f32[40,64,128]{2,1,0:T(8,128)}, u32[]{:S(2)}, u32[]{:S(2)}) %collective-permute-start.27) | collective-permute-done | bytes 1310752 | tf_op jit(solution)/shard_map/ppermute | solution.py:388
  165.0 4.6 %collective-permute-done.29.refs_15_.refs_20_ = f32[40,64,128]{2,1,0:T(8,128)} collective-permute-done((f32[40,64,128]{2,1,0:T(8,128)}, f32[40,64,128]{2,1,0:T(8,128)}, u32[]{:S(2)}, u32[]{:S(2)}) %collective-permute-start.29) | collective-permute-done | bytes 1310752 | tf_op jit(solution)/shard_map/ppermute | solution.py:389
  171.9 23.4 %collective-permute-done.31.refs_18_.refs_25_ = f32[40,64,128]{2,1,0:T(8,128)} collective-permute-done((f32[40,64,128]{2,1,0:T(8,128)}, f32[40,64,128]{2,1,0:T(8,128)}, u32[]{:S(2)}, u32[]{:S(2)}) %collective-permute-start.31) | collective-permute-done | bytes 1310752 | tf_op jit(solution)/shard_map/ppermute | solution.py:389
  196.5 5.7 %collective-permute-start.12 = (f32[2,24,64,128]{3,2,1,0:T(8,128)}, f32[2,24,64,128]{3,2,1,0:T(8,128)}, u32[]{:S(2)}, u32[]{:S(2)}) collective-permute-start(f32[2,24,64,128]{3,2,1,0:T(8,128)} %collective-permute-done.1.refs_7_.refs_9_), channel_id=1, source_target_pairs={{0,2},{1,3},{2,4},{3,5},{4,6},{5,7},{8,10},{9,11},{10,12},{11,13},... | collective-permute-start | bytes 4718600 | tf_op jit(solution)/shard_map/ppermute | solution.py:388
  202.2 38.4 %collective-permute-done.6.refs_5_.refs_7_ = f32[24,128,128]{2,1,0:T(8,128)} collective-permute-done((f32[24,128,128]{2,1,0:T(8,128)}, f32[24,128,128]{2,1,0:T(8,128)}, u32[]{:S(2)}, u32[]{:S(2)}) %collective-permute-start.6) | collective-permute-done | bytes 1572896 | tf_op jit(solution)/shard_map/ppermute | solution.py:395
  244.8 5.3 %collective-permute-start.35 = (f32[40,64,128]{2,1,0:T(8,128)}, f32[40,64,128]{2,1,0:T(8,128)S(1)}, u32[]{:S(2)}, u32[]{:S(2)}) collective-permute-start(f32[40,64,128]{2,1,0:T(8,128)} %collective-permute-done.27.refs_12_.refs_15_), channel_id=1, source_target_pairs={{0,2},{1,3},{2,4},{3,5},{4,6},{5,7},{8,10},{9,11},{10,12},{11,13},... | collective-permute-start | bytes 3932168 | tf_op jit(solution)/shard_map/ppermute | solution.py:388
  250.6 23.7 %collective-permute-done.30.refs_16_ = f32[40,64,128]{2,1,0:T(8,128)S(1)} collective-permute-done((f32[40,64,128]{2,1,0:T(8,128)}, f32[40,64,128]{2,1,0:T(8,128)S(1)}, u32[]{:S(2)}, u32[]{:S(2)}) %collective-permute-start.30) | collective-permute-done | bytes 1310752 | tf_op jit(solution)/shard_map/ppermute | solution.py:389
  274.4 2.7 collective-permute-start.36
  277.0 21.5 %collective-permute-done.32.refs_16_.refs_21_ = f32[40,64,128]{2,1,0:T(8,128)S(1)} collective-permute-done((f32[40,64,128]{2,1,0:T(8,128)}, f32[40,64,128]{2,1,0:T(8,128)S(1)}, u32[]{:S(2)}, u32[]{:S(2)}) %collective-permute-start.32) | collective-permute-done | bytes 1310752 | tf_op jit(solution)/shard_map/ppermute | solution.py:389
  301.0 4.6 %collective-permute-start.37 = (f32[40,64,128]{2,1,0:T(8,128)S(1)}, f32[40,64,128]{2,1,0:T(8,128)S(1)}, u32[]{:S(2)}, u32[]{:S(2)}) collective-permute-start(f32[40,64,128]{2,1,0:T(8,128)S(1)} %collective-permute-done.35.refs_14_.refs_19_), channel_id=1, source_target_pairs={{0,2},{1,3},{2,4},{3,5},{4,6},{5,7},{8,10},{9,11},{10,12},{11,13},... | collective-permute-start | bytes 3932168 | tf_op jit(solution)/shard_map/ppermute | solution.py:388
  308.7 19.8 %collective-permute-done.33.refs_17_ = f32[40,64,128]{2,1,0:T(8,128)S(1)} collective-permute-done((f32[40,64,128]{2,1,0:T(8,128)S(1)}, f32[40,64,128]{2,1,0:T(8,128)S(1)}, u32[]{:S(2)}, u32[]{:S(2)}) %collective-permute-start.33) | collective-permute-done | bytes 1310752 | tf_op jit(solution)/shard_map/ppermute | solution.py:389
  332.4 6.2 %collective-permute-start.13 = (f32[2,24,64,128]{3,2,1,0:T(8,128)}, f32[2,24,64,128]{3,2,1,0:T(8,128)}, u32[]{:S(2)}, u32[]{:S(2)}) collective-permute-start(f32[2,24,64,128]{3,2,1,0:T(8,128)} %collective-permute-done.12.refs_8_.refs_11_), channel_id=1, source_target_pairs={{0,2},{1,3},{2,4},{3,5},{4,6},{5,7},{8,10},{9,11},{10,12},{11,13},... | collective-permute-start | bytes 4718600 | tf_op jit(solution)/shard_map/ppermute | solution.py:388
  338.6 17.8 %shard_map.102.refs_26_ = f32[40,256,128]{2,1,0:T(8,128)} custom-call(s32[27]{0:T(128)} %concatenate.14.slot_ref, f32[40,32,128]{2,1,0:T(8,128)} %forward.8.refs_0_, f32[40,96,128]{2,1,0:T(8,128)} %forward.9.refs_1_, f32[40,128,128]{2,1,0:T(8,128)} %collective-permute-done.16.refs_2_, f32[40,32,128]{2,1,0:T(8,128)} %copy-done.4, ...), custom_call_target="tpu_custom_call" | custom-call | flops 6039797760 | bytes 28835840 | tf_op jit(solution)/shard_map/pallas_call | solution.py:258
  357.6 19.6 %shard_map.103 = (f32[128,40,128]{2,1,0:T(8,128)}, f32[128,40,128]{2,1,0:T(8,128)}) custom-call(s32[34]{0:T(128)S(1)} %concatenate.15.slot_ref, f32[40,32,128]{2,1,0:T(8,128)S(1)} %copy-done, f32[40,96,128]{2,1,0:T(8,128)} %forward.9.refs_1_, f32[40,128,128]{2,1,0:T(8,128)} %collective-permute-done.16.refs_2_, f32[40,32,128]{2,1,0:T(8,128)S(1)} %copy-done.5, ...), custom_call_target="tpu_custom_call" | custom-call | flops 4026531840 | bytes 44564480 | tf_op jit(solution)/shard_map/pallas_call | solution.py:258
  377.3 11.6 %shard_map.100.refs_15_ = f32[24,256,128]{2,1,0:T(8,128)} custom-call(s32[19]{0:T(128)} %concatenate.12.slot_ref, f32[24,128,128]{2,1,0:T(8,128)} %get-tuple-element.24.refs_0_, f32[24,128,128]{2,1,0:T(8,128)} %collective-permute-done.2.refs_1_, f32[24,128,128]{2,1,0:T(8,128)} %collective-permute-done.3.refs_2_, ...), custom_call_target="tpu_custom_call" | custom-call | flops 3623878656 | bytes 17301504 | tf_op jit(solution)/shard_map/pallas_call | solution.py:258
  389.0 12.2 %shard_map.101 = (f32[128,24,128]{2,1,0:T(8,128)S(1)}, f32[128,24,128]{2,1,0:T(8,128)S(1)}) custom-call(s32[23]{0:T(128)S(1)} %concatenate.13.slot_ref, f32[24,128,128]{2,1,0:T(8,128)} %get-tuple-element.24.refs_0_, f32[24,128,128]{2,1,0:T(8,128)} %collective-permute-done.2.refs_1_, f32[24,128,128]{2,1,0:T(8,128)} %collective-permute-done.3.refs_2_, ...), custom_call_target="tpu_custom_call" | custom-call | flops 2415919104 | bytes 26738688 | tf_op jit(solution)/shard_map/pallas_call | solution.py:258
  401.8 5.8 %inverse.2.refs_2_ = f32[128,128,128]{2,1,0:T(8,128)S(1)} custom-call(s32[1]{0:T(128)} %bitcast.core_ref, bf16[2,160,256]{2,1,0:T(8,128)(2,1)S(1)} %copy-done.10, f32[128,40,128]{2,1,0:T(8,128)S(1)} %copy-done.3, f32[128,40,128]{2,1,0:T(8,128)S(1)} %collective-permute-done.38.refs_1_), custom_call_target="tpu_custom_call" | custom-call | flops 3221225472 | bytes 16777216 | tf_op jit(solution)/shard_map/inverse/pallas_call | solution.py:303
  407.7 6.7 %inverse.3 = f32[128,128,128]{2,1,0:T(8,128)} custom-call(s32[1]{0:T(128)} %bitcast.core_ref, bf16[2,96,256]{2,1,0:T(8,128)(2,1)S(1)} %copy-done.11, f32[128,24,128]{2,1,0:T(8,128)S(1)} %get-tuple-element.28.refs_0_, f32[128,24,128]{2,1,0:T(8,128)S(1)} %collective-permute-done.14.refs_1_, f32[128,128,128]{2,1,0:T(8,128)S(1)} %inverse.2.refs_2_), custom_call_target="tpu_custom_call" | custom-call | flops 3221225472 | bytes 16777216 | tf_op jit(solution)/shard_map/inverse/pallas_call | solution.py:303
  (115 shorter events, 39.1 us)
Async XLA Ops:
  3.3 30.7 %collective-permute-start.17 = (f32[40,32,128]{2,1,0:T(8,128)}, f32[40,32,128]{2,1,0:T(8,128)S(1)}, u32[]{:S(2)}, u32[]{:S(2)}) collective-permute-start(f32[40,32,128]{2,1,0:T(8,128)} %forward.8.refs_0_), channel_id=1, source_target_pairs={{0,8},{8,24},{24,16},{16,0},{1,9},{9,25},{25,17},{17,1},{2,10},{10... | collective-permute-start | bytes 1966088 | tf_op jit(solution)/shard_map/ppermute | solution.py:394
  18.3 33.0 %collective-permute-start.15 = (f32[40,64,128]{2,1,0:T(8,128)}, f32[40,64,128]{2,1,0:T(8,128)}, u32[]{:S(2)}, u32[]{:S(2)}) collective-permute-start(f32[40,64,128]{2,1,0:T(8,128)} %forward.7.refs_9_.refs_12_), channel_id=1, source_target_pairs={{0,2},{1,3},{2,4},{3,5},{4,6},{5,7},{8,10},{9,11},{10,12},{11,13},... | collective-permute-start | bytes 3932168 | tf_op jit(solution)/shard_map/ppermute | solution.py:388
  23.4 38.7 %collective-permute-start.26 = (f32[40,64,128]{2,1,0:T(8,128)}, f32[40,64,128]{2,1,0:T(8,128)}, u32[]{:S(2)}, u32[]{:S(2)}) collective-permute-start(f32[40,64,128]{2,1,0:T(8,128)} %get-tuple-element.32), channel_id=1, source_target_pairs={{0,1},{1,0},{2,3},{3,2},{4,5},{5,4},{6,7},{7,6},{8,9},{9,8},{10,11... | collective-permute-start | bytes 3932168 | tf_op jit(solution)/shard_map/ppermute | solution.py:374
  34.0 34.8 %collective-permute-start.2 = (f32[24,128,128]{2,1,0:T(8,128)}, f32[24,128,128]{2,1,0:T(8,128)}, u32[]{:S(2)}, u32[]{:S(2)}) collective-permute-start(f32[24,128,128]{2,1,0:T(8,128)} %get-tuple-element.25), channel_id=1, source_target_pairs={{0,1},{1,0},{2,3},{3,2},{4,5},{5,4},{6,7},{7,6},{8,9},{9,8},{10,11... | collective-permute-start | bytes 4718600 | tf_op jit(solution)/shard_map/ppermute | solution.py:375
  34.4 32.9 %collective-permute-start.28 = (f32[40,64,128]{2,1,0:T(8,128)S(1)}, f32[40,64,128]{2,1,0:T(8,128)}, u32[]{:S(2)}, u32[]{:S(2)}) collective-permute-start(f32[40,64,128]{2,1,0:T(8,128)S(1)} %copy-done.1), channel_id=1, source_target_pairs={{2,0},{3,1},{4,2},{5,3},{6,4},{7,5},{10,8},{11,9},{12,10},{13,11},... | collective-permute-start | bytes 3932168 | tf_op jit(solution)/shard_map/ppermute | solution.py:389
  51.3 37.6 %collective-permute-start.3 = (f32[24,128,128]{2,1,0:T(8,128)}, f32[24,128,128]{2,1,0:T(8,128)}, u32[]{:S(2)}, u32[]{:S(2)}) collective-permute-start(f32[24,128,128]{2,1,0:T(8,128)} %get-tuple-element.24.refs_0_), channel_id=1, source_target_pairs={{0,8},{8,24},{24,16},{16,0},{1,9},{9,25},{25,17},{17,1},{2,10},{10... | collective-permute-start | bytes 4718600 | tf_op jit(solution)/shard_map/ppermute | solution.py:394
  53.6 40.8 %collective-permute-start.8 = (f32[24,128,128]{2,1,0:T(8,128)}, f32[24,128,128]{2,1,0:T(8,128)}, u32[]{:S(2)}, u32[]{:S(2)}) collective-permute-start(f32[24,128,128]{2,1,0:T(8,128)} %get-tuple-element.24.refs_0_), channel_id=1, source_target_pairs={{8,0},{24,8},{16,24},{0,16},{9,1},{25,9},{17,25},{1,17},{10,2},{26... | collective-permute-start | bytes 4718600 | tf_op jit(solution)/shard_map/ppermute | solution.py:395
  62.1 67.6 %collective-permute-start.18 = (f32[40,96,128]{2,1,0:T(8,128)}, f32[40,96,128]{2,1,0:T(8,128)}, u32[]{:S(2)}, u32[]{:S(2)}) collective-permute-start(f32[40,96,128]{2,1,0:T(8,128)} %forward.9.refs_1_), channel_id=1, source_target_pairs={{0,8},{8,24},{24,16},{16,0},{1,9},{9,25},{25,17},{17,1},{2,10},{10... | collective-permute-start | bytes 5898248 | tf_op jit(solution)/shard_map/ppermute | solution.py:394
  67.3 68.4 %collective-permute-start.25 = (f32[40,96,128]{2,1,0:T(8,128)}, f32[40,96,128]{2,1,0:T(8,128)S(1)}, u32[]{:S(2)}, u32[]{:S(2)}) collective-permute-start(f32[40,96,128]{2,1,0:T(8,128)} %forward.9.refs_1_), channel_id=1, source_target_pairs={{8,0},{24,8},{16,24},{0,16},{9,1},{25,9},{17,25},{1,17},{10,2},{26... | collective-permute-start | bytes 5898248 | tf_op jit(solution)/shard_map/ppermute | solution.py:395
  68.8 81.1 %collective-permute-start.16 = (f32[40,128,128]{2,1,0:T(8,128)}, f32[40,128,128]{2,1,0:T(8,128)}, u32[]{:S(2)}, u32[]{:S(2)}) collective-permute-start(f32[40,128,128]{2,1,0:T(8,128)} %get-tuple-element.31), channel_id=1, source_target_pairs={{0,1},{1,0},{2,3},{3,2},{4,5},{5,4},{6,7},{7,6},{8,9},{9,8},{10,11... | collective-permute-start | bytes 7864328 | tf_op jit(solution)/shard_map/ppermute | solution.py:375
  88.8 53.4 %collective-permute-start.1 = (f32[2,24,64,128]{3,2,1,0:T(8,128)S(1)}, f32[2,24,64,128]{3,2,1,0:T(8,128)}, u32[]{:S(2)}, u32[]{:S(2)}) collective-permute-start(f32[2,24,64,128]{3,2,1,0:T(8,128)S(1)} %pad_maximum_fusion.refs_6_.refs_8_), channel_id=1, source_target_pairs={{0,2},{1,3},{2,4},{3,5},{4,6},{5,7},{8,10},{9,11},{10,12},{11,13},... | collective-permute-start | bytes 4718600 | tf_op jit(solution)/shard_map/ppermute | solution.py:388
  94.4 49.2 %collective-permute-start.9 = (f32[2,24,64,128]{3,2,1,0:T(8,128)S(1)}, f32[2,24,64,128]{3,2,1,0:T(8,128)}, u32[]{:S(2)}, u32[]{:S(2)}) collective-permute-start(f32[2,24,64,128]{3,2,1,0:T(8,128)S(1)} %pad_maximum_fusion.refs_6_.refs_8_), channel_id=1, source_target_pairs={{2,0},{3,1},{4,2},{5,3},{6,4},{7,5},{10,8},{11,9},{12,10},{13,11},... | collective-permute-start | bytes 4718600 | tf_op jit(solution)/shard_map/ppermute | solution.py:389
  129.6 33.8 %collective-permute-start.27 = (f32[40,64,128]{2,1,0:T(8,128)}, f32[40,64,128]{2,1,0:T(8,128)}, u32[]{:S(2)}, u32[]{:S(2)}) collective-permute-start(f32[40,64,128]{2,1,0:T(8,128)} %collective-permute-done.26.refs_10_.refs_13_), channel_id=1, source_target_pairs={{0,2},{1,3},{2,4},{3,5},{4,6},{5,7},{8,10},{9,11},{10,12},{11,13},... | collective-permute-start | bytes 3932168 | tf_op jit(solution)/shard_map/ppermute | solution.py:388
  135.7 33.9 %collective-permute-start.29 = (f32[40,64,128]{2,1,0:T(8,128)}, f32[40,64,128]{2,1,0:T(8,128)}, u32[]{:S(2)}, u32[]{:S(2)}) collective-permute-start(f32[40,64,128]{2,1,0:T(8,128)} %collective-permute-done.28.refs_17_.refs_24_), channel_id=1, source_target_pairs={{2,0},{3,1},{4,2},{5,3},{6,4},{7,5},{10,8},{11,9},{12,10},{13,11},... | collective-permute-start | bytes 3932168 | tf_op jit(solution)/shard_map/ppermute | solution.py:389
  142.3 52.9 %collective-permute-start.31 = (f32[40,64,128]{2,1,0:T(8,128)}, f32[40,64,128]{2,1,0:T(8,128)}, u32[]{:S(2)}, u32[]{:S(2)}) collective-permute-start(f32[40,64,128]{2,1,0:T(8,128)} %collective-permute-done.26.refs_10_.refs_13_), channel_id=1, source_target_pairs={{2,0},{3,1},{4,2},{5,3},{6,4},{7,5},{10,8},{11,9},{12,10},{13,11},... | collective-permute-start | bytes 3932168 | tf_op jit(solution)/shard_map/ppermute | solution.py:389
  143.6 52.9 %collective-permute-start.34 = (f32[40,64,128]{2,1,0:T(8,128)}, f32[40,64,128]{2,1,0:T(8,128)}, u32[]{:S(2)}, u32[]{:S(2)}) collective-permute-start(f32[40,64,128]{2,1,0:T(8,128)} %collective-permute-done.15.refs_11_.refs_14_), channel_id=1, source_target_pairs={{0,2},{1,3},{2,4},{3,5},{4,6},{5,7},{8,10},{9,11},{10,12},{11,13},... | collective-permute-start | bytes 3932168 | tf_op jit(solution)/shard_map/ppermute | solution.py:388
  149.9 100.2 %collective-permute-start.22 = (f32[40,128,128]{2,1,0:T(8,128)}, f32[40,128,128]{2,1,0:T(8,128)}, u32[]{:S(2)}, u32[]{:S(2)}) collective-permute-start(f32[40,128,128]{2,1,0:T(8,128)} %collective-permute-done.16.refs_2_), channel_id=1, source_target_pairs={{8,0},{24,8},{16,24},{0,16},{9,1},{25,9},{17,25},{1,17},{10,2},{26... | collective-permute-start | bytes 7864328 | tf_op jit(solution)/shard_map/ppermute | solution.py:395
  163.5 77.1 %collective-permute-start.6 = (f32[24,128,128]{2,1,0:T(8,128)}, f32[24,128,128]{2,1,0:T(8,128)}, u32[]{:S(2)}, u32[]{:S(2)}) collective-permute-start(f32[24,128,128]{2,1,0:T(8,128)} %collective-permute-done.2.refs_1_), channel_id=1, source_target_pairs={{8,0},{24,8},{16,24},{0,16},{9,1},{25,9},{17,25},{1,17},{10,2},{26... | collective-permute-start | bytes 4718600 | tf_op jit(solution)/shard_map/ppermute | solution.py:395
  169.6 75.2 %collective-permute-start.21 = (f32[40,96,128]{2,1,0:T(8,128)}, f32[40,96,128]{2,1,0:T(8,128)}, u32[]{:S(2)}, u32[]{:S(2)}) collective-permute-start(f32[40,96,128]{2,1,0:T(8,128)} %collective-permute-done.18.refs_4_), channel_id=1, source_target_pairs={{0,8},{8,24},{24,16},{16,0},{1,9},{9,25},{25,17},{17,1},{2,10},{10... | collective-permute-start | bytes 5898248 | tf_op jit(solution)/shard_map/ppermute | solution.py:399
  195.2 46.7 %collective-permute-start.10 = (f32[2,24,64,128]{3,2,1,0:T(8,128)}, f32[2,24,64,128]{3,2,1,0:T(8,128)}, u32[]{:S(2)}, u32[]{:S(2)}) collective-permute-start(f32[2,24,64,128]{3,2,1,0:T(8,128)} %collective-permute-done.9.refs_10_.refs_14_), channel_id=1, source_target_pairs={{2,0},{3,1},{4,2},{5,3},{6,4},{7,5},{10,8},{11,9},{12,10},{13,11},... | collective-permute-start | bytes 4718600 | tf_op jit(solution)/shard_map/ppermute | solution.py:389
  196.5 46.9 %collective-permute-start.12 = (f32[2,24,64,128]{3,2,1,0:T(8,128)}, f32[2,24,64,128]{3,2,1,0:T(8,128)}, u32[]{:S(2)}, u32[]{:S(2)}) collective-permute-start(f32[2,24,64,128]{3,2,1,0:T(8,128)} %collective-permute-done.1.refs_7_.refs_9_), channel_id=1, source_target_pairs={{0,2},{1,3},{2,4},{3,5},{4,6},{5,7},{8,10},{9,11},{10,12},{11,13},... | collective-permute-start | bytes 4718600 | tf_op jit(solution)/shard_map/ppermute | solution.py:388
  240.6 33.7 %collective-permute-start.30 = (f32[40,64,128]{2,1,0:T(8,128)}, f32[40,64,128]{2,1,0:T(8,128)S(1)}, u32[]{:S(2)}, u32[]{:S(2)}) collective-permute-start(f32[40,64,128]{2,1,0:T(8,128)} %collective-permute-done.29.refs_15_.refs_20_), channel_id=1, source_target_pairs={{2,0},{3,1},{4,2},{5,3},{6,4},{7,5},{10,8},{11,9},{12,10},{13,11},... | collective-permute-start | bytes 3932168 | tf_op jit(solution)/shard_map/ppermute | solution.py:389
  241.9 65.3 %collective-permute-start.19 = (f32[40,128,128]{2,1,0:T(8,128)}, f32[40,128,128]{2,1,0:T(8,128)}, u32[]{:S(2)}, u32[]{:S(2)}) collective-permute-start(f32[40,128,128]{2,1,0:T(8,128)} %collective-permute-done.16.refs_2_), channel_id=1, source_target_pairs={{0,8},{8,24},{24,16},{16,0},{1,9},{9,25},{25,17},{17,1},{2,10},{10... | collective-permute-start | bytes 7864328 | tf_op jit(solution)/shard_map/ppermute | solution.py:394
  243.5 55.1 %collective-permute-start.32 = (f32[40,64,128]{2,1,0:T(8,128)}, f32[40,64,128]{2,1,0:T(8,128)S(1)}, u32[]{:S(2)}, u32[]{:S(2)}) collective-permute-start(f32[40,64,128]{2,1,0:T(8,128)} %collective-permute-done.31.refs_18_.refs_25_), channel_id=1, source_target_pairs={{2,0},{3,1},{4,2},{5,3},{6,4},{7,5},{10,8},{11,9},{12,10},{13,11},... | collective-permute-start | bytes 3932168 | tf_op jit(solution)/shard_map/ppermute | solution.py:389
  244.8 56.2 %collective-permute-start.35 = (f32[40,64,128]{2,1,0:T(8,128)}, f32[40,64,128]{2,1,0:T(8,128)S(1)}, u32[]{:S(2)}, u32[]{:S(2)}) collective-permute-start(f32[40,64,128]{2,1,0:T(8,128)} %collective-permute-done.27.refs_12_.refs_15_), channel_id=1, source_target_pairs={{0,2},{1,3},{2,4},{3,5},{4,6},{5,7},{8,10},{9,11},{10,12},{11,13},... | collective-permute-start | bytes 3932168 | tf_op jit(solution)/shard_map/ppermute | solution.py:388
  250.0 82.3 %collective-permute-start.23 = (f32[40,128,128]{2,1,0:T(8,128)}, f32[40,128,128]{2,1,0:T(8,128)}, u32[]{:S(2)}, u32[]{:S(2)}) collective-permute-start(f32[40,128,128]{2,1,0:T(8,128)} %collective-permute-done.22.refs_8_.refs_11_), channel_id=1, source_target_pairs={{8,0},{24,8},{16,24},{0,16},{9,1},{25,9},{17,25},{1,17},{10,2},{26... | collective-permute-start | bytes 7864328 | tf_op jit(solution)/shard_map/ppermute | solution.py:400
  274.4 31.3 %collective-permute-start.36 = (f32[40,64,128]{2,1,0:T(8,128)}, f32[40,64,128]{2,1,0:T(8,128)S(1)}, u32[]{:S(2)}, u32[]{:S(2)}) collective-permute-start(f32[40,64,128]{2,1,0:T(8,128)} %collective-permute-done.34.refs_13_.refs_18_), channel_id=1, source_target_pairs={{0,2},{1,3},{2,4},{3,5},{4,6},{5,7},{8,10},{9,11},{10,12},{11,13},... | collective-permute-start | bytes 3932168 | tf_op jit(solution)/shard_map/ppermute | solution.py:388
  305.6 71.6 %collective-permute-start.4 = (f32[24,128,128]{2,1,0:T(8,128)}, f32[24,128,128]{2,1,0:T(8,128)}, u32[]{:S(2)}, u32[]{:S(2)}) collective-permute-start(f32[24,128,128]{2,1,0:T(8,128)} %collective-permute-done.2.refs_1_), channel_id=1, source_target_pairs={{0,8},{8,24},{24,16},{16,0},{1,9},{9,25},{25,17},{17,1},{2,10},{10... | collective-permute-start | bytes 4718600 | tf_op jit(solution)/shard_map/ppermute | solution.py:394
  307.2 81.7 %collective-permute-start.5 = (f32[24,128,128]{2,1,0:T(8,128)}, f32[24,128,128]{2,1,0:T(8,128)}, u32[]{:S(2)}, u32[]{:S(2)}) collective-permute-start(f32[24,128,128]{2,1,0:T(8,128)} %collective-permute-done.3.refs_2_), channel_id=1, source_target_pairs={{0,8},{8,24},{24,16},{16,0},{1,9},{9,25},{25,17},{17,1},{2,10},{10... | collective-permute-start | bytes 4718600 | tf_op jit(solution)/shard_map/ppermute | solution.py:399
  328.6 60.4 %collective-permute-start.7 = (f32[24,128,128]{2,1,0:T(8,128)}, f32[24,128,128]{2,1,0:T(8,128)}, u32[]{:S(2)}, u32[]{:S(2)}) collective-permute-start(f32[24,128,128]{2,1,0:T(8,128)} %collective-permute-done.6.refs_5_.refs_7_), channel_id=1, source_target_pairs={{8,0},{24,8},{16,24},{0,16},{9,1},{25,9},{17,25},{1,17},{10,2},{26... | collective-permute-start | bytes 4718600 | tf_op jit(solution)/shard_map/ppermute | solution.py:400
  331.1 57.9 %collective-permute-start.11 = (f32[2,24,64,128]{3,2,1,0:T(8,128)}, f32[2,24,64,128]{3,2,1,0:T(8,128)}, u32[]{:S(2)}, u32[]{:S(2)}) collective-permute-start(f32[2,24,64,128]{3,2,1,0:T(8,128)} %collective-permute-done.10.refs_9_.refs_12_), channel_id=1, source_target_pairs={{2,0},{3,1},{4,2},{5,3},{6,4},{7,5},{10,8},{11,9},{12,10},{13,11},... | collective-permute-start | bytes 4718600 | tf_op jit(solution)/shard_map/ppermute | solution.py:389
  332.4 56.6 %collective-permute-start.13 = (f32[2,24,64,128]{3,2,1,0:T(8,128)}, f32[2,24,64,128]{3,2,1,0:T(8,128)}, u32[]{:S(2)}, u32[]{:S(2)}) collective-permute-start(f32[2,24,64,128]{3,2,1,0:T(8,128)} %collective-permute-done.12.refs_8_.refs_11_), channel_id=1, source_target_pairs={{0,2},{1,3},{2,4},{3,5},{4,6},{5,7},{8,10},{9,11},{10,12},{11,13},... | collective-permute-start | bytes 4718600 | tf_op jit(solution)/shard_map/ppermute | solution.py:388
  (29 other events, 1341.2 us)

commit v5 on v4

--- a/solution.py
+++ b/solution.py
@@ -12,9 +12,9 @@
 
 NT = 128
 NF = 64
-SPLIT = (0, 1)
 SHARES = (20, 12)
-GRANT = 50 << 20
+SMALL = 4 << 20
+GRANT = 46 << 20
 F32, BF16 = jnp.float32, jnp.bfloat16
 
 
@@ -100,12 +100,14 @@
     )(core, jnp.asarray(w), x)
 
 
-ALL, EARLY, LATE = range(3)
+ALL, EARLY, LATE, MIDDLE, FAR = range(5)
+CALLS = ((EARLY, MIDDLE, FAR), (EARLY, LATE))
 
 
 def sides(part, levels):
     pairs = [[("own", 0)]] + [[("up", s), ("down", levels - s)] for s in range(1, levels)]
-    return [[x for x in pair if part != EARLY or x[1] < levels - 1] for pair in pairs]
+    taken = {EARLY: lambda hop: hop < levels - 1, MIDDLE: lambda hop: hop < levels - 1, FAR: lambda hop: hop == levels - 1}
+    return [[x for x in pair if taken.get(part, lambda hop: True)(x[1])] for pair in pairs]
 
 
 def product_kernel(part, levels, places, d_keys, g_keys, slot_ref, *refs):
@@ -150,14 +152,15 @@
             for half_of in range(2):
                 row = 2 * b + half_of
                 blocks = [sum(g_refs[way, hop, h][row] for way, hop in pair) for pair in sides(part, levels)]
-                if part == LATE:
+                if part in (LATE, MIDDLE):
                     met = blocks[0]
                     for s in range(1, levels):
                         met = jnp.where(slot_ref[s] == 0, blocks[s], met)
+                    put_g(b, 0, h, half_of, met)
+                if part in (LATE, FAR):
                     last = g_refs["up", levels - 1, h][row] + g_refs["down", levels - 1, h][row]
-                    put_g(b, 0, h, half_of, met)
-                    put_g(b, 1, h, half_of, jnp.where(far > 0, last, 0.0))
-                else:
+                    put_g(b, len(places) - 1, h, half_of, jnp.where(far > 0, last, 0.0))
+                if part in (ALL, EARLY):
                     for s, block in enumerate(blocks):
                         put_g(b, slot_ref[s], h, half_of, block)
         for place, which in enumerate(places):
@@ -166,16 +169,16 @@
         p = jnp.dot(lhs[b % 2, :, :deep], rhs[b % 2, :deep, :], preferred_element_type=F32)
         real = p[: 2 * rows, :cols] - p[2 * rows :, cols:]
         imaginary = p[: 2 * rows, cols:] + p[2 * rows :, :cols]
-        if part == EARLY:
-            rest[0][2 * b], rest[0][2 * b + 1] = real, imaginary
+        if part not in (ALL, EARLY):
+            real, imaginary = real + rest[0][2 * b], imaginary + rest[0][2 * b + 1]
+        if part in (EARLY, MIDDLE):
+            rest[-3][2 * b], rest[-3][2 * b + 1] = real, imaginary
             continue
-        if part == LATE:
-            real, imaginary = real + rest[0][2 * b], imaginary + rest[0][2 * b + 1]
         held = rest[-3]
         row = 2 * (step % each * count + b)
         held[row], held[row + 1] = real, imaginary
 
-    if part != EARLY:
+    if part not in (EARLY, MIDDLE):
 
         @pl.when(step % each == each - 1)
         def _():
@@ -191,22 +194,25 @@
     around = len(d)
     diag = around // 2
     far_a = slot[jnp.where(z == 0, 1, levels - 1)]
-    far = ((z == 0) | (z == levels - 1)) & (far_a != diag)
+    far = ((z == 0) | (z == levels - 1)) & ((far_a != diag) | (part == FAR))
     chosen = jnp.where(far, far_a, 0)
     others = [a for a in range(around) if a != diag]
     if part == ALL:
         places, to = [[a] for a in range(around)], slot
     elif part == EARLY:
         places, to = [[a] for a in others], jnp.where(slot == diag, len(others), slot - (slot > diag))
+    elif part == FAR:
+        places, to = [list(range(around))], slot
     else:
-        places, to = [[diag], others], jnp.where(slot == diag, 0, 2)
+        places, to = [[diag], others][: 2 if part == LATE else 1], jnp.where(slot == diag, 0, 2)
     needed = []
     for a in sorted(set(sum(places, []))):
-        needed += [chosen == a if part == LATE and a != diag else True] * d[a]
+        picked = part == FAR or (part == LATE and a != diag)
+        needed += [far & (chosen == a) if picked else True] * d[a]
     for s, pair in enumerate(sides(part, levels)):
         for way, hop in pair:
             there = {"own": True, "up": z >= hop, "down": z + hop < levels}[way]
-            if part == LATE:
+            if part in (LATE, MIDDLE):
                 there = there & ((slot[s] == diag) | (hop == levels - 1))
             needed += [there] * g
     needed.append(True)
@@ -217,6 +223,7 @@
 
 def product(part, places, scalars, d, g, so_far=None):
     levels = 1 + max(hop for _, hop in g)
+    raw = part in (EARLY, MIDDLE)
     depth = d[0][0].shape[2]
     n = d[0][0].shape[0]
     rows = sum(x.shape[1] for x in d[0]) // 2
@@ -234,8 +241,9 @@
             for h, x in enumerate(g[way, hop]):
                 g_keys.append((way, hop, h if len(g[way, hop]) == 2 else None))
                 operands.append(x)
+    small = 8 * n * rows * cols <= SMALL
     if so_far is not None:
-        operands.append(so_far)
+        operands.append(pltpu.with_memory_space_constraint(so_far, pltpu.VMEM) if small else so_far)
     first = levels + 3
 
     def spec(i, x):
@@ -248,8 +256,8 @@
         pltpu.VMEM((2, 4 * rows, 3 * depth * len(places)), BF16),
         pltpu.VMEM((2, 3 * depth * (len(places) + 1), 2 * cols), BF16),
     ]
-    if part == EARLY:
-        out = jax.ShapeDtypeStruct((n, 2 * rows, cols), F32)
+    if raw:
+        out = (pltpu.VMEM if small else jax.ShapeDtypeStruct)((n, 2 * rows, cols), F32)
         out_specs = pl.BlockSpec((step, 2 * rows, cols), lambda i, c: (i, 0, 0))
     else:
         out = [jax.ShapeDtypeStruct((rows, n, cols), F32)] * 2
@@ -265,7 +273,7 @@
             scratch_shapes=scratch,
         ),
         out_shape=out,
-        compiler_params=pltpu.CompilerParams(vmem_limit_bytes=GRANT if part == LATE else None),
+        compiler_params=pltpu.CompilerParams(vmem_limit_bytes=GRANT if part == LATE and small else None),
         cost_estimate=pl.CostEstimate(
             flops=n // 2 * 2 * 4 * rows * 3 * len(places) * depth * 2 * cols,
             bytes_accessed=4 * sum(x.size for x in operands),
@@ -310,7 +318,7 @@
             out_specs=pl.BlockSpec((step, cols, NT), lambda i, c: (i, 0, 0)),
         ),
         out_shape=(pltpu.VMEM if so_far is None else jax.ShapeDtypeStruct)((rows, cols, NT), F32),
-        compiler_params=pltpu.CompilerParams(vmem_limit_bytes=GRANT - (12 << 20)),
+        compiler_params=pltpu.CompilerParams(vmem_limit_bytes=GRANT - (8 << 20)),
         cost_estimate=pl.CostEstimate(
             flops=12 * rows * cols * NT * NT, bytes_accessed=8 * rows * cols * NT, transcendentals=0
         ),
@@ -374,7 +382,7 @@
         g_own = [g_parts[c], lax.ppermute(g_parts[chunks + c], "src", partner)]
         d_swapped = lax.ppermute(d_parts[chunks + c], "src", partner)
         d_own = [d_parts[c], d_swapped] if c else head + [d_parts[c], d_swapped]
-        calls = (EARLY, LATE) if c in SPLIT else (ALL,)
+        calls = CALLS[c]
         counts = {a: len(d_own) for a in range(around)}
         plans = [numbers(part, me, counts, 1 if c else 2) for part in calls]
         if c:

time: 416 us -> 433 us (1.041)
  Pallas kernels: 107 us -> 117 us
  waiting for transfers between devices: 216 us -> 223 us
  starting transfers between devices: 80.5 us -> 75.1 us
    ppermute x9, waiting for transfers between devices: 27.1 us -> 84.2 us  [local(): up = [lax.ppermute(x, 'src', upward) for x in up]]
    ppermute x9, waiting for transfers between devices: 97.6 us -> 52.7 us  [local(): down = [lax.ppermute(x, 'src', downward) for x in down]]
    ppermute x5, waiting for transfers between devices: 52.5 us -> 22.2 us  [local(): right = [lax.ppermute(x, 'freq', clockwise) for x in right]]
    ppermute x3, waiting for transfers between devices: 0.01 us -> 29.4 us  [local(): d[last] = [lax.ppermute(x, 'freq', clockwise) for x in right[:mine]]]
    pallas_call x4 -> x5, Pallas kernels: 61.3 us -> 70.8 us  [product(): pl.pallas_call(functools.partial(product_kernel, part, levels, places, d_...]
  transfers between devices with their start and end apart: 39 -> 39, of which waited for: 12 -> 14; matrix products, arithmetic and copies ran while one was open for 1% -> 2% of each run, Pallas kernels for 23% -> 25%
where the time goes in v5:
time: 433 us; the launch traced here: 431 us
  waiting for transfers between devices  223 us (52%)
  Pallas kernels  117 us (27%)
  starting transfers between devices  75.1 us (17%)
  local copies, waits for them, and re-layouts  9.07 us (2%)
  between operations  5.12 us (1%)
    ppermute x9, waiting for transfers between devices, local(): up = [lax.ppermute(x, 'src', upward) for x in up]  84.2 us
    pallas_call x5, Pallas kernels, product(): pl.pallas_call(functools.partial(product_kernel, part, levels, places, d_...  70.8 us
    ppermute x9, waiting for transfers between devices, local(): down = [lax.ppermute(x, 'src', downward) for x in down]  52.7 us
    ppermute x9, starting transfers between devices, local(): up = [lax.ppermute(x, 'src', upward) for x in up]  43.3 us
    ppermute x5, waiting for transfers between devices, local(): left = [lax.ppermute(x, 'freq', counter) for x in left]  34.4 us
    pallas_call x5, Pallas kernels, forward(): pl.pallas_call(functools.partial(forward_kernel, counts), grid_spec=pltpu...  32.7 us
    ppermute x3, waiting for transfers between devices, local(): d[last] = [lax.ppermute(x, 'freq', clockwise) for x in right[:mine]]  29.4 us
    ppermute x5, waiting for transfers between devices, local(): right = [lax.ppermute(x, 'freq', clockwise) for x in right]  22.2 us
  transfers between devices with their start and end apart: 39, of which 14 were waited for; matrix products, arithmetic and copies ran while one was open for 2% of the time, Pallas kernels for 25%

profile of v5, /device:TPU:0, one launch (start us, length us, event | category | flops | bytes accessed | tf_op | source)
XLA Modules:
  0.0 430.9 jit_solution(12422573932000134220)
XLA Ops:
  6.4 5.4 %forward.7.refs_9_.refs_3_ = f32[40,64,128]{2,1,0:T(8,128)} custom-call(s32[1]{0:T(128)} %bitcast.core_ref, bf16[2,80,256]{2,1,0:T(8,128)(2,1)} %constant.81.clone.w_ref, f32[64,128,128]{2,1,0:T(8,128)} %x_ref.7), custom_call_target="tpu_custom_call" | custom-call | flops 1610612736 | bytes 8388608 | tf_op jit(solution)/shard_map/forward/pallas_call | solution.py:84
  11.8 4.2 collective-permute-start.15
  16.0 6.5 %forward.5 = (f32[24,64,128]{2,1,0:T(8,128)}, f32[40,64,128]{2,1,0:T(8,128)}, f32[24,64,128]{2,1,0:T(8,128)}) custom-call(s32[1]{0:T(128)} %bitcast.core_ref, bf16[2,176,256]{2,1,0:T(8,128)(2,1)} %constant.82.clone.w_ref, f32[64,128,128]{2,1,0:T(8,128)} %x_ref.7), custom_call_target="tpu_custom_call" | custom-call | flops 1610612736 | bytes 8388608 | tf_op jit(solution)/shard_map/forward/pallas_call | solution.py:84
  24.4 10.4 %forward.6 = (f32[24,128,128]{2,1,0:T(8,128)}, f32[40,128,128]{2,1,0:T(8,128)}, f32[24,128,128]{2,1,0:T(8,128)}) custom-call(s32[1]{0:T(128)} %bitcast.core_ref, bf16[2,176,256]{2,1,0:T(8,128)(2,1)} %constant.82.clone.w_ref, f32[128,128,128]{2,1,0:T(8,128)} %x_ref.9), custom_call_target="tpu_custom_call" | custom-call | flops 3221225472 | bytes 16777216 | tf_op jit(solution)/shard_map/forward/pallas_call | solution.py:84
  36.5 7.2 %collective-permute-done.15.refs_11_.refs_5_ = f32[40,64,128]{2,1,0:T(8,128)S(1)} collective-permute-done((f32[40,64,128]{2,1,0:T(8,128)}, f32[40,64,128]{2,1,0:T(8,128)S(1)}, u32[]{:S(2)}, u32[]{:S(2)}) %collective-permute-start.15) | collective-permute-done | bytes 1310752 | tf_op jit(solution)/shard_map/ppermute | solution.py:396
  45.7 7.0 %forward.9.refs_1_ = f32[40,96,128]{2,1,0:T(8,128)} custom-call(s32[1]{0:T(128)} %bitcast.core_ref, bf16[2,80,256]{2,1,0:T(8,128)(2,1)} %constant.81.clone.w_ref, f32[128,128,128]{2,1,0:T(8,128)} %x_ref.9), custom_call_target="tpu_custom_call" | custom-call | flops 2415919104 | bytes 12582912 | tf_op jit(solution)/shard_map/forward/pallas_call | solution.py:84
  57.2 29.4 %collective-permute-done.20.refs_0_.refs_6_ = f32[40,32,128]{2,1,0:T(8,128)} collective-permute-done((f32[40,32,128]{2,1,0:T(8,128)S(1)}, f32[40,32,128]{2,1,0:T(8,128)}, u32[]{:S(2)}, u32[]{:S(2)}) %collective-permute-start.20) | collective-permute-done | bytes 655392 | tf_op jit(solution)/shard_map/ppermute | solution.py:407
  89.6 5.5 %collective-permute-start.1 = (f32[2,24,64,128]{3,2,1,0:T(8,128)S(1)}, f32[2,24,64,128]{3,2,1,0:T(8,128)}, u32[]{:S(2)}, u32[]{:S(2)}) collective-permute-start(f32[2,24,64,128]{3,2,1,0:T(8,128)S(1)} %pad_maximum_fusion.refs_6_.refs_8_), channel_id=1, source_target_pairs={{0,2},{1,3},{2,4},{3,5},{4,6},{5,7},{8,10},{9,11},{10,12},{11,13},... | collective-permute-start | bytes 4718600 | tf_op jit(solution)/shard_map/ppermute | solution.py:396
  105.9 22.2 %collective-permute-done.18.refs_4_ = f32[40,96,128]{2,1,0:T(8,128)} collective-permute-done((f32[40,96,128]{2,1,0:T(8,128)}, f32[40,96,128]{2,1,0:T(8,128)}, u32[]{:S(2)}, u32[]{:S(2)}) %collective-permute-start.18) | collective-permute-done | bytes 1966112 | tf_op jit(solution)/shard_map/ppermute | solution.py:402
  128.1 5.4 %collective-permute-start.33 = (f32[40,64,128]{2,1,0:T(8,128)}, f32[40,64,128]{2,1,0:T(8,128)}, u32[]{:S(2)}, u32[]{:S(2)}) collective-permute-start(f32[40,64,128]{2,1,0:T(8,128)} %copy-done.11), channel_id=1, source_target_pairs={{0,2},{1,3},{2,4},{3,5},{4,6},{5,7},{8,10},{9,11},{10,12},{11,13},... | collective-permute-start | bytes 3932168 | tf_op jit(solution)/shard_map/ppermute | solution.py:396
  134.8 5.6 %collective-permute-start.35 = (f32[40,64,128]{2,1,0:T(8,128)}, f32[40,64,128]{2,1,0:T(8,128)}, u32[]{:S(2)}, u32[]{:S(2)}) collective-permute-start(f32[40,64,128]{2,1,0:T(8,128)} %collective-permute-done.29.refs_10_.refs_4_), channel_id=1, source_target_pairs={{0,2},{1,3},{2,4},{3,5},{4,6},{5,7},{8,10},{9,11},{10,12},{11,13},... | collective-permute-start | bytes 3932168 | tf_op jit(solution)/shard_map/ppermute | solution.py:396
  143.2 18.6 %collective-permute-done.33.refs_13_.refs_7_ = f32[40,64,128]{2,1,0:T(8,128)} collective-permute-done((f32[40,64,128]{2,1,0:T(8,128)}, f32[40,64,128]{2,1,0:T(8,128)}, u32[]{:S(2)}, u32[]{:S(2)}) %collective-permute-start.33) | collective-permute-done | bytes 1310752 | tf_op jit(solution)/shard_map/ppermute | solution.py:396
  163.3 4.0 collective-permute-done.30.refs_18_.refs_12_
  168.8 19.5 %collective-permute-done.35.refs_12_.refs_6_ = f32[40,64,128]{2,1,0:T(8,128)} collective-permute-done((f32[40,64,128]{2,1,0:T(8,128)}, f32[40,64,128]{2,1,0:T(8,128)}, u32[]{:S(2)}, u32[]{:S(2)}) %collective-permute-start.35) | collective-permute-done | bytes 1310752 | tf_op jit(solution)/shard_map/ppermute | solution.py:396
  189.6 5.1 %collective-permute-done.27.refs_15_.refs_9_ = f32[40,64,128]{2,1,0:T(8,128)} collective-permute-done((f32[40,64,128]{2,1,0:T(8,128)}, f32[40,64,128]{2,1,0:T(8,128)}, u32[]{:S(2)}, u32[]{:S(2)}) %collective-permute-start.27) | collective-permute-done | bytes 1310752 | tf_op jit(solution)/shard_map/ppermute | solution.py:397
  194.7 4.0 collective-permute-start.36
  198.7 34.4 %collective-permute-done.6.refs_5_.refs_7_ = f32[24,128,128]{2,1,0:T(8,128)} collective-permute-done((f32[24,128,128]{2,1,0:T(8,128)}, f32[24,128,128]{2,1,0:T(8,128)}, u32[]{:S(2)}, u32[]{:S(2)}) %collective-permute-start.6) | collective-permute-done | bytes 1572896 | tf_op jit(solution)/shard_map/ppermute | solution.py:403
  233.0 5.3 %collective-permute-start.34 = (f32[40,64,128]{2,1,0:T(8,128)}, f32[40,64,128]{2,1,0:T(8,128)}, u32[]{:S(2)}, u32[]{:S(2)}) collective-permute-start(f32[40,64,128]{2,1,0:T(8,128)} %collective-permute-done.33.refs_13_.refs_7_), channel_id=1, source_target_pairs={{0,2},{1,3},{2,4},{3,5},{4,6},{5,7},{8,10},{9,11},{10,12},{11,13},... | collective-permute-start | bytes 3932168 | tf_op jit(solution)/shard_map/ppermute | solution.py:396
  245.8 20.9 %collective-permute-done.34.refs_14_ = f32[40,64,128]{2,1,0:T(8,128)} collective-permute-done((f32[40,64,128]{2,1,0:T(8,128)}, f32[40,64,128]{2,1,0:T(8,128)}, u32[]{:S(2)}, u32[]{:S(2)}) %collective-permute-start.34) | collective-permute-done | bytes 1310752 | tf_op jit(solution)/shard_map/ppermute | solution.py:396
  268.0 9.6 %collective-permute-done.28.refs_12_ = f32[40,64,128]{2,1,0:T(8,128)S(1)} collective-permute-done((f32[40,64,128]{2,1,0:T(8,128)}, f32[40,64,128]{2,1,0:T(8,128)S(1)}, u32[]{:S(2)}, u32[]{:S(2)}) %collective-permute-start.28) | collective-permute-done | bytes 1310752 | tf_op jit(solution)/shard_map/ppermute | solution.py:397
  279.0 17.9 %collective-permute-done.12.refs_8_.refs_11_ = f32[2,24,64,128]{3,2,1,0:T(8,128)} collective-permute-done((f32[2,24,64,128]{3,2,1,0:T(8,128)}, f32[2,24,64,128]{3,2,1,0:T(8,128)}, u32[]{:S(2)}, u32[]{:S(2)}) %collective-permute-start.12) | collective-permute-done | bytes 1572896 | tf_op jit(solution)/shard_map/ppermute | solution.py:396
  296.9 5.5 %collective-permute-start.37 = (f32[40,64,128]{2,1,0:T(8,128)}, f32[40,64,128]{2,1,0:T(8,128)}, u32[]{:S(2)}, u32[]{:S(2)}) collective-permute-start(f32[40,64,128]{2,1,0:T(8,128)} %collective-permute-done.36.refs_14_.refs_8_), channel_id=1, source_target_pairs={{0,2},{1,3},{2,4},{3,5},{4,6},{5,7},{8,10},{9,11},{10,12},{11,13},... | collective-permute-start | bytes 3932168 | tf_op jit(solution)/shard_map/ppermute | solution.py:396
  302.4 9.1 %collective-permute-done.10.refs_9_.refs_12_ = f32[2,24,64,128]{3,2,1,0:T(8,128)} collective-permute-done((f32[2,24,64,128]{3,2,1,0:T(8,128)}, f32[2,24,64,128]{3,2,1,0:T(8,128)}, u32[]{:S(2)}, u32[]{:S(2)}) %collective-permute-start.10) | collective-permute-done | bytes 1572896 | tf_op jit(solution)/shard_map/ppermute | solution.py:397
  313.5 21.9 %collective-permute-done.32.refs_13_ = f32[40,64,128]{2,1,0:T(8,128)} collective-permute-done((f32[40,64,128]{2,1,0:T(8,128)}, f32[40,64,128]{2,1,0:T(8,128)}, u32[]{:S(2)}, u32[]{:S(2)}) %collective-permute-start.32) | collective-permute-done | bytes 1310752 | tf_op jit(solution)/shard_map/ppermute | solution.py:397
  336.0 4.4 %collective-permute-start.13 = (f32[2,24,64,128]{3,2,1,0:T(8,128)}, f32[2,24,64,128]{3,2,1,0:T(8,128)}, u32[]{:S(2)}, u32[]{:S(2)}) collective-permute-start(f32[2,24,64,128]{3,2,1,0:T(8,128)} %collective-permute-done.12.refs_8_.refs_11_), channel_id=1, source_target_pairs={{0,2},{1,3},{2,4},{3,5},{4,6},{5,7},{8,10},{9,11},{10,12},{11,13},... | collective-permute-start | bytes 4718600 | tf_op jit(solution)/shard_map/ppermute | solution.py:396
  341.9 17.9 %shard_map.102.refs_13_ = f32[40,256,128]{2,1,0:T(8,128)} custom-call(s32[27]{0:T(128)} %concatenate.17.slot_ref, f32[40,32,128]{2,1,0:T(8,128)} %forward.8.refs_0_, f32[40,96,128]{2,1,0:T(8,128)} %forward.9.refs_1_, f32[40,128,128]{2,1,0:T(8,128)} %collective-permute-done.16.refs_2_, f32[40,32,128]{2,1,0:T(8,128)} %copy-done.12, ...), custom_call_target="tpu_custom_call" | custom-call | flops 6039797760 | bytes 28835840 | tf_op jit(solution)/shard_map/pallas_call | solution.py:266
  359.7 13.0 %shard_map.103.refs_16_ = f32[40,256,128]{2,1,0:T(8,128)} custom-call(s32[21]{0:T(128)} %concatenate.18.slot_ref, f32[40,32,128]{2,1,0:T(8,128)} %collective-permute-done.20.refs_0_.refs_6_, f32[40,96,128]{2,1,0:T(8,128)} %collective-permute-done.21.refs_1_.refs_7_, f32[40,128,128]{2,1,0:T(8,128)} %collective-permute-done.23.refs_2_.refs_8_, ...), custom_call_target="tpu_custom_call" | custom-call | flops 2013265920 | bytes 23592960 | tf_op jit(solution)/shard_map/pallas_call | solution.py:266
  372.7 17.6 %shard_map.104 = (f32[128,40,128]{2,1,0:T(8,128)}, f32[128,40,128]{2,1,0:T(8,128)}) custom-call(s32[24]{0:T(128)} %concatenate.19.slot_ref, f32[40,32,128]{2,1,0:T(8,128)} %forward.8.refs_0_, f32[40,96,128]{2,1,0:T(8,128)} %forward.9.refs_1_, f32[40,128,128]{2,1,0:T(8,128)} %collective-permute-done.16.refs_2_, f32[40,32,128]{2,1,0:T(8,128)} %copy-done.12, ...), custom_call_target="tpu_custom_call" | custom-call | flops 2013265920 | bytes 31457280 | tf_op jit(solution)/shard_map/pallas_call | solution.py:266
  391.6 10.8 %shard_map.100.refs_15_ = f32[24,256,128]{2,1,0:T(8,128)S(1)} custom-call(s32[19]{0:T(128)} %concatenate.15.slot_ref, f32[24,128,128]{2,1,0:T(8,128)} %get-tuple-element.25.refs_0_, f32[24,128,128]{2,1,0:T(8,128)} %collective-permute-done.2.refs_1_, f32[24,128,128]{2,1,0:T(8,128)} %collective-permute-done.3.refs_2_, f32[24,128,128]{2,1,0:T(8,128)} %copy-done.9, ...), custom_call_target="tpu_custom_call" | custom-call | flops 3623878656 | bytes 17301504 | tf_op jit(solution)/shard_map/pallas_call | solution.py:266
  403.9 11.5 %shard_map.101 = (f32[128,24,128]{2,1,0:T(8,128)S(1)}, f32[128,24,128]{2,1,0:T(8,128)S(1)}) custom-call(s32[23]{0:T(128)S(1)} %concatenate.16.slot_ref, f32[24,128,128]{2,1,0:T(8,128)S(1)} %copy-done, f32[24,128,128]{2,1,0:T(8,128)} %collective-permute-done.2.refs_1_, f32[24,128,128]{2,1,0:T(8,128)} %collective-permute-done.3.refs_2_, ...), custom_call_target="tpu_custom_call" | custom-call | flops 2415919104 | bytes 26738688 | tf_op jit(solution)/shard_map/pallas_call | solution.py:266
  417.1 7.0 %inverse.2.refs_2_ = f32[128,128,128]{2,1,0:T(8,128)S(1)} custom-call(s32[1]{0:T(128)} %bitcast.core_ref, bf16[2,160,256]{2,1,0:T(8,128)(2,1)S(1)} %copy-done.4, f32[128,40,128]{2,1,0:T(8,128)S(1)} %copy-done.1, f32[128,40,128]{2,1,0:T(8,128)} %collective-permute-done.38.refs_1_), custom_call_target="tpu_custom_call" | custom-call | flops 3221225472 | bytes 16777216 | tf_op jit(solution)/shard_map/inverse/pallas_call | solution.py:311
  424.2 6.7 %inverse.3 = f32[128,128,128]{2,1,0:T(8,128)} custom-call(s32[1]{0:T(128)} %bitcast.core_ref, bf16[2,96,256]{2,1,0:T(8,128)(2,1)S(1)} %copy-done.5, f32[128,24,128]{2,1,0:T(8,128)S(1)} %copy-done.3, f32[128,24,128]{2,1,0:T(8,128)S(1)} %collective-permute-done.14.refs_1_, f32[128,128,128]{2,1,0:T(8,128)S(1)} %inverse.2.refs_2_), custom_call_target="tpu_custom_call" | custom-call | flops 3221225472 | bytes 16777216 | tf_op jit(solution)/shard_map/inverse/pallas_call | solution.py:311
  (101 shorter events, 52.2 us)
Async XLA Ops:
  22.5 33.2 %collective-permute-start.26 = (f32[40,64,128]{2,1,0:T(8,128)S(1)}, f32[40,64,128]{2,1,0:T(8,128)}, u32[]{:S(2)}, u32[]{:S(2)}) collective-permute-start(f32[40,64,128]{2,1,0:T(8,128)S(1)} %copy-done.10), channel_id=1, source_target_pairs={{2,0},{3,1},{4,2},{5,3},{6,4},{7,5},{10,8},{11,9},{12,10},{13,11},... | collective-permute-start | bytes 3932168 | tf_op jit(solution)/shard_map/ppermute | solution.py:397
  34.8 53.3 %collective-permute-start.2 = (f32[24,128,128]{2,1,0:T(8,128)}, f32[24,128,128]{2,1,0:T(8,128)}, u32[]{:S(2)}, u32[]{:S(2)}) collective-permute-start(f32[24,128,128]{2,1,0:T(8,128)} %get-tuple-element.26), channel_id=1, source_target_pairs={{0,1},{1,0},{2,3},{3,2},{4,5},{5,4},{6,7},{7,6},{8,9},{9,8},{10,11... | collective-permute-start | bytes 4718600 | tf_op jit(solution)/shard_map/ppermute | solution.py:383
  35.0 54.7 %collective-permute-start.3 = (f32[24,128,128]{2,1,0:T(8,128)}, f32[24,128,128]{2,1,0:T(8,128)}, u32[]{:S(2)}, u32[]{:S(2)}) collective-permute-start(f32[24,128,128]{2,1,0:T(8,128)} %get-tuple-element.25.refs_0_), channel_id=1, source_target_pairs={{0,8},{8,24},{24,16},{16,0},{1,9},{9,25},{25,17},{17,1},{2,10},{10... | collective-permute-start | bytes 4718600 | tf_op jit(solution)/shard_map/ppermute | solution.py:402
  43.7 52.1 %collective-permute-start.8 = (f32[24,128,128]{2,1,0:T(8,128)}, f32[24,128,128]{2,1,0:T(8,128)}, u32[]{:S(2)}, u32[]{:S(2)}) collective-permute-start(f32[24,128,128]{2,1,0:T(8,128)} %get-tuple-element.25.refs_0_), channel_id=1, source_target_pairs={{8,0},{24,8},{16,24},{0,16},{9,1},{25,9},{17,25},{1,17},{10,2},{26... | collective-permute-start | bytes 4718600 | tf_op jit(solution)/shard_map/ppermute | solution.py:403
  45.2 41.4 %collective-permute-start.20 = (f32[40,32,128]{2,1,0:T(8,128)S(1)}, f32[40,32,128]{2,1,0:T(8,128)}, u32[]{:S(2)}, u32[]{:S(2)}) collective-permute-start(f32[40,32,128]{2,1,0:T(8,128)S(1)} %collective-permute-done.17.refs_3_), channel_id=1, source_target_pairs={{0,8},{8,24},{24,16},{16,0},{1,9},{9,25},{25,17},{17,1},{2,10},{10... | collective-permute-start | bytes 1966088 | tf_op jit(solution)/shard_map/ppermute | solution.py:407
  55.7 72.4 %collective-permute-start.18 = (f32[40,96,128]{2,1,0:T(8,128)}, f32[40,96,128]{2,1,0:T(8,128)}, u32[]{:S(2)}, u32[]{:S(2)}) collective-permute-start(f32[40,96,128]{2,1,0:T(8,128)} %forward.9.refs_1_), channel_id=1, source_target_pairs={{0,8},{8,24},{24,16},{16,0},{1,9},{9,25},{25,17},{17,1},{2,10},{10... | collective-permute-start | bytes 5898248 | tf_op jit(solution)/shard_map/ppermute | solution.py:402
  86.6 46.9 %collective-permute-start.25 = (f32[40,96,128]{2,1,0:T(8,128)}, f32[40,96,128]{2,1,0:T(8,128)S(1)}, u32[]{:S(2)}, u32[]{:S(2)}) collective-permute-start(f32[40,96,128]{2,1,0:T(8,128)} %forward.9.refs_1_), channel_id=1, source_target_pairs={{8,0},{24,8},{16,24},{0,16},{9,1},{25,9},{17,25},{1,17},{10,2},{26... | collective-permute-start | bytes 5898248 | tf_op jit(solution)/shard_map/ppermute | solution.py:403
  88.1 53.6 %collective-permute-start.16 = (f32[40,128,128]{2,1,0:T(8,128)}, f32[40,128,128]{2,1,0:T(8,128)}, u32[]{:S(2)}, u32[]{:S(2)}) collective-permute-start(f32[40,128,128]{2,1,0:T(8,128)} %get-tuple-element.32), channel_id=1, source_target_pairs={{0,1},{1,0},{2,3},{3,2},{4,5},{5,4},{6,7},{7,6},{8,9},{9,8},{10,11... | collective-permute-start | bytes 7864328 | tf_op jit(solution)/shard_map/ppermute | solution.py:383
  89.6 45.1 %collective-permute-start.1 = (f32[2,24,64,128]{3,2,1,0:T(8,128)S(1)}, f32[2,24,64,128]{3,2,1,0:T(8,128)}, u32[]{:S(2)}, u32[]{:S(2)}) collective-permute-start(f32[2,24,64,128]{3,2,1,0:T(8,128)S(1)} %pad_maximum_fusion.refs_6_.refs_8_), channel_id=1, source_target_pairs={{0,2},{1,3},{2,4},{3,5},{4,6},{5,7},{8,10},{9,11},{10,12},{11,13},... | collective-permute-start | bytes 4718600 | tf_op jit(solution)/shard_map/ppermute | solution.py:396
  95.8 44.5 %collective-permute-start.9 = (f32[2,24,64,128]{3,2,1,0:T(8,128)S(1)}, f32[2,24,64,128]{3,2,1,0:T(8,128)}, u32[]{:S(2)}, u32[]{:S(2)}) collective-permute-start(f32[2,24,64,128]{3,2,1,0:T(8,128)S(1)} %pad_maximum_fusion.refs_6_.refs_8_), channel_id=1, source_target_pairs={{2,0},{3,1},{4,2},{5,3},{6,4},{7,5},{10,8},{11,9},{12,10},{13,11},... | collective-permute-start | bytes 4718600 | tf_op jit(solution)/shard_map/ppermute | solution.py:397
  128.1 33.7 %collective-permute-start.33 = (f32[40,64,128]{2,1,0:T(8,128)}, f32[40,64,128]{2,1,0:T(8,128)}, u32[]{:S(2)}, u32[]{:S(2)}) collective-permute-start(f32[40,64,128]{2,1,0:T(8,128)} %copy-done.11), channel_id=1, source_target_pairs={{0,2},{1,3},{2,4},{3,5},{4,6},{5,7},{8,10},{9,11},{10,12},{11,13},... | collective-permute-start | bytes 3932168 | tf_op jit(solution)/shard_map/ppermute | solution.py:396
  133.5 33.8 %collective-permute-start.30 = (f32[40,64,128]{2,1,0:T(8,128)}, f32[40,64,128]{2,1,0:T(8,128)}, u32[]{:S(2)}, u32[]{:S(2)}) collective-permute-start(f32[40,64,128]{2,1,0:T(8,128)} %collective-permute-done.29.refs_10_.refs_4_), channel_id=1, source_target_pairs={{2,0},{3,1},{4,2},{5,3},{6,4},{7,5},{10,8},{11,9},{12,10},{13,11},... | collective-permute-start | bytes 3932168 | tf_op jit(solution)/shard_map/ppermute | solution.py:397
  134.8 53.5 %collective-permute-start.35 = (f32[40,64,128]{2,1,0:T(8,128)}, f32[40,64,128]{2,1,0:T(8,128)}, u32[]{:S(2)}, u32[]{:S(2)}) collective-permute-start(f32[40,64,128]{2,1,0:T(8,128)} %collective-permute-done.29.refs_10_.refs_4_), channel_id=1, source_target_pairs={{0,2},{1,3},{2,4},{3,5},{4,6},{5,7},{8,10},{9,11},{10,12},{11,13},... | collective-permute-start | bytes 3932168 | tf_op jit(solution)/shard_map/ppermute | solution.py:396
  140.4 54.3 %collective-permute-start.27 = (f32[40,64,128]{2,1,0:T(8,128)}, f32[40,64,128]{2,1,0:T(8,128)}, u32[]{:S(2)}, u32[]{:S(2)}) collective-permute-start(f32[40,64,128]{2,1,0:T(8,128)} %collective-permute-done.26.refs_17_.refs_11_), channel_id=1, source_target_pairs={{2,0},{3,1},{4,2},{5,3},{6,4},{7,5},{10,8},{11,9},{12,10},{13,11},... | collective-permute-start | bytes 3932168 | tf_op jit(solution)/shard_map/ppermute | solution.py:397
  141.7 103.6 %collective-permute-start.22 = (f32[40,128,128]{2,1,0:T(8,128)}, f32[40,128,128]{2,1,0:T(8,128)}, u32[]{:S(2)}, u32[]{:S(2)}) collective-permute-start(f32[40,128,128]{2,1,0:T(8,128)} %collective-permute-done.16.refs_2_), channel_id=1, source_target_pairs={{8,0},{24,8},{16,24},{0,16},{9,1},{25,9},{17,25},{1,17},{10,2},{26... | collective-permute-start | bytes 7864328 | tf_op jit(solution)/shard_map/ppermute | solution.py:403
  161.8 71.2 %collective-permute-start.6 = (f32[24,128,128]{2,1,0:T(8,128)}, f32[24,128,128]{2,1,0:T(8,128)}, u32[]{:S(2)}, u32[]{:S(2)}) collective-permute-start(f32[24,128,128]{2,1,0:T(8,128)} %collective-permute-done.2.refs_1_), channel_id=1, source_target_pairs={{8,0},{24,8},{16,24},{0,16},{9,1},{25,9},{17,25},{1,17},{10,2},{26... | collective-permute-start | bytes 4718600 | tf_op jit(solution)/shard_map/ppermute | solution.py:403
  167.3 76.6 %collective-permute-start.21 = (f32[40,96,128]{2,1,0:T(8,128)}, f32[40,96,128]{2,1,0:T(8,128)}, u32[]{:S(2)}, u32[]{:S(2)}) collective-permute-start(f32[40,96,128]{2,1,0:T(8,128)} %collective-permute-done.18.refs_4_), channel_id=1, source_target_pairs={{0,8},{8,24},{24,16},{16,0},{1,9},{9,25},{25,17},{17,1},{2,10},{10... | collective-permute-start | bytes 5898248 | tf_op jit(solution)/shard_map/ppermute | solution.py:407
  188.3 50.7 %collective-permute-start.31 = (f32[40,64,128]{2,1,0:T(8,128)}, f32[40,64,128]{2,1,0:T(8,128)}, u32[]{:S(2)}, u32[]{:S(2)}) collective-permute-start(f32[40,64,128]{2,1,0:T(8,128)} %collective-permute-done.30.refs_18_.refs_12_), channel_id=1, source_target_pairs={{2,0},{3,1},{4,2},{5,3},{6,4},{7,5},{10,8},{11,9},{12,10},{13,11},... | collective-permute-start | bytes 3932168 | tf_op jit(solution)/shard_map/ppermute | solution.py:397
  194.7 47.8 %collective-permute-start.36 = (f32[40,64,128]{2,1,0:T(8,128)}, f32[40,64,128]{2,1,0:T(8,128)}, u32[]{:S(2)}, u32[]{:S(2)}) collective-permute-start(f32[40,64,128]{2,1,0:T(8,128)} %collective-permute-done.35.refs_12_.refs_6_), channel_id=1, source_target_pairs={{0,2},{1,3},{2,4},{3,5},{4,6},{5,7},{8,10},{9,11},{10,12},{11,13},... | collective-permute-start | bytes 3932168 | tf_op jit(solution)/shard_map/ppermute | solution.py:396
  233.0 33.7 %collective-permute-start.34 = (f32[40,64,128]{2,1,0:T(8,128)}, f32[40,64,128]{2,1,0:T(8,128)}, u32[]{:S(2)}, u32[]{:S(2)}) collective-permute-start(f32[40,64,128]{2,1,0:T(8,128)} %collective-permute-done.33.refs_13_.refs_7_), channel_id=1, source_target_pairs={{0,2},{1,3},{2,4},{3,5},{4,6},{5,7},{8,10},{9,11},{10,12},{11,13},... | collective-permute-start | bytes 3932168 | tf_op jit(solution)/shard_map/ppermute | solution.py:396
  239.0 57.9 %collective-permute-start.12 = (f32[2,24,64,128]{3,2,1,0:T(8,128)}, f32[2,24,64,128]{3,2,1,0:T(8,128)}, u32[]{:S(2)}, u32[]{:S(2)}) collective-permute-start(f32[2,24,64,128]{3,2,1,0:T(8,128)} %collective-permute-done.1.refs_7_.refs_9_), channel_id=1, source_target_pairs={{0,2},{1,3},{2,4},{3,5},{4,6},{5,7},{8,10},{9,11},{10,12},{11,13},... | collective-permute-start | bytes 4718600 | tf_op jit(solution)/shard_map/ppermute | solution.py:396
  242.4 70.6 %collective-permute-start.19 = (f32[40,128,128]{2,1,0:T(8,128)}, f32[40,128,128]{2,1,0:T(8,128)}, u32[]{:S(2)}, u32[]{:S(2)}) collective-permute-start(f32[40,128,128]{2,1,0:T(8,128)} %collective-permute-done.16.refs_2_), channel_id=1, source_target_pairs={{0,8},{8,24},{24,16},{16,0},{1,9},{9,25},{25,17},{17,1},{2,10},{10... | collective-permute-start | bytes 7864328 | tf_op jit(solution)/shard_map/ppermute | solution.py:402
  243.9 33.7 %collective-permute-start.28 = (f32[40,64,128]{2,1,0:T(8,128)}, f32[40,64,128]{2,1,0:T(8,128)S(1)}, u32[]{:S(2)}, u32[]{:S(2)}) collective-permute-start(f32[40,64,128]{2,1,0:T(8,128)} %collective-permute-done.27.refs_15_.refs_9_), channel_id=1, source_target_pairs={{2,0},{3,1},{4,2},{5,3},{6,4},{7,5},{10,8},{11,9},{12,10},{13,11},... | collective-permute-start | bytes 3932168 | tf_op jit(solution)/shard_map/ppermute | solution.py:397
  245.2 95.2 %collective-permute-start.23 = (f32[40,128,128]{2,1,0:T(8,128)}, f32[40,128,128]{2,1,0:T(8,128)}, u32[]{:S(2)}, u32[]{:S(2)}) collective-permute-start(f32[40,128,128]{2,1,0:T(8,128)} %collective-permute-done.22.refs_8_.refs_11_), channel_id=1, source_target_pairs={{8,0},{24,8},{16,24},{0,16},{9,1},{25,9},{17,25},{1,17},{10,2},{26... | collective-permute-start | bytes 7864328 | tf_op jit(solution)/shard_map/ppermute | solution.py:408
  266.8 44.7 %collective-permute-start.10 = (f32[2,24,64,128]{3,2,1,0:T(8,128)}, f32[2,24,64,128]{3,2,1,0:T(8,128)}, u32[]{:S(2)}, u32[]{:S(2)}) collective-permute-start(f32[2,24,64,128]{3,2,1,0:T(8,128)} %collective-permute-done.9.refs_10_.refs_14_), channel_id=1, source_target_pairs={{2,0},{3,1},{4,2},{5,3},{6,4},{7,5},{10,8},{11,9},{12,10},{13,11},... | collective-permute-start | bytes 4718600 | tf_op jit(solution)/shard_map/ppermute | solution.py:397
  277.7 57.8 %collective-permute-start.32 = (f32[40,64,128]{2,1,0:T(8,128)}, f32[40,64,128]{2,1,0:T(8,128)}, u32[]{:S(2)}, u32[]{:S(2)}) collective-permute-start(f32[40,64,128]{2,1,0:T(8,128)} %collective-permute-done.31.refs_16_.refs_10_), channel_id=1, source_target_pairs={{2,0},{3,1},{4,2},{5,3},{6,4},{7,5},{10,8},{11,9},{12,10},{13,11},... | collective-permute-start | bytes 3932168 | tf_op jit(solution)/shard_map/ppermute | solution.py:397
  296.9 39.1 %collective-permute-start.37 = (f32[40,64,128]{2,1,0:T(8,128)}, f32[40,64,128]{2,1,0:T(8,128)}, u32[]{:S(2)}, u32[]{:S(2)}) collective-permute-start(f32[40,64,128]{2,1,0:T(8,128)} %collective-permute-done.36.refs_14_.refs_8_), channel_id=1, source_target_pairs={{0,2},{1,3},{2,4},{3,5},{4,6},{5,7},{8,10},{9,11},{10,12},{11,13},... | collective-permute-start | bytes 3932168 | tf_op jit(solution)/shard_map/ppermute | solution.py:396
  311.5 78.9 %collective-permute-start.4 = (f32[24,128,128]{2,1,0:T(8,128)}, f32[24,128,128]{2,1,0:T(8,128)S(1)}, u32[]{:S(2)}, u32[]{:S(2)}) collective-permute-start(f32[24,128,128]{2,1,0:T(8,128)} %collective-permute-done.2.refs_1_), channel_id=1, source_target_pairs={{0,8},{8,24},{24,16},{16,0},{1,9},{9,25},{25,17},{17,1},{2,10},{10... | collective-permute-start | bytes 4718600 | tf_op jit(solution)/shard_map/ppermute | solution.py:402
  313.0 89.4 %collective-permute-start.5 = (f32[24,128,128]{2,1,0:T(8,128)}, f32[24,128,128]{2,1,0:T(8,128)}, u32[]{:S(2)}, u32[]{:S(2)}) collective-permute-start(f32[24,128,128]{2,1,0:T(8,128)} %collective-permute-done.3.refs_2_), channel_id=1, source_target_pairs={{0,8},{8,24},{24,16},{16,0},{1,9},{9,25},{25,17},{17,1},{2,10},{10... | collective-permute-start | bytes 4718600 | tf_op jit(solution)/shard_map/ppermute | solution.py:407
  335.4 67.0 %collective-permute-start.7 = (f32[24,128,128]{2,1,0:T(8,128)}, f32[24,128,128]{2,1,0:T(8,128)}, u32[]{:S(2)}, u32[]{:S(2)}) collective-permute-start(f32[24,128,128]{2,1,0:T(8,128)} %collective-permute-done.6.refs_5_.refs_7_), channel_id=1, source_target_pairs={{8,0},{24,8},{16,24},{0,16},{9,1},{25,9},{17,25},{1,17},{10,2},{26... | collective-permute-start | bytes 4718600 | tf_op jit(solution)/shard_map/ppermute | solution.py:408
  336.0 66.4 %collective-permute-start.13 = (f32[2,24,64,128]{3,2,1,0:T(8,128)}, f32[2,24,64,128]{3,2,1,0:T(8,128)}, u32[]{:S(2)}, u32[]{:S(2)}) collective-permute-start(f32[2,24,64,128]{3,2,1,0:T(8,128)} %collective-permute-done.12.refs_8_.refs_11_), channel_id=1, source_target_pairs={{0,2},{1,3},{2,4},{3,5},{4,6},{5,7},{8,10},{9,11},{10,12},{11,13},... | collective-permute-start | bytes 4718600 | tf_op jit(solution)/shard_map/ppermute | solution.py:396
  340.4 62.0 %collective-permute-start.11 = (f32[2,24,64,128]{3,2,1,0:T(8,128)}, f32[2,24,64,128]{3,2,1,0:T(8,128)}, u32[]{:S(2)}, u32[]{:S(2)}) collective-permute-start(f32[2,24,64,128]{3,2,1,0:T(8,128)} %collective-permute-done.10.refs_9_.refs_12_), channel_id=1, source_target_pairs={{2,0},{3,1},{4,2},{5,3},{6,4},{7,5},{10,8},{11,9},{12,10},{13,11},... | collective-permute-start | bytes 4718600 | tf_op jit(solution)/shard_map/ppermute | solution.py:397
  (21 other events, 652.9 us)

commit v6 on v4

--- a/solution.py
+++ b/solution.py
@@ -14,7 +14,8 @@
 NF = 64
 SPLIT = (0, 1)
 SHARES = (20, 12)
-GRANT = 50 << 20
+SMALL = 4 << 20
+GRANT = 46 << 20
 F32, BF16 = jnp.float32, jnp.bfloat16
 
 
@@ -234,8 +235,9 @@
             for h, x in enumerate(g[way, hop]):
                 g_keys.append((way, hop, h if len(g[way, hop]) == 2 else None))
                 operands.append(x)
+    small = 8 * n * rows * cols <= SMALL
     if so_far is not None:
-        operands.append(so_far)
+        operands.append(pltpu.with_memory_space_constraint(so_far, pltpu.VMEM) if small else so_far)
     first = levels + 3
 
     def spec(i, x):
@@ -249,7 +251,7 @@
         pltpu.VMEM((2, 3 * depth * (len(places) + 1), 2 * cols), BF16),
     ]
     if part == EARLY:
-        out = jax.ShapeDtypeStruct((n, 2 * rows, cols), F32)
+        out = (pltpu.VMEM if small else jax.ShapeDtypeStruct)((n, 2 * rows, cols), F32)
         out_specs = pl.BlockSpec((step, 2 * rows, cols), lambda i, c: (i, 0, 0))
     else:
         out = [jax.ShapeDtypeStruct((rows, n, cols), F32)] * 2
@@ -265,7 +267,7 @@
             scratch_shapes=scratch,
         ),
         out_shape=out,
-        compiler_params=pltpu.CompilerParams(vmem_limit_bytes=GRANT if part == LATE else None),
+        compiler_params=pltpu.CompilerParams(vmem_limit_bytes=GRANT if part == LATE and small else None),
         cost_estimate=pl.CostEstimate(
             flops=n // 2 * 2 * 4 * rows * 3 * len(places) * depth * 2 * cols,
             bytes_accessed=4 * sum(x.size for x in operands),
@@ -310,7 +312,7 @@
             out_specs=pl.BlockSpec((step, cols, NT), lambda i, c: (i, 0, 0)),
         ),
         out_shape=(pltpu.VMEM if so_far is None else jax.ShapeDtypeStruct)((rows, cols, NT), F32),
-        compiler_params=pltpu.CompilerParams(vmem_limit_bytes=GRANT - (12 << 20)),
+        compiler_params=pltpu.CompilerParams(vmem_limit_bytes=GRANT - (8 << 20)),
         cost_estimate=pl.CostEstimate(
             flops=12 * rows * cols * NT * NT, bytes_accessed=8 * rows * cols * NT, transcendentals=0
         ),
@@ -376,9 +378,7 @@
         d_own = [d_parts[c], d_swapped] if c else head + [d_parts[c], d_swapped]
         calls = (EARLY, LATE) if c in SPLIT else (ALL,)
         counts = {a: len(d_own) for a in range(around)}
-        plans = [numbers(part, me, counts, 1 if c else 2) for part in calls]
-        if c:
-            g_own = [jnp.stack(g_own)]
+        plans = [numbers(part, me, counts, 2) for part in calls]
         g = {("own", 0): g_own}
         up, down = g_own, g_own
         for s in range(1, levels):

time: 416 us -> 432 us (1.038)
  local copies, waits for them, and re-layouts: 5.87 us -> 12.3 us
  waiting for transfers between devices: 216 us -> 221 us
    ppermute x9 -> x12, waiting for transfers between devices: 97.6 us -> 175 us  [local(): down = [lax.ppermute(x, 'src', downward) for x in down]]
    ppermute x5, waiting for transfers between devices: 52.5 us -> 0.01 us  [local(): right = [lax.ppermute(x, 'freq', clockwise) for x in right]]
    ppermute x5, waiting for transfers between devices: 38.4 us -> 14.6 us  [local(): left = [lax.ppermute(x, 'freq', counter) for x in left]]
    unnamed x44 -> x60, local copies, waits for them, and re-layouts: 3.11 us -> 8.92 us
    ppermute x9 -> x12, waiting for transfers between devices: 27.1 us -> 31.1 us  [local(): up = [lax.ppermute(x, 'src', upward) for x in up]]
    ppermute x9 -> x12, starting transfers between devices: 11.6 us -> 15.4 us  [local(): down = [lax.ppermute(x, 'src', downward) for x in down]]
    ppermute x9 -> x12, starting transfers between devices: 46.8 us -> 49.8 us  [local(): up = [lax.ppermute(x, 'src', upward) for x in up]]
  transfers between devices with their start and end apart: 39 -> 45, of which waited for: 12 -> 18; matrix products, arithmetic and copies ran while one was open for 1% -> 1% of each run, Pallas kernels for 23% -> 23%
where the time goes in v6:
time: 432 us; the launch traced here: 429 us
  waiting for transfers between devices  221 us (51%)
  Pallas kernels  109 us (25%)
  starting transfers between devices  82.4 us (19%)
  local copies, waits for them, and re-layouts  12.3 us (3%)
  between operations  4.56 us (1%)
    ppermute x12, waiting for transfers between devices, local(): down = [lax.ppermute(x, 'src', downward) for x in down]  175 us
    pallas_call x4, Pallas kernels, product(): pl.pallas_call(functools.partial(product_kernel, part, levels, places, d_...  62.1 us
    ppermute x12, starting transfers between devices, local(): up = [lax.ppermute(x, 'src', upward) for x in up]  49.8 us
    pallas_call x5, Pallas kernels, forward(): pl.pallas_call(functools.partial(forward_kernel, counts), grid_spec=pltpu...  32.9 us
    ppermute x12, waiting for transfers between devices, local(): up = [lax.ppermute(x, 'src', upward) for x in up]  31.1 us
    ppermute x12, starting transfers between devices, local(): down = [lax.ppermute(x, 'src', downward) for x in down]  15.4 us
    ppermute x5, waiting for transfers between devices, local(): left = [lax.ppermute(x, 'freq', counter) for x in left]  14.6 us
    pallas_call x2, Pallas kernels, inverse(): pl.pallas_call(functools.partial(inverse_kernel, len(ms)), grid_spec=pltp...  13.8 us
  transfers between devices with their start and end apart: 45, of which 18 were waited for; matrix products, arithmetic and copies ran while one was open for 1% of the time, Pallas kernels for 23%

profile of v6, /device:TPU:0, one launch (start us, length us, event | category | flops | bytes accessed | tf_op | source)
XLA Modules:
  0.0 428.6 jit_solution(5269298398848299518)
XLA Ops:
  6.3 6.5 %forward.5 = (f32[24,64,128]{2,1,0:T(8,128)}, f32[40,64,128]{2,1,0:T(8,128)}, f32[24,64,128]{2,1,0:T(8,128)}) custom-call(s32[1]{0:T(128)} %bitcast.core_ref, bf16[2,176,256]{2,1,0:T(8,128)(2,1)} %constant.81.clone.w_ref, f32[64,128,128]{2,1,0:T(8,128)} %x_ref.7), custom_call_target="tpu_custom_call" | custom-call | flops 1610612736 | bytes 8388608 | tf_op jit(solution)/shard_map/forward/pallas_call | solution.py:85
  16.4 5.5 %forward.7.refs_9_.refs_12_ = f32[40,64,128]{2,1,0:T(8,128)} custom-call(s32[1]{0:T(128)} %bitcast.core_ref, bf16[2,80,256]{2,1,0:T(8,128)(2,1)} %constant.80.clone.w_ref, f32[64,128,128]{2,1,0:T(8,128)} %x_ref.7), custom_call_target="tpu_custom_call" | custom-call | flops 1610612736 | bytes 8388608 | tf_op jit(solution)/shard_map/forward/pallas_call | solution.py:85
  21.9 4.5 %collective-permute-start.21 = (f32[40,64,128]{2,1,0:T(8,128)}, f32[40,64,128]{2,1,0:T(8,128)}, u32[]{:S(2)}, u32[]{:S(2)}) collective-permute-start(f32[40,64,128]{2,1,0:T(8,128)} %forward.7.refs_9_.refs_12_), channel_id=1, source_target_pairs={{0,2},{1,3},{2,4},{3,5},{4,6},{5,7},{8,10},{9,11},{10,12},{11,13},... | collective-permute-start | bytes 3932168 | tf_op jit(solution)/shard_map/ppermute | solution.py:388
  28.3 13.8 %collective-permute-done.30.refs_6_.refs_9_ = f32[40,32,128]{2,1,0:T(8,128)S(1)} collective-permute-done((f32[40,32,128]{2,1,0:T(8,128)S(1)}, f32[40,32,128]{2,1,0:T(8,128)S(1)}, u32[]{:S(2)}, u32[]{:S(2)}) %collective-permute-start.30) | collective-permute-done | bytes 655392 | tf_op jit(solution)/shard_map/ppermute | solution.py:395
  43.6 10.6 %forward.6 = (f32[24,128,128]{2,1,0:T(8,128)}, f32[40,128,128]{2,1,0:T(8,128)}, f32[24,128,128]{2,1,0:T(8,128)}) custom-call(s32[1]{0:T(128)} %bitcast.core_ref, bf16[2,176,256]{2,1,0:T(8,128)(2,1)} %constant.81.clone.w_ref, f32[128,128,128]{2,1,0:T(8,128)} %x_ref.9), custom_call_target="tpu_custom_call" | custom-call | flops 3221225472 | bytes 16777216 | tf_op jit(solution)/shard_map/forward/pallas_call | solution.py:85
  55.4 5.9 %collective-permute-done.21.refs_11_.refs_14_ = f32[40,64,128]{2,1,0:T(8,128)} collective-permute-done((f32[40,64,128]{2,1,0:T(8,128)}, f32[40,64,128]{2,1,0:T(8,128)}, u32[]{:S(2)}, u32[]{:S(2)}) %collective-permute-start.21) | collective-permute-done | bytes 1310752 | tf_op jit(solution)/shard_map/ppermute | solution.py:388
  63.2 7.0 %forward.9.refs_1_ = f32[40,96,128]{2,1,0:T(8,128)} custom-call(s32[1]{0:T(128)} %bitcast.core_ref, bf16[2,80,256]{2,1,0:T(8,128)(2,1)} %constant.80.clone.w_ref, f32[128,128,128]{2,1,0:T(8,128)} %x_ref.9), custom_call_target="tpu_custom_call" | custom-call | flops 2415919104 | bytes 12582912 | tf_op jit(solution)/shard_map/forward/pallas_call | solution.py:85
  70.2 23.6 %collective-permute-done.34.refs_17_.refs_24_ = f32[40,64,128]{2,1,0:T(8,128)} collective-permute-done((f32[40,64,128]{2,1,0:T(8,128)}, f32[40,64,128]{2,1,0:T(8,128)}, u32[]{:S(2)}, u32[]{:S(2)}) %collective-permute-start.34) | collective-permute-done | bytes 1310752 | tf_op jit(solution)/shard_map/ppermute | solution.py:389
  95.4 3.7 collective-permute-start.9
  106.3 6.9 %collective-permute-done.9.refs_9_.refs_11_ = f32[24,64,128]{2,1,0:T(8,128)S(1)} collective-permute-done((f32[24,64,128]{2,1,0:T(8,128)S(1)}, f32[24,64,128]{2,1,0:T(8,128)S(1)}, u32[]{:S(2)}, u32[]{:S(2)}) %collective-permute-start.9) | collective-permute-done | bytes 786464 | tf_op jit(solution)/shard_map/ppermute | solution.py:388
  115.3 5.5 %collective-permute-done.11.refs_12_.refs_16_ = f32[24,64,128]{2,1,0:T(8,128)S(1)} collective-permute-done((f32[24,64,128]{2,1,0:T(8,128)}, f32[24,64,128]{2,1,0:T(8,128)S(1)}, u32[]{:S(2)}, u32[]{:S(2)}) %collective-permute-start.11) | collective-permute-done | bytes 786464 | tf_op jit(solution)/shard_map/ppermute | solution.py:389
  120.9 4.1 collective-permute-start.16
  124.9 9.9 %collective-permute-done.13.refs_15_.refs_21_ = f32[24,64,128]{2,1,0:T(8,128)} collective-permute-done((f32[24,64,128]{2,1,0:T(8,128)S(1)}, f32[24,64,128]{2,1,0:T(8,128)}, u32[]{:S(2)}, u32[]{:S(2)}) %collective-permute-start.13) | collective-permute-done | bytes 786464 | tf_op jit(solution)/shard_map/ppermute | solution.py:389
  143.9 17.0 %collective-permute-done.12.refs_12_ = f32[24,64,128]{2,1,0:T(8,128)S(1)} collective-permute-done((f32[24,64,128]{2,1,0:T(8,128)}, f32[24,64,128]{2,1,0:T(8,128)S(1)}, u32[]{:S(2)}, u32[]{:S(2)}) %collective-permute-start.12) | collective-permute-done | bytes 786464 | tf_op jit(solution)/shard_map/ppermute | solution.py:389
  163.3 38.8 %collective-permute-done.14.refs_13_.refs_17_ = f32[24,64,128]{2,1,0:T(8,128)} collective-permute-done((f32[24,64,128]{2,1,0:T(8,128)}, f32[24,64,128]{2,1,0:T(8,128)}, u32[]{:S(2)}, u32[]{:S(2)}) %collective-permute-start.14) | collective-permute-done | bytes 786464 | tf_op jit(solution)/shard_map/ppermute | solution.py:389
  205.3 4.6 %collective-permute-start.40 = (f32[40,64,128]{2,1,0:T(8,128)}, f32[40,64,128]{2,1,0:T(8,128)S(1)}, u32[]{:S(2)}, u32[]{:S(2)}) collective-permute-start(f32[40,64,128]{2,1,0:T(8,128)} %collective-permute-done.21.refs_11_.refs_14_), channel_id=1, source_target_pairs={{0,2},{1,3},{2,4},{3,5},{4,6},{5,7},{8,10},{9,11},{10,12},{11,13},... | collective-permute-start | bytes 3932168 | tf_op jit(solution)/shard_map/ppermute | solution.py:388
  209.9 21.3 %collective-permute-done.37.refs_18_.refs_25_ = f32[40,64,128]{2,1,0:T(8,128)} collective-permute-done((f32[40,64,128]{2,1,0:T(8,128)}, f32[40,64,128]{2,1,0:T(8,128)}, u32[]{:S(2)}, u32[]{:S(2)}) %collective-permute-start.37) | collective-permute-done | bytes 1310752 | tf_op jit(solution)/shard_map/ppermute | solution.py:389
  237.6 5.0 %collective-permute-start.41 = (f32[40,64,128]{2,1,0:T(8,128)S(1)}, f32[40,64,128]{2,1,0:T(8,128)S(1)}, u32[]{:S(2)}, u32[]{:S(2)}) collective-permute-start(f32[40,64,128]{2,1,0:T(8,128)S(1)} %collective-permute-done.33.refs_12_.refs_15_), channel_id=1, source_target_pairs={{0,2},{1,3},{2,4},{3,5},{4,6},{5,7},{8,10},{9,11},{10,12},{11,13},... | collective-permute-start | bytes 3932168 | tf_op jit(solution)/shard_map/ppermute | solution.py:388
  243.3 21.7 %collective-permute-done.36.refs_16_ = f32[40,64,128]{2,1,0:T(8,128)S(1)} collective-permute-done((f32[40,64,128]{2,1,0:T(8,128)}, f32[40,64,128]{2,1,0:T(8,128)S(1)}, u32[]{:S(2)}, u32[]{:S(2)}) %collective-permute-start.36) | collective-permute-done | bytes 1310752 | tf_op jit(solution)/shard_map/ppermute | solution.py:389
  267.5 20.8 %collective-permute-done.38.refs_16_.refs_21_ = f32[40,64,128]{2,1,0:T(8,128)S(1)} collective-permute-done((f32[40,64,128]{2,1,0:T(8,128)}, f32[40,64,128]{2,1,0:T(8,128)S(1)}, u32[]{:S(2)}, u32[]{:S(2)}) %collective-permute-start.38) | collective-permute-done | bytes 1310752 | tf_op jit(solution)/shard_map/ppermute | solution.py:389
  289.7 4.6 %collective-permute-start.43 = (f32[40,64,128]{2,1,0:T(8,128)S(1)}, f32[40,64,128]{2,1,0:T(8,128)S(1)}, u32[]{:S(2)}, u32[]{:S(2)}) collective-permute-start(f32[40,64,128]{2,1,0:T(8,128)S(1)} %collective-permute-done.41.refs_14_.refs_19_), channel_id=1, source_target_pairs={{0,2},{1,3},{2,4},{3,5},{4,6},{5,7},{8,10},{9,11},{10,12},{11,13},... | collective-permute-start | bytes 3932168 | tf_op jit(solution)/shard_map/ppermute | solution.py:388
  294.3 5.4 %collective-permute-done.42.refs_22_ = f32[40,64,128]{2,1,0:T(8,128)S(1)} collective-permute-done((f32[40,64,128]{2,1,0:T(8,128)S(1)}, f32[40,64,128]{2,1,0:T(8,128)S(1)}, u32[]{:S(2)}, u32[]{:S(2)}) %collective-permute-start.42) | collective-permute-done | bytes 1310752 | tf_op jit(solution)/shard_map/ppermute | solution.py:388
  302.9 12.7 %collective-permute-done.39.refs_17_ = f32[40,64,128]{2,1,0:T(8,128)S(1)} collective-permute-done((f32[40,64,128]{2,1,0:T(8,128)S(1)}, f32[40,64,128]{2,1,0:T(8,128)S(1)}, u32[]{:S(2)}, u32[]{:S(2)}) %collective-permute-start.39) | collective-permute-done | bytes 1310752 | tf_op jit(solution)/shard_map/ppermute | solution.py:389
  319.0 8.9 %collective-permute-done.43.refs_23_ = f32[40,64,128]{2,1,0:T(8,128)S(1)} collective-permute-done((f32[40,64,128]{2,1,0:T(8,128)S(1)}, f32[40,64,128]{2,1,0:T(8,128)S(1)}, u32[]{:S(2)}, u32[]{:S(2)}) %collective-permute-start.43) | collective-permute-done | bytes 1310752 | tf_op jit(solution)/shard_map/ppermute | solution.py:388
  327.9 4.4 %collective-permute-start.18 = (f32[24,64,128]{2,1,0:T(8,128)}, f32[24,64,128]{2,1,0:T(8,128)S(1)}, u32[]{:S(2)}, u32[]{:S(2)}) collective-permute-start(f32[24,64,128]{2,1,0:T(8,128)} %collective-permute-done.16.refs_10_.refs_14_), channel_id=1, source_target_pairs={{0,2},{1,3},{2,4},{3,5},{4,6},{5,7},{8,10},{9,11},{10,12},{11,13},... | collective-permute-start | bytes 2359304 | tf_op jit(solution)/shard_map/ppermute | solution.py:388
  332.7 17.8 %shard_map.102.refs_26_ = f32[40,256,128]{2,1,0:T(8,128)} custom-call(s32[27]{0:T(128)} %concatenate.14.slot_ref, f32[40,32,128]{2,1,0:T(8,128)} %forward.8.refs_0_, f32[40,96,128]{2,1,0:T(8,128)} %forward.9.refs_1_, f32[40,128,128]{2,1,0:T(8,128)} %collective-permute-done.22.refs_2_, f32[40,32,128]{2,1,0:T(8,128)} %collective-permute-done.23.refs_3_, ...), custom_call_target="tpu_custom_call" | custom-call | flops 6039797760 | bytes 28835840 | tf_op jit(solution)/shard_map/pallas_call | solution.py:260
  350.6 20.7 %shard_map.103 = (f32[128,40,128]{2,1,0:T(8,128)}, f32[128,40,128]{2,1,0:T(8,128)}) custom-call(s32[34]{0:T(128)} %concatenate.15.slot_ref, f32[40,32,128]{2,1,0:T(8,128)} %forward.8.refs_0_, f32[40,96,128]{2,1,0:T(8,128)} %forward.9.refs_1_, f32[40,128,128]{2,1,0:T(8,128)} %collective-permute-done.22.refs_2_, ...), custom_call_target="tpu_custom_call" | custom-call | flops 4026531840 | bytes 44564480 | tf_op jit(solution)/shard_map/pallas_call | solution.py:260
  373.9 5.8 %collective-permute-start.19 = (f32[24,64,128]{2,1,0:T(8,128)}, f32[24,64,128]{2,1,0:T(8,128)}, u32[]{:S(2)}, u32[]{:S(2)}) collective-permute-start(f32[24,64,128]{2,1,0:T(8,128)} %collective-permute-done.17.refs_11_.refs_15_), channel_id=1, source_target_pairs={{0,2},{1,3},{2,4},{3,5},{4,6},{5,7},{8,10},{9,11},{10,12},{11,13},... | collective-permute-start | bytes 2359304 | tf_op jit(solution)/shard_map/ppermute | solution.py:388
  379.7 11.1 %shard_map.100.refs_22_ = f32[24,256,128]{2,1,0:T(8,128)S(1)} custom-call(s32[24]{0:T(128)} %concatenate.12.slot_ref, f32[24,128,128]{2,1,0:T(8,128)} %get-tuple-element.23.refs_0_, f32[24,128,128]{2,1,0:T(8,128)} %collective-permute-done.1.refs_1_, f32[24,128,128]{2,1,0:T(8,128)} %collective-permute-done.2.refs_2_, f32[24,128,128]{2,1,0:T(8,128)} %copy-done.16, ...), custom_call_target="tpu_custom_call" | custom-call | flops 3623878656 | bytes 17301504 | tf_op jit(solution)/shard_map/pallas_call | solution.py:260
  402.2 12.4 %shard_map.101 = (f32[128,24,128]{2,1,0:T(8,128)}, f32[128,24,128]{2,1,0:T(8,128)}) custom-call(s32[30]{0:T(128)S(1)} %concatenate.13.slot_ref, f32[24,128,128]{2,1,0:T(8,128)} %get-tuple-element.23.refs_0_, f32[24,128,128]{2,1,0:T(8,128)} %collective-permute-done.1.refs_1_, f32[24,128,128]{2,1,0:T(8,128)} %collective-permute-done.2.refs_2_, ...), custom_call_target="tpu_custom_call" | custom-call | flops 2415919104 | bytes 26738688 | tf_op jit(solution)/shard_map/pallas_call | solution.py:260
  414.8 7.0 %inverse.2.refs_2_ = f32[128,128,128]{2,1,0:T(8,128)S(1)} custom-call(s32[1]{0:T(128)} %bitcast.core_ref, bf16[2,160,256]{2,1,0:T(8,128)(2,1)S(1)} %copy-done.12, f32[128,40,128]{2,1,0:T(8,128)S(1)} %copy-done.8, f32[128,40,128]{2,1,0:T(8,128)} %collective-permute-done.44.refs_1_), custom_call_target="tpu_custom_call" | custom-call | flops 3221225472 | bytes 16777216 | tf_op jit(solution)/shard_map/inverse/pallas_call | solution.py:305
  421.8 6.7 %inverse.3 = f32[128,128,128]{2,1,0:T(8,128)} custom-call(s32[1]{0:T(128)} %bitcast.core_ref, bf16[2,96,256]{2,1,0:T(8,128)(2,1)S(1)} %copy-done.13, f32[128,24,128]{2,1,0:T(8,128)S(1)} %copy-done.9, f32[128,24,128]{2,1,0:T(8,128)S(1)} %collective-permute-done.20.refs_1_, f32[128,128,128]{2,1,0:T(8,128)S(1)} %inverse.2.refs_2_), custom_call_target="tpu_custom_call" | custom-call | flops 3221225472 | bytes 16777216 | tf_op jit(solution)/shard_map/inverse/pallas_call | solution.py:305
  (141 shorter events, 69.5 us)
Async XLA Ops:
  12.8 30.8 %collective-permute-start = (f32[24,64,128]{2,1,0:T(8,128)}, f32[24,64,128]{2,1,0:T(8,128)S(1)}, u32[]{:S(2)}, u32[]{:S(2)}) collective-permute-start(f32[24,64,128]{2,1,0:T(8,128)} %get-tuple-element.21.refs_6_.refs_8_), channel_id=1, source_target_pairs={{0,2},{1,3},{2,4},{3,5},{4,6},{5,7},{8,10},{9,11},{10,12},{11,13},... | collective-permute-start | bytes 2359304 | tf_op jit(solution)/shard_map/ppermute | solution.py:388
  21.9 39.4 %collective-permute-start.21 = (f32[40,64,128]{2,1,0:T(8,128)}, f32[40,64,128]{2,1,0:T(8,128)}, u32[]{:S(2)}, u32[]{:S(2)}) collective-permute-start(f32[40,64,128]{2,1,0:T(8,128)} %forward.7.refs_9_.refs_12_), channel_id=1, source_target_pairs={{0,2},{1,3},{2,4},{3,5},{4,6},{5,7},{8,10},{9,11},{10,12},{11,13},... | collective-permute-start | bytes 3932168 | tf_op jit(solution)/shard_map/ppermute | solution.py:388
  26.9 27.3 %collective-permute-start.8 = (f32[24,64,128]{2,1,0:T(8,128)}, f32[24,64,128]{2,1,0:T(8,128)S(1)}, u32[]{:S(2)}, u32[]{:S(2)}) collective-permute-start(f32[24,64,128]{2,1,0:T(8,128)} %get-tuple-element.25), channel_id=1, source_target_pairs={{0,1},{1,0},{2,3},{3,2},{4,5},{5,4},{6,7},{7,6},{8,9},{9,8},{10,11... | collective-permute-start | bytes 2359304 | tf_op jit(solution)/shard_map/ppermute | solution.py:376
  27.0 27.6 %collective-permute-start.10 = (f32[24,64,128]{2,1,0:T(8,128)S(1)}, f32[24,64,128]{2,1,0:T(8,128)}, u32[]{:S(2)}, u32[]{:S(2)}) collective-permute-start(f32[24,64,128]{2,1,0:T(8,128)S(1)} %copy-done), channel_id=1, source_target_pairs={{2,0},{3,1},{4,2},{5,3},{6,4},{7,5},{10,8},{11,9},{12,10},{13,11},... | collective-permute-start | bytes 2359304 | tf_op jit(solution)/shard_map/ppermute | solution.py:389
  54.2 41.1 %collective-permute-start.1 = (f32[24,128,128]{2,1,0:T(8,128)}, f32[24,128,128]{2,1,0:T(8,128)}, u32[]{:S(2)}, u32[]{:S(2)}) collective-permute-start(f32[24,128,128]{2,1,0:T(8,128)} %get-tuple-element.24), channel_id=1, source_target_pairs={{0,1},{1,0},{2,3},{3,2},{4,5},{5,4},{6,7},{7,6},{8,9},{9,8},{10,11... | collective-permute-start | bytes 4718600 | tf_op jit(solution)/shard_map/ppermute | solution.py:377
  54.6 44.5 %collective-permute-start.2 = (f32[24,128,128]{2,1,0:T(8,128)}, f32[24,128,128]{2,1,0:T(8,128)}, u32[]{:S(2)}, u32[]{:S(2)}) collective-permute-start(f32[24,128,128]{2,1,0:T(8,128)} %get-tuple-element.23.refs_0_), channel_id=1, source_target_pairs={{0,8},{8,24},{24,16},{16,0},{1,9},{9,25},{25,17},{17,1},{2,10},{10... | collective-permute-start | bytes 4718600 | tf_op jit(solution)/shard_map/ppermute | solution.py:394
  61.3 38.4 %collective-permute-start.7 = (f32[24,128,128]{2,1,0:T(8,128)}, f32[24,128,128]{2,1,0:T(8,128)}, u32[]{:S(2)}, u32[]{:S(2)}) collective-permute-start(f32[24,128,128]{2,1,0:T(8,128)} %get-tuple-element.23.refs_0_), channel_id=1, source_target_pairs={{8,0},{24,8},{16,24},{0,16},{9,1},{25,9},{17,25},{1,17},{10,2},{26... | collective-permute-start | bytes 4718600 | tf_op jit(solution)/shard_map/ppermute | solution.py:395
  61.8 32.0 %collective-permute-start.34 = (f32[40,64,128]{2,1,0:T(8,128)}, f32[40,64,128]{2,1,0:T(8,128)}, u32[]{:S(2)}, u32[]{:S(2)}) collective-permute-start(f32[40,64,128]{2,1,0:T(8,128)} %forward.7.refs_9_.refs_12_), channel_id=1, source_target_pairs={{2,0},{3,1},{4,2},{5,3},{6,4},{7,5},{10,8},{11,9},{12,10},{13,11},... | collective-permute-start | bytes 3932168 | tf_op jit(solution)/shard_map/ppermute | solution.py:389
  63.1 77.9 %collective-permute-start.22 = (f32[40,128,128]{2,1,0:T(8,128)}, f32[40,128,128]{2,1,0:T(8,128)}, u32[]{:S(2)}, u32[]{:S(2)}) collective-permute-start(f32[40,128,128]{2,1,0:T(8,128)} %get-tuple-element.31), channel_id=1, source_target_pairs={{0,1},{1,0},{2,3},{3,2},{4,5},{5,4},{6,7},{7,6},{8,9},{9,8},{10,11... | collective-permute-start | bytes 7864328 | tf_op jit(solution)/shard_map/ppermute | solution.py:377
  93.9 45.8 %collective-permute-start.24 = (f32[40,96,128]{2,1,0:T(8,128)}, f32[40,96,128]{2,1,0:T(8,128)}, u32[]{:S(2)}, u32[]{:S(2)}) collective-permute-start(f32[40,96,128]{2,1,0:T(8,128)} %forward.9.refs_1_), channel_id=1, source_target_pairs={{0,8},{8,24},{24,16},{16,0},{1,9},{9,25},{25,17},{17,1},{2,10},{10... | collective-permute-start | bytes 5898248 | tf_op jit(solution)/shard_map/ppermute | solution.py:394
  99.1 43.5 %collective-permute-start.31 = (f32[40,96,128]{2,1,0:T(8,128)}, f32[40,96,128]{2,1,0:T(8,128)}, u32[]{:S(2)}, u32[]{:S(2)}) collective-permute-start(f32[40,96,128]{2,1,0:T(8,128)} %forward.9.refs_1_), channel_id=1, source_target_pairs={{8,0},{24,8},{16,24},{0,16},{9,1},{25,9},{17,25},{1,17},{10,2},{26... | collective-permute-start | bytes 5898248 | tf_op jit(solution)/shard_map/ppermute | solution.py:395
  134.9 68.5 %collective-permute-start.33 = (f32[40,64,128]{2,1,0:T(8,128)}, f32[40,64,128]{2,1,0:T(8,128)S(1)}, u32[]{:S(2)}, u32[]{:S(2)}) collective-permute-start(f32[40,64,128]{2,1,0:T(8,128)} %collective-permute-done.32.refs_10_.refs_13_), channel_id=1, source_target_pairs={{0,2},{1,3},{2,4},{3,5},{4,6},{5,7},{8,10},{9,11},{10,12},{11,13},... | collective-permute-start | bytes 3932168 | tf_op jit(solution)/shard_map/ppermute | solution.py:388
  139.7 65.6 %collective-permute-start.35 = (f32[40,64,128]{2,1,0:T(8,128)}, f32[40,64,128]{2,1,0:T(8,128)}, u32[]{:S(2)}, u32[]{:S(2)}) collective-permute-start(f32[40,64,128]{2,1,0:T(8,128)} %collective-permute-done.34.refs_17_.refs_24_), channel_id=1, source_target_pairs={{2,0},{3,1},{4,2},{5,3},{6,4},{7,5},{10,8},{11,9},{12,10},{13,11},... | collective-permute-start | bytes 3932168 | tf_op jit(solution)/shard_map/ppermute | solution.py:389
  141.0 101.6 %collective-permute-start.28 = (f32[40,128,128]{2,1,0:T(8,128)}, f32[40,128,128]{2,1,0:T(8,128)}, u32[]{:S(2)}, u32[]{:S(2)}) collective-permute-start(f32[40,128,128]{2,1,0:T(8,128)} %collective-permute-done.22.refs_2_), channel_id=1, source_target_pairs={{8,0},{24,8},{16,24},{0,16},{9,1},{25,9},{17,25},{1,17},{10,2},{26... | collective-permute-start | bytes 7864328 | tf_op jit(solution)/shard_map/ppermute | solution.py:395
  142.6 59.5 %collective-permute-start.14 = (f32[24,64,128]{2,1,0:T(8,128)}, f32[24,64,128]{2,1,0:T(8,128)}, u32[]{:S(2)}, u32[]{:S(2)}) collective-permute-start(f32[24,64,128]{2,1,0:T(8,128)} %collective-permute-done.13.refs_15_.refs_21_), channel_id=1, source_target_pairs={{2,0},{3,1},{4,2},{5,3},{6,4},{7,5},{10,8},{11,9},{12,10},{13,11},... | collective-permute-start | bytes 2359304 | tf_op jit(solution)/shard_map/ppermute | solution.py:389
  161.8 75.8 %collective-permute-start.27 = (f32[40,96,128]{2,1,0:T(8,128)}, f32[40,96,128]{2,1,0:T(8,128)}, u32[]{:S(2)}, u32[]{:S(2)}) collective-permute-start(f32[40,96,128]{2,1,0:T(8,128)} %collective-permute-done.24.refs_4_), channel_id=1, source_target_pairs={{0,8},{8,24},{24,16},{16,0},{1,9},{9,25},{25,17},{17,1},{2,10},{10... | collective-permute-start | bytes 5898248 | tf_op jit(solution)/shard_map/ppermute | solution.py:399
  202.1 29.1 %collective-permute-start.37 = (f32[40,64,128]{2,1,0:T(8,128)}, f32[40,64,128]{2,1,0:T(8,128)}, u32[]{:S(2)}, u32[]{:S(2)}) collective-permute-start(f32[40,64,128]{2,1,0:T(8,128)} %collective-permute-done.32.refs_10_.refs_13_), channel_id=1, source_target_pairs={{2,0},{3,1},{4,2},{5,3},{6,4},{7,5},{10,8},{11,9},{12,10},{13,11},... | collective-permute-start | bytes 3932168 | tf_op jit(solution)/shard_map/ppermute | solution.py:389
  203.4 32.9 %collective-permute-start.5 = (f32[24,128,128]{2,1,0:T(8,128)}, f32[24,128,128]{2,1,0:T(8,128)}, u32[]{:S(2)}, u32[]{:S(2)}) collective-permute-start(f32[24,128,128]{2,1,0:T(8,128)} %collective-permute-done.1.refs_1_), channel_id=1, source_target_pairs={{8,0},{24,8},{16,24},{0,16},{9,1},{25,9},{17,25},{1,17},{10,2},{26... | collective-permute-start | bytes 4718600 | tf_op jit(solution)/shard_map/ppermute | solution.py:395
  205.3 28.8 %collective-permute-start.40 = (f32[40,64,128]{2,1,0:T(8,128)}, f32[40,64,128]{2,1,0:T(8,128)S(1)}, u32[]{:S(2)}, u32[]{:S(2)}) collective-permute-start(f32[40,64,128]{2,1,0:T(8,128)} %collective-permute-done.21.refs_11_.refs_14_), channel_id=1, source_target_pairs={{0,2},{1,3},{2,4},{3,5},{4,6},{5,7},{8,10},{9,11},{10,12},{11,13},... | collective-permute-start | bytes 3932168 | tf_op jit(solution)/shard_map/ppermute | solution.py:388
  231.2 33.7 %collective-permute-start.36 = (f32[40,64,128]{2,1,0:T(8,128)}, f32[40,64,128]{2,1,0:T(8,128)S(1)}, u32[]{:S(2)}, u32[]{:S(2)}) collective-permute-start(f32[40,64,128]{2,1,0:T(8,128)} %collective-permute-done.35.refs_15_.refs_20_), channel_id=1, source_target_pairs={{2,0},{3,1},{4,2},{5,3},{6,4},{7,5},{10,8},{11,9},{12,10},{13,11},... | collective-permute-start | bytes 3932168 | tf_op jit(solution)/shard_map/ppermute | solution.py:389
  234.1 67.2 %collective-permute-start.25 = (f32[40,128,128]{2,1,0:T(8,128)}, f32[40,128,128]{2,1,0:T(8,128)S(1)}, u32[]{:S(2)}, u32[]{:S(2)}) collective-permute-start(f32[40,128,128]{2,1,0:T(8,128)} %collective-permute-done.22.refs_2_), channel_id=1, source_target_pairs={{0,8},{8,24},{24,16},{16,0},{1,9},{9,25},{25,17},{17,1},{2,10},{10... | collective-permute-start | bytes 7864328 | tf_op jit(solution)/shard_map/ppermute | solution.py:394
  236.3 52.0 %collective-permute-start.38 = (f32[40,64,128]{2,1,0:T(8,128)}, f32[40,64,128]{2,1,0:T(8,128)S(1)}, u32[]{:S(2)}, u32[]{:S(2)}) collective-permute-start(f32[40,64,128]{2,1,0:T(8,128)} %collective-permute-done.37.refs_18_.refs_25_), channel_id=1, source_target_pairs={{2,0},{3,1},{4,2},{5,3},{6,4},{7,5},{10,8},{11,9},{12,10},{13,11},... | collective-permute-start | bytes 3932168 | tf_op jit(solution)/shard_map/ppermute | solution.py:389
  237.6 52.0 %collective-permute-start.41 = (f32[40,64,128]{2,1,0:T(8,128)S(1)}, f32[40,64,128]{2,1,0:T(8,128)S(1)}, u32[]{:S(2)}, u32[]{:S(2)}) collective-permute-start(f32[40,64,128]{2,1,0:T(8,128)S(1)} %collective-permute-done.33.refs_12_.refs_15_), channel_id=1, source_target_pairs={{0,2},{1,3},{2,4},{3,5},{4,6},{5,7},{8,10},{9,11},{10,12},{11,13},... | collective-permute-start | bytes 3932168 | tf_op jit(solution)/shard_map/ppermute | solution.py:388
  242.6 89.7 %collective-permute-start.29 = (f32[40,128,128]{2,1,0:T(8,128)}, f32[40,128,128]{2,1,0:T(8,128)}, u32[]{:S(2)}, u32[]{:S(2)}) collective-permute-start(f32[40,128,128]{2,1,0:T(8,128)} %collective-permute-done.28.refs_8_.refs_11_), channel_id=1, source_target_pairs={{8,0},{24,8},{16,24},{0,16},{9,1},{25,9},{17,25},{1,17},{10,2},{26... | collective-permute-start | bytes 7864328 | tf_op jit(solution)/shard_map/ppermute | solution.py:400
  265.0 34.8 %collective-permute-start.42 = (f32[40,64,128]{2,1,0:T(8,128)S(1)}, f32[40,64,128]{2,1,0:T(8,128)S(1)}, u32[]{:S(2)}, u32[]{:S(2)}) collective-permute-start(f32[40,64,128]{2,1,0:T(8,128)S(1)} %collective-permute-done.40.refs_13_.refs_18_), channel_id=1, source_target_pairs={{0,2},{1,3},{2,4},{3,5},{4,6},{5,7},{8,10},{9,11},{10,12},{11,13},... | collective-permute-start | bytes 3932168 | tf_op jit(solution)/shard_map/ppermute | solution.py:388
  289.7 38.2 %collective-permute-start.43 = (f32[40,64,128]{2,1,0:T(8,128)S(1)}, f32[40,64,128]{2,1,0:T(8,128)S(1)}, u32[]{:S(2)}, u32[]{:S(2)}) collective-permute-start(f32[40,64,128]{2,1,0:T(8,128)S(1)} %collective-permute-done.41.refs_14_.refs_19_), channel_id=1, source_target_pairs={{0,2},{1,3},{2,4},{3,5},{4,6},{5,7},{8,10},{9,11},{10,12},{11,13},... | collective-permute-start | bytes 3932168 | tf_op jit(solution)/shard_map/ppermute | solution.py:388
  299.8 72.9 %collective-permute-start.3 = (f32[24,128,128]{2,1,0:T(8,128)}, f32[24,128,128]{2,1,0:T(8,128)S(1)}, u32[]{:S(2)}, u32[]{:S(2)}) collective-permute-start(f32[24,128,128]{2,1,0:T(8,128)} %collective-permute-done.1.refs_1_), channel_id=1, source_target_pairs={{0,8},{8,24},{24,16},{16,0},{1,9},{9,25},{25,17},{17,1},{2,10},{10... | collective-permute-start | bytes 4718600 | tf_op jit(solution)/shard_map/ppermute | solution.py:394
  301.3 89.4 %collective-permute-start.4 = (f32[24,128,128]{2,1,0:T(8,128)}, f32[24,128,128]{2,1,0:T(8,128)}, u32[]{:S(2)}, u32[]{:S(2)}) collective-permute-start(f32[24,128,128]{2,1,0:T(8,128)} %collective-permute-done.2.refs_2_), channel_id=1, source_target_pairs={{0,8},{8,24},{24,16},{16,0},{1,9},{9,25},{25,17},{17,1},{2,10},{10... | collective-permute-start | bytes 4718600 | tf_op jit(solution)/shard_map/ppermute | solution.py:399
  315.6 55.7 %collective-permute-start.17 = (f32[24,64,128]{2,1,0:T(8,128)S(1)}, f32[24,64,128]{2,1,0:T(8,128)}, u32[]{:S(2)}, u32[]{:S(2)}) collective-permute-start(f32[24,64,128]{2,1,0:T(8,128)S(1)} %collective-permute-done.9.refs_9_.refs_11_), channel_id=1, source_target_pairs={{0,2},{1,3},{2,4},{3,5},{4,6},{5,7},{8,10},{9,11},{10,12},{11,13},... | collective-permute-start | bytes 2359304 | tf_op jit(solution)/shard_map/ppermute | solution.py:388
  327.9 43.5 %collective-permute-start.18 = (f32[24,64,128]{2,1,0:T(8,128)}, f32[24,64,128]{2,1,0:T(8,128)S(1)}, u32[]{:S(2)}, u32[]{:S(2)}) collective-permute-start(f32[24,64,128]{2,1,0:T(8,128)} %collective-permute-done.16.refs_10_.refs_14_), channel_id=1, source_target_pairs={{0,2},{1,3},{2,4},{3,5},{4,6},{5,7},{8,10},{9,11},{10,12},{11,13},... | collective-permute-start | bytes 2359304 | tf_op jit(solution)/shard_map/ppermute | solution.py:388
  332.3 64.2 %collective-permute-start.6 = (f32[24,128,128]{2,1,0:T(8,128)}, f32[24,128,128]{2,1,0:T(8,128)}, u32[]{:S(2)}, u32[]{:S(2)}) collective-permute-start(f32[24,128,128]{2,1,0:T(8,128)} %collective-permute-done.5.refs_5_.refs_7_), channel_id=1, source_target_pairs={{8,0},{24,8},{16,24},{0,16},{9,1},{25,9},{17,25},{1,17},{10,2},{26... | collective-permute-start | bytes 4718600 | tf_op jit(solution)/shard_map/ppermute | solution.py:400
  371.3 43.4 %collective-permute-start.44 = (f32[128,40,128]{2,1,0:T(8,128)}, f32[128,40,128]{2,1,0:T(8,128)}, u32[]{:S(2)}, u32[]{:S(2)}) collective-permute-start(f32[128,40,128]{2,1,0:T(8,128)} %get-tuple-element.36), channel_id=1, source_target_pairs={{0,1},{1,0},{2,3},{3,2},{4,5},{5,4},{6,7},{7,6},{8,9},{9,8},{10,11... | collective-permute-start | bytes 7864328 | tf_op jit(solution)/shard_map/ppermute | solution.py:404
  (43 other events, 1139.9 us)

commit v7 on v6

--- a/solution.py
+++ b/solution.py
@@ -62,8 +62,9 @@
         at = 0
         for out, count in zip(out_refs, counts):
             view = out.at[:, pl.ds(first, group), :]
-            for i in range(group):
-                view[:, i, :] = res[at : at + count, i * m : (i + 1) * m]
+            for r in range(0, count, group):
+                eight = [res[at + r : at + r + group, i * m : (i + 1) * m] for i in range(group)]
+                view[r : r + group] = jnp.swapaxes(jnp.stack(eight), 0, 1)
             at += count
         return carry
 
@@ -81,7 +82,7 @@
     w = np.concatenate(
         [np.concatenate([high, high], axis=2), np.concatenate([low, np.zeros_like(low)], axis=2)], axis=1
     )
-    step = 32 if n > 64 else 16
+    step = 32 if n >= 64 else 16
     return pl.pallas_call(
         functools.partial(forward_kernel, counts),
         grid_spec=pltpu.PrefetchScalarGridSpec(
@@ -181,9 +182,9 @@
         @pl.when(step % each == each - 1)
         def _():
             out_a, out_b, held = rest[-5:-2]
-            for c in range(held.shape[0]):
-                out_a[:, c, :] = held[c, :rows]
-                out_b[:, c, :] = held[c, rows:]
+            for i in range(0, rows, 8):
+                out_a[i : i + 8] = jnp.swapaxes(held[:, i : i + 8, :], 0, 1)
+                out_b[i : i + 8] = jnp.swapaxes(held[:, rows + i : rows + i + 8, :], 0, 1)
 
 
 def numbers(part, me, d, g):
@@ -378,7 +379,9 @@
         d_own = [d_parts[c], d_swapped] if c else head + [d_parts[c], d_swapped]
         calls = (EARLY, LATE) if c in SPLIT else (ALL,)
         counts = {a: len(d_own) for a in range(around)}
-        plans = [numbers(part, me, counts, 2) for part in calls]
+        plans = [numbers(part, me, counts, 1 if c else 2) for part in calls]
+        if c:
+            g_own = [jnp.stack(g_own)]
         g = {("own", 0): g_own}
         up, down = g_own, g_own
         for s in range(1, levels):

time: 432 us -> 416 us (0.963)
  Pallas kernels: 109 us -> 102 us
  local copies, waits for them, and re-layouts: 12.3 us -> 7.98 us
    ppermute x12 -> x9, waiting for transfers between devices: 175 us -> 96.3 us  [local(): down = [lax.ppermute(x, 'src', downward) for x in down]]
    ppermute x5, waiting for transfers between devices: 0.01 us -> 54.4 us  [local(): right = [lax.ppermute(x, 'freq', clockwise) for x in right]]
    ppermute x5, waiting for transfers between devices: 14.6 us -> 39.1 us  [local(): left = [lax.ppermute(x, 'freq', counter) for x in left]]
    unnamed x60 -> x40, local copies, waits for them, and re-layouts: 8.92 us -> 4.59 us
    ppermute x12 -> x9, starting transfers between devices: 49.8 us -> 45.6 us  [local(): up = [lax.ppermute(x, 'src', upward) for x in up]]
    ppermute x12 -> x9, starting transfers between devices: 15.4 us -> 11.5 us  [local(): down = [lax.ppermute(x, 'src', downward) for x in down]]
    ppermute x12 -> x9, waiting for transfers between devices: 31.1 us -> 30 us  [local(): up = [lax.ppermute(x, 'src', upward) for x in up]]
  transfers between devices with their start and end apart: 45 -> 39, of which waited for: 18 -> 13; matrix products, arithmetic and copies ran while one was open for 1% -> 1% of each run, Pallas kernels for 23% -> 22%
where the time goes in v7:
time: 416 us; the launch traced here: 414 us
  waiting for transfers between devices  220 us (53%)
  Pallas kernels  102 us (25%)
  starting transfers between devices  78.4 us (19%)
  local copies, waits for them, and re-layouts  7.98 us (2%)
  between operations  4.4 us (1%)
    ppermute x9, waiting for transfers between devices, local(): down = [lax.ppermute(x, 'src', downward) for x in down]  96.3 us
    pallas_call x4, Pallas kernels, product(): pl.pallas_call(functools.partial(product_kernel, part, levels, places, d_...  57.9 us
    ppermute x5, waiting for transfers between devices, local(): right = [lax.ppermute(x, 'freq', clockwise) for x in right]  54.4 us
    ppermute x9, starting transfers between devices, local(): up = [lax.ppermute(x, 'src', upward) for x in up]  45.6 us
    ppermute x5, waiting for transfers between devices, local(): left = [lax.ppermute(x, 'freq', counter) for x in left]  39.1 us
    pallas_call x5, Pallas kernels, forward(): pl.pallas_call(functools.partial(forward_kernel, counts), grid_spec=pltpu...  30.5 us
    ppermute x9, waiting for transfers between devices, local(): up = [lax.ppermute(x, 'src', upward) for x in up]  30 us
    pallas_call x2, Pallas kernels, inverse(): pl.pallas_call(functools.partial(inverse_kernel, len(ms)), grid_spec=pltp...  13.8 us
  transfers between devices with their start and end apart: 39, of which 13 were waited for; matrix products, arithmetic and copies ran while one was open for 1% of the time, Pallas kernels for 22%

profile of v7, /device:TPU:0, one launch (start us, length us, event | category | flops | bytes accessed | tf_op | source)
XLA Modules:
  0.0 414.3 jit_solution(9413818098081003898)
XLA Ops:
  0.0 3.3 forward.8.refs_0_
  3.3 3.0 collective-permute-start.17
  6.3 5.8 %forward.5 = (f32[24,64,128]{2,1,0:T(8,128)}, f32[40,64,128]{2,1,0:T(8,128)}, f32[24,64,128]{2,1,0:T(8,128)}) custom-call(s32[1]{0:T(128)} %bitcast.core_ref, bf16[2,176,256]{2,1,0:T(8,128)(2,1)} %constant.82.clone.w_ref, f32[64,128,128]{2,1,0:T(8,128)} %x_ref.7), custom_call_target="tpu_custom_call" | custom-call | flops 1610612736 | bytes 8388608 | tf_op jit(solution)/shard_map/forward/pallas_call | solution.py:86
  12.1 5.0 %forward.7.refs_9_.refs_12_ = f32[40,64,128]{2,1,0:T(8,128)} custom-call(s32[1]{0:T(128)} %bitcast.core_ref, bf16[2,80,256]{2,1,0:T(8,128)(2,1)} %constant.81.clone.w_ref, f32[64,128,128]{2,1,0:T(8,128)} %x_ref.7), custom_call_target="tpu_custom_call" | custom-call | flops 1610612736 | bytes 8388608 | tf_op jit(solution)/shard_map/forward/pallas_call | solution.py:86
  17.1 4.0 collective-permute-start.15
  21.4 9.6 %forward.6 = (f32[24,128,128]{2,1,0:T(8,128)}, f32[40,128,128]{2,1,0:T(8,128)}, f32[24,128,128]{2,1,0:T(8,128)}) custom-call(s32[1]{0:T(128)} %bitcast.core_ref, bf16[2,176,256]{2,1,0:T(8,128)(2,1)} %constant.82.clone.w_ref, f32[128,128,128]{2,1,0:T(8,128)} %x_ref.9), custom_call_target="tpu_custom_call" | custom-call | flops 3221225472 | bytes 16777216 | tf_op jit(solution)/shard_map/forward/pallas_call | solution.py:86
  34.2 15.9 %collective-permute-done.15.refs_11_.refs_14_ = f32[40,64,128]{2,1,0:T(8,128)S(1)} collective-permute-done((f32[40,64,128]{2,1,0:T(8,128)}, f32[40,64,128]{2,1,0:T(8,128)S(1)}, u32[]{:S(2)}, u32[]{:S(2)}) %collective-permute-start.15) | collective-permute-done | bytes 1310752 | tf_op jit(solution)/shard_map/ppermute | solution.py:391
  52.9 6.8 %forward.9.refs_1_ = f32[40,96,128]{2,1,0:T(8,128)} custom-call(s32[1]{0:T(128)} %bitcast.core_ref, bf16[2,80,256]{2,1,0:T(8,128)(2,1)} %constant.81.clone.w_ref, f32[128,128,128]{2,1,0:T(8,128)} %x_ref.9), custom_call_target="tpu_custom_call" | custom-call | flops 2415919104 | bytes 12582912 | tf_op jit(solution)/shard_map/forward/pallas_call | solution.py:86
  61.3 3.0 collective-permute-done.28.refs_17_.refs_24_
  67.3 20.3 %collective-permute-done.3.refs_2_ = f32[24,128,128]{2,1,0:T(8,128)} collective-permute-done((f32[24,128,128]{2,1,0:T(8,128)}, f32[24,128,128]{2,1,0:T(8,128)}, u32[]{:S(2)}, u32[]{:S(2)}) %collective-permute-start.3) | collective-permute-done | bytes 1572896 | tf_op jit(solution)/shard_map/ppermute | solution.py:397
  87.6 5.4 %collective-permute-start.1 = (f32[2,24,64,128]{3,2,1,0:T(8,128)S(1)}, f32[2,24,64,128]{3,2,1,0:T(8,128)}, u32[]{:S(2)}, u32[]{:S(2)}) collective-permute-start(f32[2,24,64,128]{3,2,1,0:T(8,128)S(1)} %pad_maximum_fusion.refs_6_.refs_8_), channel_id=1, source_target_pairs={{0,2},{1,3},{2,4},{3,5},{4,6},{5,7},{8,10},{9,11},{10,12},{11,13},... | collective-permute-start | bytes 4718600 | tf_op jit(solution)/shard_map/ppermute | solution.py:391
  94.4 34.0 %collective-permute-done.18.refs_4_ = f32[40,96,128]{2,1,0:T(8,128)} collective-permute-done((f32[40,96,128]{2,1,0:T(8,128)}, f32[40,96,128]{2,1,0:T(8,128)}, u32[]{:S(2)}, u32[]{:S(2)}) %collective-permute-start.18) | collective-permute-done | bytes 1966112 | tf_op jit(solution)/shard_map/ppermute | solution.py:397
  128.5 5.4 %collective-permute-start.27 = (f32[40,64,128]{2,1,0:T(8,128)}, f32[40,64,128]{2,1,0:T(8,128)}, u32[]{:S(2)}, u32[]{:S(2)}) collective-permute-start(f32[40,64,128]{2,1,0:T(8,128)} %collective-permute-done.26.refs_10_.refs_13_), channel_id=1, source_target_pairs={{0,2},{1,3},{2,4},{3,5},{4,6},{5,7},{8,10},{9,11},{10,12},{11,13},... | collective-permute-start | bytes 3932168 | tf_op jit(solution)/shard_map/ppermute | solution.py:391
  143.1 6.3 %collective-permute-start.34 = (f32[40,64,128]{2,1,0:T(8,128)}, f32[40,64,128]{2,1,0:T(8,128)}, u32[]{:S(2)}, u32[]{:S(2)}) collective-permute-start(f32[40,64,128]{2,1,0:T(8,128)} %copy-done.11), channel_id=1, source_target_pairs={{0,2},{1,3},{2,4},{3,5},{4,6},{5,7},{8,10},{9,11},{10,12},{11,13},... | collective-permute-start | bytes 3932168 | tf_op jit(solution)/shard_map/ppermute | solution.py:391
  150.9 11.4 %collective-permute-done.27.refs_12_.refs_15_ = f32[40,64,128]{2,1,0:T(8,128)} collective-permute-done((f32[40,64,128]{2,1,0:T(8,128)}, f32[40,64,128]{2,1,0:T(8,128)}, u32[]{:S(2)}, u32[]{:S(2)}) %collective-permute-start.27) | collective-permute-done | bytes 1310752 | tf_op jit(solution)/shard_map/ppermute | solution.py:391
  163.8 4.6 %collective-permute-done.29.refs_15_.refs_20_ = f32[40,64,128]{2,1,0:T(8,128)} collective-permute-done((f32[40,64,128]{2,1,0:T(8,128)}, f32[40,64,128]{2,1,0:T(8,128)}, u32[]{:S(2)}, u32[]{:S(2)}) %collective-permute-start.29) | collective-permute-done | bytes 1310752 | tf_op jit(solution)/shard_map/ppermute | solution.py:392
  170.6 23.5 %collective-permute-done.31.refs_18_.refs_25_ = f32[40,64,128]{2,1,0:T(8,128)} collective-permute-done((f32[40,64,128]{2,1,0:T(8,128)}, f32[40,64,128]{2,1,0:T(8,128)}, u32[]{:S(2)}, u32[]{:S(2)}) %collective-permute-start.31) | collective-permute-done | bytes 1310752 | tf_op jit(solution)/shard_map/ppermute | solution.py:392
  195.4 5.7 %collective-permute-start.12 = (f32[2,24,64,128]{3,2,1,0:T(8,128)}, f32[2,24,64,128]{3,2,1,0:T(8,128)}, u32[]{:S(2)}, u32[]{:S(2)}) collective-permute-start(f32[2,24,64,128]{3,2,1,0:T(8,128)} %collective-permute-done.1.refs_7_.refs_9_), channel_id=1, source_target_pairs={{0,2},{1,3},{2,4},{3,5},{4,6},{5,7},{8,10},{9,11},{10,12},{11,13},... | collective-permute-start | bytes 4718600 | tf_op jit(solution)/shard_map/ppermute | solution.py:391
  201.1 39.1 %collective-permute-done.6.refs_5_.refs_7_ = f32[24,128,128]{2,1,0:T(8,128)} collective-permute-done((f32[24,128,128]{2,1,0:T(8,128)}, f32[24,128,128]{2,1,0:T(8,128)}, u32[]{:S(2)}, u32[]{:S(2)}) %collective-permute-start.6) | collective-permute-done | bytes 1572896 | tf_op jit(solution)/shard_map/ppermute | solution.py:398
  244.4 5.3 %collective-permute-start.35 = (f32[40,64,128]{2,1,0:T(8,128)}, f32[40,64,128]{2,1,0:T(8,128)S(1)}, u32[]{:S(2)}, u32[]{:S(2)}) collective-permute-start(f32[40,64,128]{2,1,0:T(8,128)} %collective-permute-done.27.refs_12_.refs_15_), channel_id=1, source_target_pairs={{0,2},{1,3},{2,4},{3,5},{4,6},{5,7},{8,10},{9,11},{10,12},{11,13},... | collective-permute-start | bytes 3932168 | tf_op jit(solution)/shard_map/ppermute | solution.py:391
  250.2 23.7 %collective-permute-done.30.refs_16_ = f32[40,64,128]{2,1,0:T(8,128)S(1)} collective-permute-done((f32[40,64,128]{2,1,0:T(8,128)}, f32[40,64,128]{2,1,0:T(8,128)S(1)}, u32[]{:S(2)}, u32[]{:S(2)}) %collective-permute-start.30) | collective-permute-done | bytes 1310752 | tf_op jit(solution)/shard_map/ppermute | solution.py:392
  273.9 2.7 collective-permute-start.36
  276.7 21.6 %collective-permute-done.32.refs_16_.refs_21_ = f32[40,64,128]{2,1,0:T(8,128)S(1)} collective-permute-done((f32[40,64,128]{2,1,0:T(8,128)}, f32[40,64,128]{2,1,0:T(8,128)S(1)}, u32[]{:S(2)}, u32[]{:S(2)}) %collective-permute-start.32) | collective-permute-done | bytes 1310752 | tf_op jit(solution)/shard_map/ppermute | solution.py:392
  299.6 4.6 %collective-permute-start.37 = (f32[40,64,128]{2,1,0:T(8,128)S(1)}, f32[40,64,128]{2,1,0:T(8,128)S(1)}, u32[]{:S(2)}, u32[]{:S(2)}) collective-permute-start(f32[40,64,128]{2,1,0:T(8,128)S(1)} %collective-permute-done.35.refs_14_.refs_19_), channel_id=1, source_target_pairs={{0,2},{1,3},{2,4},{3,5},{4,6},{5,7},{8,10},{9,11},{10,12},{11,13},... | collective-permute-start | bytes 3932168 | tf_op jit(solution)/shard_map/ppermute | solution.py:391
  307.3 19.9 %collective-permute-done.33.refs_17_ = f32[40,64,128]{2,1,0:T(8,128)S(1)} collective-permute-done((f32[40,64,128]{2,1,0:T(8,128)S(1)}, f32[40,64,128]{2,1,0:T(8,128)S(1)}, u32[]{:S(2)}, u32[]{:S(2)}) %collective-permute-start.33) | collective-permute-done | bytes 1310752 | tf_op jit(solution)/shard_map/ppermute | solution.py:392
  332.1 6.2 %collective-permute-start.13 = (f32[2,24,64,128]{3,2,1,0:T(8,128)}, f32[2,24,64,128]{3,2,1,0:T(8,128)}, u32[]{:S(2)}, u32[]{:S(2)}) collective-permute-start(f32[2,24,64,128]{3,2,1,0:T(8,128)} %collective-permute-done.12.refs_8_.refs_11_), channel_id=1, source_target_pairs={{0,2},{1,3},{2,4},{3,5},{4,6},{5,7},{8,10},{9,11},{10,12},{11,13},... | collective-permute-start | bytes 4718600 | tf_op jit(solution)/shard_map/ppermute | solution.py:391
  338.2 17.8 %shard_map.102.refs_26_ = f32[40,256,128]{2,1,0:T(8,128)} custom-call(s32[27]{0:T(128)} %concatenate.14.slot_ref, f32[40,32,128]{2,1,0:T(8,128)} %forward.8.refs_0_, f32[40,96,128]{2,1,0:T(8,128)} %forward.9.refs_1_, f32[40,128,128]{2,1,0:T(8,128)} %collective-permute-done.16.refs_2_, f32[40,32,128]{2,1,0:T(8,128)} %copy-done.14, ...), custom_call_target="tpu_custom_call" | custom-call | flops 6039797760 | bytes 28835840 | tf_op jit(solution)/shard_map/pallas_call | solution.py:261
  356.1 18.8 %shard_map.103 = (f32[128,40,128]{2,1,0:T(8,128)}, f32[128,40,128]{2,1,0:T(8,128)}) custom-call(s32[34]{0:T(128)} %concatenate.15.slot_ref, f32[40,32,128]{2,1,0:T(8,128)} %forward.8.refs_0_, f32[40,96,128]{2,1,0:T(8,128)} %forward.9.refs_1_, f32[40,128,128]{2,1,0:T(8,128)} %collective-permute-done.16.refs_2_, f32[40,32,128]{2,1,0:T(8,128)} %copy-done.14, ...), custom_call_target="tpu_custom_call" | custom-call | flops 4026531840 | bytes 44564480 | tf_op jit(solution)/shard_map/pallas_call | solution.py:261
  376.1 10.8 %shard_map.100.refs_15_ = f32[24,256,128]{2,1,0:T(8,128)S(1)} custom-call(s32[19]{0:T(128)} %concatenate.12.slot_ref, f32[24,128,128]{2,1,0:T(8,128)} %get-tuple-element.24.refs_0_, f32[24,128,128]{2,1,0:T(8,128)} %collective-permute-done.2.refs_1_, f32[24,128,128]{2,1,0:T(8,128)} %collective-permute-done.3.refs_2_, f32[24,128,128]{2,1,0:T(8,128)} %copy-done.9, ...), custom_call_target="tpu_custom_call" | custom-call | flops 3623878656 | bytes 17301504 | tf_op jit(solution)/shard_map/pallas_call | solution.py:261
  388.3 10.4 %shard_map.101 = (f32[128,24,128]{2,1,0:T(8,128)S(1)}, f32[128,24,128]{2,1,0:T(8,128)S(1)}) custom-call(s32[23]{0:T(128)S(1)} %concatenate.13.slot_ref, f32[24,128,128]{2,1,0:T(8,128)S(1)} %copy-done, f32[24,128,128]{2,1,0:T(8,128)} %collective-permute-done.2.refs_1_, f32[24,128,128]{2,1,0:T(8,128)} %collective-permute-done.3.refs_2_, ...), custom_call_target="tpu_custom_call" | custom-call | flops 2415919104 | bytes 26738688 | tf_op jit(solution)/shard_map/pallas_call | solution.py:261
  400.5 7.0 %inverse.2.refs_2_ = f32[128,128,128]{2,1,0:T(8,128)S(1)} custom-call(s32[1]{0:T(128)} %bitcast.core_ref, bf16[2,160,256]{2,1,0:T(8,128)(2,1)S(1)} %copy-done.4, f32[128,40,128]{2,1,0:T(8,128)S(1)} %copy-done.1, f32[128,40,128]{2,1,0:T(8,128)} %collective-permute-done.38.refs_1_), custom_call_target="tpu_custom_call" | custom-call | flops 3221225472 | bytes 16777216 | tf_op jit(solution)/shard_map/inverse/pallas_call | solution.py:306
  407.5 6.7 %inverse.3 = f32[128,128,128]{2,1,0:T(8,128)} custom-call(s32[1]{0:T(128)} %bitcast.core_ref, bf16[2,96,256]{2,1,0:T(8,128)(2,1)S(1)} %copy-done.5, f32[128,24,128]{2,1,0:T(8,128)S(1)} %copy-done.3, f32[128,24,128]{2,1,0:T(8,128)S(1)} %collective-permute-done.14.refs_1_, f32[128,128,128]{2,1,0:T(8,128)S(1)} %inverse.2.refs_2_), custom_call_target="tpu_custom_call" | custom-call | flops 3221225472 | bytes 16777216 | tf_op jit(solution)/shard_map/inverse/pallas_call | solution.py:306
  (111 shorter events, 42.1 us)
Async XLA Ops:
  17.1 33.0 %collective-permute-start.15 = (f32[40,64,128]{2,1,0:T(8,128)}, f32[40,64,128]{2,1,0:T(8,128)S(1)}, u32[]{:S(2)}, u32[]{:S(2)}) collective-permute-start(f32[40,64,128]{2,1,0:T(8,128)} %forward.7.refs_9_.refs_12_), channel_id=1, source_target_pairs={{0,2},{1,3},{2,4},{3,5},{4,6},{5,7},{8,10},{9,11},{10,12},{11,13},... | collective-permute-start | bytes 3932168 | tf_op jit(solution)/shard_map/ppermute | solution.py:391
  21.2 38.6 %collective-permute-start.26 = (f32[40,64,128]{2,1,0:T(8,128)}, f32[40,64,128]{2,1,0:T(8,128)}, u32[]{:S(2)}, u32[]{:S(2)}) collective-permute-start(f32[40,64,128]{2,1,0:T(8,128)} %get-tuple-element.32), channel_id=1, source_target_pairs={{0,1},{1,0},{2,3},{3,2},{4,5},{5,4},{6,7},{7,6},{8,9},{9,8},{10,11... | collective-permute-start | bytes 3932168 | tf_op jit(solution)/shard_map/ppermute | solution.py:377
  31.0 34.8 %collective-permute-start.2 = (f32[24,128,128]{2,1,0:T(8,128)}, f32[24,128,128]{2,1,0:T(8,128)}, u32[]{:S(2)}, u32[]{:S(2)}) collective-permute-start(f32[24,128,128]{2,1,0:T(8,128)} %get-tuple-element.25), channel_id=1, source_target_pairs={{0,1},{1,0},{2,3},{3,2},{4,5},{5,4},{6,7},{7,6},{8,9},{9,8},{10,11... | collective-permute-start | bytes 4718600 | tf_op jit(solution)/shard_map/ppermute | solution.py:378
  31.3 33.0 %collective-permute-start.28 = (f32[40,64,128]{2,1,0:T(8,128)S(1)}, f32[40,64,128]{2,1,0:T(8,128)}, u32[]{:S(2)}, u32[]{:S(2)}) collective-permute-start(f32[40,64,128]{2,1,0:T(8,128)S(1)} %copy-done.10), channel_id=1, source_target_pairs={{2,0},{3,1},{4,2},{5,3},{6,4},{7,5},{10,8},{11,9},{12,10},{13,11},... | collective-permute-start | bytes 3932168 | tf_op jit(solution)/shard_map/ppermute | solution.py:392
  50.1 37.6 %collective-permute-start.3 = (f32[24,128,128]{2,1,0:T(8,128)}, f32[24,128,128]{2,1,0:T(8,128)}, u32[]{:S(2)}, u32[]{:S(2)}) collective-permute-start(f32[24,128,128]{2,1,0:T(8,128)} %get-tuple-element.24.refs_0_), channel_id=1, source_target_pairs={{0,8},{8,24},{24,16},{16,0},{1,9},{9,25},{25,17},{17,1},{2,10},{10... | collective-permute-start | bytes 4718600 | tf_op jit(solution)/shard_map/ppermute | solution.py:397
  52.4 40.7 %collective-permute-start.8 = (f32[24,128,128]{2,1,0:T(8,128)}, f32[24,128,128]{2,1,0:T(8,128)}, u32[]{:S(2)}, u32[]{:S(2)}) collective-permute-start(f32[24,128,128]{2,1,0:T(8,128)} %get-tuple-element.24.refs_0_), channel_id=1, source_target_pairs={{8,0},{24,8},{16,24},{0,16},{9,1},{25,9},{17,25},{1,17},{10,2},{26... | collective-permute-start | bytes 4718600 | tf_op jit(solution)/shard_map/ppermute | solution.py:398
  59.8 68.7 %collective-permute-start.18 = (f32[40,96,128]{2,1,0:T(8,128)}, f32[40,96,128]{2,1,0:T(8,128)}, u32[]{:S(2)}, u32[]{:S(2)}) collective-permute-start(f32[40,96,128]{2,1,0:T(8,128)} %forward.9.refs_1_), channel_id=1, source_target_pairs={{0,8},{8,24},{24,16},{16,0},{1,9},{9,25},{25,17},{17,1},{2,10},{10... | collective-permute-start | bytes 5898248 | tf_op jit(solution)/shard_map/ppermute | solution.py:397
  64.3 70.2 %collective-permute-start.25 = (f32[40,96,128]{2,1,0:T(8,128)}, f32[40,96,128]{2,1,0:T(8,128)S(1)}, u32[]{:S(2)}, u32[]{:S(2)}) collective-permute-start(f32[40,96,128]{2,1,0:T(8,128)} %forward.9.refs_1_), channel_id=1, source_target_pairs={{8,0},{24,8},{16,24},{0,16},{9,1},{25,9},{17,25},{1,17},{10,2},{26... | collective-permute-start | bytes 5898248 | tf_op jit(solution)/shard_map/ppermute | solution.py:398
  65.8 83.5 %collective-permute-start.16 = (f32[40,128,128]{2,1,0:T(8,128)}, f32[40,128,128]{2,1,0:T(8,128)}, u32[]{:S(2)}, u32[]{:S(2)}) collective-permute-start(f32[40,128,128]{2,1,0:T(8,128)} %get-tuple-element.31), channel_id=1, source_target_pairs={{0,1},{1,0},{2,3},{3,2},{4,5},{5,4},{6,7},{7,6},{8,9},{9,8},{10,11... | collective-permute-start | bytes 7864328 | tf_op jit(solution)/shard_map/ppermute | solution.py:378
  87.6 54.2 %collective-permute-start.1 = (f32[2,24,64,128]{3,2,1,0:T(8,128)S(1)}, f32[2,24,64,128]{3,2,1,0:T(8,128)}, u32[]{:S(2)}, u32[]{:S(2)}) collective-permute-start(f32[2,24,64,128]{3,2,1,0:T(8,128)S(1)} %pad_maximum_fusion.refs_6_.refs_8_), channel_id=1, source_target_pairs={{0,2},{1,3},{2,4},{3,5},{4,6},{5,7},{8,10},{9,11},{10,12},{11,13},... | collective-permute-start | bytes 4718600 | tf_op jit(solution)/shard_map/ppermute | solution.py:391
  93.1 50.0 %collective-permute-start.9 = (f32[2,24,64,128]{3,2,1,0:T(8,128)S(1)}, f32[2,24,64,128]{3,2,1,0:T(8,128)}, u32[]{:S(2)}, u32[]{:S(2)}) collective-permute-start(f32[2,24,64,128]{3,2,1,0:T(8,128)S(1)} %pad_maximum_fusion.refs_6_.refs_8_), channel_id=1, source_target_pairs={{2,0},{3,1},{4,2},{5,3},{6,4},{7,5},{10,8},{11,9},{12,10},{13,11},... | collective-permute-start | bytes 4718600 | tf_op jit(solution)/shard_map/ppermute | solution.py:392
  128.5 33.8 %collective-permute-start.27 = (f32[40,64,128]{2,1,0:T(8,128)}, f32[40,64,128]{2,1,0:T(8,128)}, u32[]{:S(2)}, u32[]{:S(2)}) collective-permute-start(f32[40,64,128]{2,1,0:T(8,128)} %collective-permute-done.26.refs_10_.refs_13_), channel_id=1, source_target_pairs={{0,2},{1,3},{2,4},{3,5},{4,6},{5,7},{8,10},{9,11},{10,12},{11,13},... | collective-permute-start | bytes 3932168 | tf_op jit(solution)/shard_map/ppermute | solution.py:391
  134.5 33.9 %collective-permute-start.29 = (f32[40,64,128]{2,1,0:T(8,128)}, f32[40,64,128]{2,1,0:T(8,128)}, u32[]{:S(2)}, u32[]{:S(2)}) collective-permute-start(f32[40,64,128]{2,1,0:T(8,128)} %collective-permute-done.28.refs_17_.refs_24_), channel_id=1, source_target_pairs={{2,0},{3,1},{4,2},{5,3},{6,4},{7,5},{10,8},{11,9},{12,10},{13,11},... | collective-permute-start | bytes 3932168 | tf_op jit(solution)/shard_map/ppermute | solution.py:392
  141.8 52.3 %collective-permute-start.31 = (f32[40,64,128]{2,1,0:T(8,128)}, f32[40,64,128]{2,1,0:T(8,128)}, u32[]{:S(2)}, u32[]{:S(2)}) collective-permute-start(f32[40,64,128]{2,1,0:T(8,128)} %collective-permute-done.26.refs_10_.refs_13_), channel_id=1, source_target_pairs={{2,0},{3,1},{4,2},{5,3},{6,4},{7,5},{10,8},{11,9},{12,10},{13,11},... | collective-permute-start | bytes 3932168 | tf_op jit(solution)/shard_map/ppermute | solution.py:392
  143.1 52.3 %collective-permute-start.34 = (f32[40,64,128]{2,1,0:T(8,128)}, f32[40,64,128]{2,1,0:T(8,128)}, u32[]{:S(2)}, u32[]{:S(2)}) collective-permute-start(f32[40,64,128]{2,1,0:T(8,128)} %copy-done.11), channel_id=1, source_target_pairs={{0,2},{1,3},{2,4},{3,5},{4,6},{5,7},{8,10},{9,11},{10,12},{11,13},... | collective-permute-start | bytes 3932168 | tf_op jit(solution)/shard_map/ppermute | solution.py:391
  149.4 100.3 %collective-permute-start.22 = (f32[40,128,128]{2,1,0:T(8,128)}, f32[40,128,128]{2,1,0:T(8,128)}, u32[]{:S(2)}, u32[]{:S(2)}) collective-permute-start(f32[40,128,128]{2,1,0:T(8,128)} %collective-permute-done.16.refs_2_), channel_id=1, source_target_pairs={{8,0},{24,8},{16,24},{0,16},{9,1},{25,9},{17,25},{1,17},{10,2},{26... | collective-permute-start | bytes 7864328 | tf_op jit(solution)/shard_map/ppermute | solution.py:398
  162.3 77.9 %collective-permute-start.6 = (f32[24,128,128]{2,1,0:T(8,128)}, f32[24,128,128]{2,1,0:T(8,128)}, u32[]{:S(2)}, u32[]{:S(2)}) collective-permute-start(f32[24,128,128]{2,1,0:T(8,128)} %collective-permute-done.2.refs_1_), channel_id=1, source_target_pairs={{8,0},{24,8},{16,24},{0,16},{9,1},{25,9},{17,25},{1,17},{10,2},{26... | collective-permute-start | bytes 4718600 | tf_op jit(solution)/shard_map/ppermute | solution.py:398
  168.4 76.0 %collective-permute-start.21 = (f32[40,96,128]{2,1,0:T(8,128)}, f32[40,96,128]{2,1,0:T(8,128)}, u32[]{:S(2)}, u32[]{:S(2)}) collective-permute-start(f32[40,96,128]{2,1,0:T(8,128)} %collective-permute-done.18.refs_4_), channel_id=1, source_target_pairs={{0,8},{8,24},{24,16},{16,0},{1,9},{9,25},{25,17},{17,1},{2,10},{10... | collective-permute-start | bytes 5898248 | tf_op jit(solution)/shard_map/ppermute | solution.py:402
  194.1 47.4 %collective-permute-start.10 = (f32[2,24,64,128]{3,2,1,0:T(8,128)}, f32[2,24,64,128]{3,2,1,0:T(8,128)}, u32[]{:S(2)}, u32[]{:S(2)}) collective-permute-start(f32[2,24,64,128]{3,2,1,0:T(8,128)} %collective-permute-done.9.refs_10_.refs_14_), channel_id=1, source_target_pairs={{2,0},{3,1},{4,2},{5,3},{6,4},{7,5},{10,8},{11,9},{12,10},{13,11},... | collective-permute-start | bytes 4718600 | tf_op jit(solution)/shard_map/ppermute | solution.py:392
  195.4 47.6 %collective-permute-start.12 = (f32[2,24,64,128]{3,2,1,0:T(8,128)}, f32[2,24,64,128]{3,2,1,0:T(8,128)}, u32[]{:S(2)}, u32[]{:S(2)}) collective-permute-start(f32[2,24,64,128]{3,2,1,0:T(8,128)} %collective-permute-done.1.refs_7_.refs_9_), channel_id=1, source_target_pairs={{0,2},{1,3},{2,4},{3,5},{4,6},{5,7},{8,10},{9,11},{10,12},{11,13},... | collective-permute-start | bytes 4718600 | tf_op jit(solution)/shard_map/ppermute | solution.py:391
  240.2 33.7 %collective-permute-start.30 = (f32[40,64,128]{2,1,0:T(8,128)}, f32[40,64,128]{2,1,0:T(8,128)S(1)}, u32[]{:S(2)}, u32[]{:S(2)}) collective-permute-start(f32[40,64,128]{2,1,0:T(8,128)} %collective-permute-done.29.refs_15_.refs_20_), channel_id=1, source_target_pairs={{2,0},{3,1},{4,2},{5,3},{6,4},{7,5},{10,8},{11,9},{12,10},{13,11},... | collective-permute-start | bytes 3932168 | tf_op jit(solution)/shard_map/ppermute | solution.py:392
  241.5 65.1 %collective-permute-start.19 = (f32[40,128,128]{2,1,0:T(8,128)}, f32[40,128,128]{2,1,0:T(8,128)}, u32[]{:S(2)}, u32[]{:S(2)}) collective-permute-start(f32[40,128,128]{2,1,0:T(8,128)} %collective-permute-done.16.refs_2_), channel_id=1, source_target_pairs={{0,8},{8,24},{24,16},{16,0},{1,9},{9,25},{25,17},{17,1},{2,10},{10... | collective-permute-start | bytes 7864328 | tf_op jit(solution)/shard_map/ppermute | solution.py:397
  243.1 55.2 %collective-permute-start.32 = (f32[40,64,128]{2,1,0:T(8,128)}, f32[40,64,128]{2,1,0:T(8,128)S(1)}, u32[]{:S(2)}, u32[]{:S(2)}) collective-permute-start(f32[40,64,128]{2,1,0:T(8,128)} %collective-permute-done.31.refs_18_.refs_25_), channel_id=1, source_target_pairs={{2,0},{3,1},{4,2},{5,3},{6,4},{7,5},{10,8},{11,9},{12,10},{13,11},... | collective-permute-start | bytes 3932168 | tf_op jit(solution)/shard_map/ppermute | solution.py:392
  244.4 55.2 %collective-permute-start.35 = (f32[40,64,128]{2,1,0:T(8,128)}, f32[40,64,128]{2,1,0:T(8,128)S(1)}, u32[]{:S(2)}, u32[]{:S(2)}) collective-permute-start(f32[40,64,128]{2,1,0:T(8,128)} %collective-permute-done.27.refs_12_.refs_15_), channel_id=1, source_target_pairs={{0,2},{1,3},{2,4},{3,5},{4,6},{5,7},{8,10},{9,11},{10,12},{11,13},... | collective-permute-start | bytes 3932168 | tf_op jit(solution)/shard_map/ppermute | solution.py:391
  249.6 82.4 %collective-permute-start.23 = (f32[40,128,128]{2,1,0:T(8,128)}, f32[40,128,128]{2,1,0:T(8,128)}, u32[]{:S(2)}, u32[]{:S(2)}) collective-permute-start(f32[40,128,128]{2,1,0:T(8,128)} %collective-permute-done.22.refs_8_.refs_11_), channel_id=1, source_target_pairs={{8,0},{24,8},{16,24},{0,16},{9,1},{25,9},{17,25},{1,17},{10,2},{26... | collective-permute-start | bytes 7864328 | tf_op jit(solution)/shard_map/ppermute | solution.py:403
  273.9 31.1 %collective-permute-start.36 = (f32[40,64,128]{2,1,0:T(8,128)}, f32[40,64,128]{2,1,0:T(8,128)S(1)}, u32[]{:S(2)}, u32[]{:S(2)}) collective-permute-start(f32[40,64,128]{2,1,0:T(8,128)} %collective-permute-done.34.refs_13_.refs_18_), channel_id=1, source_target_pairs={{0,2},{1,3},{2,4},{3,5},{4,6},{5,7},{8,10},{9,11},{10,12},{11,13},... | collective-permute-start | bytes 3932168 | tf_op jit(solution)/shard_map/ppermute | solution.py:391
  299.6 31.2 %collective-permute-start.37 = (f32[40,64,128]{2,1,0:T(8,128)S(1)}, f32[40,64,128]{2,1,0:T(8,128)S(1)}, u32[]{:S(2)}, u32[]{:S(2)}) collective-permute-start(f32[40,64,128]{2,1,0:T(8,128)S(1)} %collective-permute-done.35.refs_14_.refs_19_), channel_id=1, source_target_pairs={{0,2},{1,3},{2,4},{3,5},{4,6},{5,7},{8,10},{9,11},{10,12},{11,13},... | collective-permute-start | bytes 3932168 | tf_op jit(solution)/shard_map/ppermute | solution.py:391
  305.0 69.9 %collective-permute-start.4 = (f32[24,128,128]{2,1,0:T(8,128)}, f32[24,128,128]{2,1,0:T(8,128)S(1)}, u32[]{:S(2)}, u32[]{:S(2)}) collective-permute-start(f32[24,128,128]{2,1,0:T(8,128)} %collective-permute-done.2.refs_1_), channel_id=1, source_target_pairs={{0,8},{8,24},{24,16},{16,0},{1,9},{9,25},{25,17},{17,1},{2,10},{10... | collective-permute-start | bytes 4718600 | tf_op jit(solution)/shard_map/ppermute | solution.py:397
  306.6 80.3 %collective-permute-start.5 = (f32[24,128,128]{2,1,0:T(8,128)}, f32[24,128,128]{2,1,0:T(8,128)}, u32[]{:S(2)}, u32[]{:S(2)}) collective-permute-start(f32[24,128,128]{2,1,0:T(8,128)} %collective-permute-done.3.refs_2_), channel_id=1, source_target_pairs={{0,8},{8,24},{24,16},{16,0},{1,9},{9,25},{25,17},{17,1},{2,10},{10... | collective-permute-start | bytes 4718600 | tf_op jit(solution)/shard_map/ppermute | solution.py:402
  327.3 59.6 %collective-permute-start.7 = (f32[24,128,128]{2,1,0:T(8,128)}, f32[24,128,128]{2,1,0:T(8,128)}, u32[]{:S(2)}, u32[]{:S(2)}) collective-permute-start(f32[24,128,128]{2,1,0:T(8,128)} %collective-permute-done.6.refs_5_.refs_7_), channel_id=1, source_target_pairs={{8,0},{24,8},{16,24},{0,16},{9,1},{25,9},{17,25},{1,17},{10,2},{26... | collective-permute-start | bytes 4718600 | tf_op jit(solution)/shard_map/ppermute | solution.py:403
  330.7 56.2 %collective-permute-start.11 = (f32[2,24,64,128]{3,2,1,0:T(8,128)}, f32[2,24,64,128]{3,2,1,0:T(8,128)}, u32[]{:S(2)}, u32[]{:S(2)}) collective-permute-start(f32[2,24,64,128]{3,2,1,0:T(8,128)} %collective-permute-done.10.refs_9_.refs_12_), channel_id=1, source_target_pairs={{2,0},{3,1},{4,2},{5,3},{6,4},{7,5},{10,8},{11,9},{12,10},{13,11},... | collective-permute-start | bytes 4718600 | tf_op jit(solution)/shard_map/ppermute | solution.py:392
  332.1 54.9 %collective-permute-start.13 = (f32[2,24,64,128]{3,2,1,0:T(8,128)}, f32[2,24,64,128]{3,2,1,0:T(8,128)}, u32[]{:S(2)}, u32[]{:S(2)}) collective-permute-start(f32[2,24,64,128]{3,2,1,0:T(8,128)} %collective-permute-done.12.refs_8_.refs_11_), channel_id=1, source_target_pairs={{0,2},{1,3},{2,4},{3,5},{4,6},{5,7},{8,10},{9,11},{10,12},{11,13},... | collective-permute-start | bytes 4718600 | tf_op jit(solution)/shard_map/ppermute | solution.py:391
  (27 other events, 743.7 us)
